TPU v7x, 256 devices: a whole 4x4x8 slice. The times are simulated.
256 devices in a mesh: space: 16 (over y, x_hi, core), offset: 16 (over z, x_lo).
Axes of the slice: x: 4 (x_hi: 2, x_lo: 2; x = x_hi * 2 + x_lo), y: 4, z: 8, core: 2. Of those that a mesh axis runs over, the one named last changes fastest.
Arguments:
- src_prev: float32 [4, 256, 2048], P(None, 'offset', 'space'), may hold values from -6 to 6
- src_now: float32 [4, 256, 2048], P(None, 'offset', 'space'), may hold values from -6 to 6
- rcv_prev: float32 [4, 256, 2048], P(None, 'offset', 'space'), may hold values from -6 to 6
- rcv_now: float32 [4, 256, 2048], P(None, 'offset', 'space'), may hold values from -6 to 6
- velocity: float32 [4, 256, 2048], P(None, 'offset', 'space'), may hold values from 0.03 to 0.16
- shift_table: int32 [256, 2], P('offset'), may hold values from -8 to 7, as said below
- ref_image: bfloat16 [256, 4, 256, 2048], P('offset', None, None, 'space'), may hold values from -6 to 6
Outputs:
- image: bfloat16 [256, 4, 256, 2048], P('offset', None, None, 'space')
- adjoint: float32 [4, 256, 2048], P(None, 'offset', 'space')
Inputs may be any that keep to these rules, and one draw needn't show every extreme that they name: `shift_table`: each row is (hx, hy); every pair with both entries in the range appears exactly once, in an order drawn from the seed.
All inputs are finite; a program needn't handle non-finite values.
Results may differ from a plain program's by a relative error of at most 0.001.
Values sent between devices are 32-bit elements; how exact they have to be, the bound alone decides.
No kernel may reach another device: no remote copies, remote signals or barrier semaphores. Data moves between devices by JAX's collectives and lax.ppermute only.
A program may use at most 64 MiB of HBM per device.

v0:
```python
import jax
import jax.numpy as jnp
from jax import lax
from jax.sharding import PartitionSpec as P

OFF_SIDE = 16
STEPS = 2
HMAX = 8


def with_halo(block, sides, width):
    for axis, dim in sides:
        count = lax.axis_size(axis)
        forward = [(i, i + 1) for i in range(count - 1)]
        backward = [(target, source) for source, target in forward]
        low = lax.ppermute(
            lax.slice_in_dim(block, block.shape[dim] - width, None, axis=dim), axis, forward
        )
        high = lax.ppermute(lax.slice_in_dim(block, 0, width, axis=dim), axis, backward)
        block = jnp.concatenate([low, block, high], axis=dim)
    return block


def passed_along(block, axis, distance):
    devices = range(lax.axis_size(axis))
    route = [(i - distance, i) for i in devices if i - distance in devices]
    return lax.ppermute(block, axis, route)


def advance(prev, now, speed, padded):
    deep = jnp.pad(now, ((0, 0), (1, 1), (0, 0), (0, 0)))
    beside = deep[:, 2:] + deep[:, :-2]
    beside = beside + padded[:, :, 2:, 1:-1] + padded[:, :, :-2, 1:-1]
    beside = beside + padded[:, :, 1:-1, 2:] + padded[:, :, 1:-1, :-2]
    return 2.0 * now - prev + speed * (beside - 6.0 * now)


def on_device(src_prev, src_now, rcv_prev, rcv_now, velocity, shift_table, ref_image):
    depth, rows, cols = src_now.shape
    extended = []
    prev = jnp.stack([src_prev, rcv_prev])
    now = jnp.stack([src_now, rcv_now])
    for step in range(STEPS):
        padded = with_halo(now, (("space", 3), ("offset", 2)), 1)
        prev, now = (now, advance(prev, now, velocity, padded))
        snap = lax.all_gather(now, "offset", axis=2, tiled=True)
        wide = with_halo(snap, (("space", 3),), HMAX)
        extended.append(jnp.pad(wide, ((0, 0), (0, 0), (HMAX, HMAX), (0, 0))))
    full_rows = extended[0].shape[2] - 2 * HMAX
    zero_index = jnp.zeros((), jnp.int32)

    def per_offset(carry, inputs):
        row, observed = inputs
        shift_x = row[0]
        shift_y = row[1]
        full = jnp.zeros((depth, full_rows, cols), jnp.float32)
        source_shifted = full
        for pair in extended:
            source_shifted = lax.dynamic_slice(
                pair[0], (zero_index, HMAX - shift_y, HMAX - shift_x), (depth, full_rows, cols)
            )
            rcv_shifted = lax.dynamic_slice(
                pair[1], (zero_index, HMAX + shift_y, HMAX + shift_x), (depth, full_rows, cols)
            )
            full = full + source_shifted * rcv_shifted
        term = (full - observed.astype(jnp.float32)) * source_shifted
        starts = (zero_index, HMAX + shift_y, HMAX + shift_x)
        window = lax.dynamic_slice(carry, starts, (depth, full_rows, cols))
        carry = lax.dynamic_update_slice(carry, window + term, starts)
        return (carry, full.astype(jnp.bfloat16))

    start = jnp.zeros((depth, full_rows + 2 * HMAX, cols + 2 * HMAX), jnp.float32)
    carry, image = lax.scan(per_offset, start, (shift_table, ref_image))
    partial_value = carry[:, HMAX : HMAX + full_rows, :]
    total = lax.psum(partial_value, "offset")
    owned = lax.dynamic_slice_in_dim(total, lax.axis_index("offset") * rows, rows, 1)
    from_left = passed_along(owned[:, :, HMAX + cols :], "space", 1)
    from_right = passed_along(owned[:, :, :HMAX], "space", -1)
    core = owned[:, :, HMAX : HMAX + cols]
    core = core.at[:, :, :HMAX].add(from_left)
    core = core.at[:, :, cols - HMAX :].add(from_right)
    return (image, core / OFF_SIDE)


def solution(mesh):
    in_specs = (
        P(None, "offset", "space"),
        P(None, "offset", "space"),
        P(None, "offset", "space"),
        P(None, "offset", "space"),
        P(None, "offset", "space"),
        P("offset", None),
        P("offset", None, None, "space"),
    )
    out_specs = (P("offset", None, None, "space"), P(None, "offset", "space"))
    return jax.shard_map(
        on_device, mesh=mesh, in_specs=in_specs, out_specs=out_specs, check_vma=False
    )
```

profile of v0, /device:TPU:16, one launch (start us, length us, event | category | flops | bytes accessed | tf_op | source)
XLA Modules:
  0.0 638.3 jit_solution(10496569499931545567)
XLA Ops:
  10.1 6.0 collective-permute-start.1
  20.2 4.5 collective-permute-start.3
  28.0 3.4 collective-permute-start.6
  31.5 4.5 collective-permute-start.7
  40.0 4.9 collective-permute-start.9
  48.6 53.6 %all-gather.3.cloned.1.call-done = f32[2,4,256,128]{3,1,0,2:T(4,128)} async-done(((f32[2,4,16,128]{3,1,0,2:T(4,128)}), f32[2,4,256,128]{3,1,0,2:T(4,128)}) %all-gather.3.cloned.1.call-update) | async-done | bytes 1048592 | tf_op jit(solution)/shard_map/all_gather | solution.py:46
  102.1 2.2 fusion.27
  107.2 6.0 collective-permute-start.5
  113.2 59.9 %all-gather.5.cloned.1.call-done = f32[2,4,256,128]{3,1,0,2:T(4,128)} async-done(((f32[2,4,16,128]{3,1,0,2:T(4,128)}), f32[2,4,256,128]{3,1,0,2:T(4,128)}) %all-gather.5.cloned.1.call-update) | async-done | bytes 1048592 | tf_op jit(solution)/shard_map/all_gather | solution.py:46
  173.1 2.3 fusion.26
  178.9 6.2 collective-permute-start.11
  192.2 3.2 pad_maximum_fusion.1
  198.9 278.9 %while.17 = (s32[]{:T(128)}, f32[4,272,144]{2,1,0:T(8,128)}, bf16[16,4,256,128]{3,2,1,0:T(8,128)(2,1)}, s32[16,2]{0,1:T(2,128)S(1)}, f32[2,4,272,144]{3,2,1,0:T(...) while((s32[]{:T(128)}, f32[4,272,144]{2,1,0:T(8,128)}, ...), condition=%wide.region_1.2_spmd, body=%wide.region_0.1_spmd.sunk | while | flops 1441810 | bytes 11830137 | solution.py:73
  210.2 6.2 dynamic_update_slice.19
  227.7 6.3 dynamic_update_slice.19
  245.3 5.3 dynamic_update_slice.19
  261.8 6.3 dynamic_update_slice.19
  279.4 6.3 dynamic_update_slice.19
  296.9 6.3 dynamic_update_slice.19
  314.5 6.2 dynamic_update_slice.19
  332.1 6.3 dynamic_update_slice.19
  349.6 6.3 dynamic_update_slice.19
  367.2 5.2 dynamic_update_slice.19
  383.7 6.3 dynamic_update_slice.19
  401.3 6.2 dynamic_update_slice.19
  418.9 6.2 dynamic_update_slice.19
  436.4 6.3 dynamic_update_slice.19
  454.0 6.3 dynamic_update_slice.19
  471.5 6.2 dynamic_update_slice.19
  477.8 2.3 slice.209
  480.1 139.4 %all-reduce.6.cloned.1.call-done = f32[4,256,144]{2,1,0:T(8,128)} async-done(((f32[4,256,144]{2,1,0:T(8,128)}), f32[4,256,144]{2,1,0:T(8,128)}) %all-reduce.6.cloned.1.call-update) | async-done | bytes 589840 | tf_op jit(solution)/shard_map/psum | solution.py:75
  622.3 6.0 collective-permute-start.13
  (148 shorter events, 137.0 us)
Async XLA Ops:
  7.2 95.0 %all-gather.3.cloned.1.call-start = ((), (), s32[]{:S(2)}) async-start(), calls=%async_computation | async-start | bytes 1114112 | tf_op jit(solution)/shard_map/all_gather | solution.py:46
  8.1 9.5 %collective-permute-start = (f32[2,4,16,1]{3,2,1,0:T(8,128)S(1)}, f32[2,4,16,1]{3,2,1,0:T(8,128)S(1)}, u32[]{:S(2)}, u32[]{:S(2)}) collective-permute-start(f32[2,4,16,1]{3,2,1,0:T(8,128)S(1)} %get-tuple-element.202), channel_id=1, source_target_pairs={{0,16},{16,32},{32,48},{48,64},{64,80},{80,96},{96,112},{112,128},... | collective-permute-start | bytes 1544 | tf_op jit(solution)/shard_map/ppermute | solution.py:16
  10.1 7.9 %collective-permute-start.1 = (f32[2,4,16,1]{3,2,1,0:T(8,128)S(1)}, f32[2,4,16,1]{3,2,1,0:T(8,128)S(1)}, u32[]{:S(2)}, u32[]{:S(2)}) collective-permute-start(f32[2,4,16,1]{3,2,1,0:T(8,128)S(1)} %get-tuple-element.203), channel_id=1, source_target_pairs={{16,0},{32,16},{48,32},{64,48},{80,64},{96,80},{112,96},{128,112},... | collective-permute-start | bytes 1544 | tf_op jit(solution)/shard_map/ppermute | solution.py:19
  18.9 7.0 %collective-permute-start.2 = (f32[2,4,1,130]{3,1,2,0:T(4,128)S(1)}, f32[2,4,1,130]{3,1,2,0:T(4,128)S(1)}, u32[]{:S(2)}, u32[]{:S(2)}) collective-permute-start(f32[2,4,1,130]{3,1,2,0:T(4,128)S(1)} %copy.83), channel_id=1, source_target_pairs={{1,0},{2,1},{3,2},{4,3},{5,4},{6,5},{7,6},{8,7},{9,8},{10,9},{11,1... | collective-permute-start | bytes 12488 | tf_op jit(solution)/shard_map/ppermute | solution.py:19
  20.2 5.9 collective-permute-start.3
  27.0 146.1 %all-gather.5.cloned.1.call-start = ((), (), s32[]{:S(2)}) async-start(), calls=%async_computation.1 | async-start | bytes 1114112 | tf_op jit(solution)/shard_map/all_gather | solution.py:46
  28.0 8.0 %collective-permute-start.6 = (f32[2,4,16,1]{3,1,0,2:T(4,128)S(1)}, f32[2,4,16,1]{3,1,0,2:T(4,128)S(1)}, u32[]{:S(2)}, u32[]{:S(2)}) collective-permute-start(f32[2,4,16,1]{3,1,0,2:T(4,128)S(1)} %get-tuple-element.198), channel_id=1, source_target_pairs={{0,16},{16,32},{32,48},{48,64},{64,80},{80,96},{96,112},{112,128},... | collective-permute-start | bytes 1544 | tf_op jit(solution)/shard_map/ppermute | solution.py:16
  31.5 6.4 %collective-permute-start.7 = (f32[2,4,16,1]{3,1,0,2:T(4,128)S(1)}, f32[2,4,16,1]{3,1,0,2:T(4,128)S(1)}, u32[]{:S(2)}, u32[]{:S(2)}) collective-permute-start(f32[2,4,16,1]{3,1,0,2:T(4,128)S(1)} %get-tuple-element.197), channel_id=1, source_target_pairs={{16,0},{32,16},{48,32},{64,48},{80,64},{96,80},{112,96},{128,112},... | collective-permute-start | bytes 1544 | tf_op jit(solution)/shard_map/ppermute | solution.py:19
  38.7 6.2 collective-permute-start.8
  40.0 6.3 collective-permute-start.9
  48.5 571.0 %all-reduce.6.cloned.1.call-start = ((), (), s32[]{:S(2)}) async-start(), calls=%async_computation.2 | async-start | bytes 2097152 | tf_op jit(solution)/shard_map/psum | solution.py:75
  104.8 80.3 %collective-permute-start.4 = (f32[2,4,256,8]{2,3,1,0:T(8,128)S(1)}, f32[2,4,256,8]{2,3,1,0:T(8,128)S(1)}, u32[]{:S(2)}, u32[]{:S(2)}) collective-permute-start(f32[2,4,256,8]{2,3,1,0:T(8,128)S(1)} %copy.68), channel_id=1, source_target_pairs={{0,16},{16,32},{32,48},{48,64},{64,80},{80,96},{96,112},{112,128},... | collective-permute-start | bytes 196616 | tf_op jit(solution)/shard_map/ppermute | solution.py:16
  107.2 78.5 %collective-permute-start.5 = (f32[2,4,256,8]{2,3,1,0:T(8,128)S(1)}, f32[2,4,256,8]{2,3,1,0:T(8,128)S(1)}, u32[]{:S(2)}, u32[]{:S(2)}) collective-permute-start(f32[2,4,256,8]{2,3,1,0:T(8,128)S(1)} %copy.69), channel_id=1, source_target_pairs={{16,0},{32,16},{48,32},{64,48},{80,64},{96,80},{112,96},{128,112},... | collective-permute-start | bytes 196616 | tf_op jit(solution)/shard_map/ppermute | solution.py:19
  175.4 10.7 %copy-start = (f32[2,4,256,128]{3,1,0,2:T(4,128)S(1)}, f32[2,4,256,128]{3,1,0,2:T(4,128)}, u32[]{:S(2)}) copy-start(f32[2,4,256,128]{3,1,0,2:T(4,128)} %all-gather.3.cloned.1.call-done) | copy-start | bytes 3145732
  175.9 12.8 %collective-permute-start.10 = (f32[2,4,256,8]{2,3,1,0:T(8,128)S(1)}, f32[2,4,256,8]{2,3,1,0:T(8,128)S(1)}, u32[]{:S(2)}, u32[]{:S(2)}) collective-permute-start(f32[2,4,256,8]{2,3,1,0:T(8,128)S(1)} %copy.77), channel_id=1, source_target_pairs={{0,16},{16,32},{32,48},{48,64},{64,80},{80,96},{96,112},{112,128},... | collective-permute-start | bytes 196616 | tf_op jit(solution)/shard_map/ppermute | solution.py:16
  178.9 11.2 %collective-permute-start.11 = (f32[2,4,256,8]{2,3,1,0:T(8,128)}, f32[2,4,256,8]{2,3,1,0:T(8,128)}, u32[]{:S(2)}, u32[]{:S(2)}) collective-permute-start(f32[2,4,256,8]{2,3,1,0:T(8,128)} %copy.78), channel_id=1, source_target_pairs={{16,0},{32,16},{48,32},{64,48},{80,64},{96,80},{112,96},{128,112},... | collective-permute-start | bytes 196616 | tf_op jit(solution)/shard_map/ppermute | solution.py:19
  188.7 3.5 copy-start.1
  196.1 2.7 copy-start.2
  620.4 8.9 %collective-permute-start.12 = (f32[4,16,8]{2,1,0:T(8,128)S(1)}, f32[4,16,8]{2,1,0:T(8,128)S(1)}, u32[]{:S(2)}, u32[]{:S(2)}) collective-permute-start(f32[4,16,8]{2,1,0:T(8,128)S(1)} %get-tuple-element.188), channel_id=1, source_target_pairs={{0,16},{16,32},{32,48},{48,64},{64,80},{80,96},{96,112},{112,128},... | collective-permute-start | bytes 6152 | tf_op jit(solution)/shard_map/ppermute | solution.py:27
  622.3 8.1 %collective-permute-start.13 = (f32[4,16,8]{2,1,0:T(8,128)S(1)}, f32[4,16,8]{2,1,0:T(8,128)S(1)}, u32[]{:S(2)}, u32[]{:S(2)}) collective-permute-start(f32[4,16,8]{2,1,0:T(8,128)S(1)} %get-tuple-element.187), channel_id=1, source_target_pairs={{16,0},{32,16},{48,32},{64,48},{80,64},{96,80},{112,96},{128,112},... | collective-permute-start | bytes 6152 | tf_op jit(solution)/shard_map/ppermute | solution.py:27
Sparse Core Ops, SparseCore 0:
  27.1 74.9 all-gather.2
  103.9 69.1 all-gather.4
  480.2 139.2 all-reduce.5
where the time goes:
time: 650 us; the launch traced here: 638 us
  waiting for transfers between devices  257 us (40%)
  local copies, waits for them, and re-layouts  163 us (25%)
  loops' own time  84.1 us (13%)
  other arithmetic  68.3 us (11%)
  starting transfers between devices  52.2 us (8%)
  between operations  14.1 us (2%)
    psum x1, waiting for transfers between devices, on_device(): total = lax.psum(partial_value, 'offset')  139 us
    all_gather x2, waiting for transfers between devices, on_device(): snap = lax.all_gather(now, 'offset', axis=2, tiled=True)  113 us
    dynamic_update_slice x16, local copies, waits for them, and re-layouts, per_offset(): carry = lax.dynamic_update_slice(carry, window + term, starts)  98.3 us
    another operation x1, loops' own time, on_device(): carry, image = lax.scan(per_offset, start, (shift_table, ref_image))  84.1 us
    add x16, other arithmetic, per_offset(): carry = lax.dynamic_update_slice(carry, window + term, starts)  32.9 us
    slice x16, local copies, waits for them, and re-layouts, per_offset(): pair[0]  31.5 us
    ppermute x6, starting transfers between devices, with_halo(): lax.ppermute(lax.slice_in_dim(block, 0, width, axis=dim), axis, backward)  25.4 us
    dynamic_update_slice x16, other arithmetic, on_device(): carry, image = lax.scan(per_offset, start, (shift_table, ref_image))  21.6 us
  transfers between devices with their start and end apart: 17, of which 7 were waited for; matrix products, arithmetic and copies ran while one was open for 3% of the time, Pallas kernels for 0%

commit v1 on v0

v1 whole, which is shorter than its diff:
```python
import jax
import jax.numpy as jnp
from jax import lax
from jax.experimental import pallas as pl
from jax.experimental.pallas import tpu as pltpu
from jax.sharding import PartitionSpec as P

OFF_SIDE = 16
HMAX = 8
STEPS = 2
REACH = HMAX + STEPS
LANES = 128


def chain(count):
    forward = [(i, i + 1) for i in range(count - 1)]
    return forward, [(b, a) for a, b in forward]


def roll_lanes(x, shift):
    return pltpu.roll(x, shift, x.ndim - 1)


def wave_kernel(u_ref, tile_ref):
    depth = u_ref.shape[1]
    rows = tile_ref.shape[1]
    high_rows, width = u_ref.shape[2], u_ref.shape[3]
    lane = lax.broadcasted_iota(jnp.int32, (rows, LANES), 1)
    speed = [u_ref[4, z] for z in range(depth)]

    def advance(prev, now):
        out = []
        for z in range(depth):
            c = now[z]
            beside = pltpu.roll(c, 1, 0) + pltpu.roll(c, high_rows - 1, 0)
            beside = beside + roll_lanes(c, 1) + roll_lanes(c, width - 1)
            if z > 0:
                beside = beside + now[z - 1]
            if z < depth - 1:
                beside = beside + now[z + 1]
            out.append(2.0 * c - prev[z] + speed[z] * (beside - 6.0 * c))
        return out

    packed = [jnp.zeros((rows, LANES), jnp.float32) for _ in range(2)]
    for pair in range(2):
        prev = [u_ref[2 * pair, z] for z in range(depth)]
        now = [u_ref[2 * pair + 1, z] for z in range(depth)]
        for t in range(STEPS):
            prev, now = now, advance(prev, now)
            for z in range(depth):
                plane = (pair * STEPS + t) * depth + z
                tile_ref[plane] = now[z][:rows, :LANES]
                q = plane % 8
                beside = roll_lanes(now[z][:rows, LANES:], (8 + 16 * q) % LANES)
                here = (lane >= 16 * q) & (lane < 16 * q + 16)
                packed[plane // 8] = jnp.where(here, beside, packed[plane // 8])
    for k in range(2):
        tile_ref[4 * depth + k] = packed[k]


def image_kernel(place_ref, shifts_ref, *refs):
    tiles = refs[:8]
    ref_ref, image_ref, adj_ref, main, side, acc, acc_side = refs[8:]
    step = pl.program_id(0)
    depth, all_rows = ref_ref.shape[1], ref_ref.shape[2]
    rows = tiles[0].shape[2]
    planes = 4 * depth

    @pl.when(step == 0)
    def _():
        zeros = jnp.zeros((planes, HMAX, LANES), jnp.float32)
        for edge in (0, HMAX + all_rows):
            main[:, edge:edge + HMAX, :] = zeros
            side[:, edge:edge + HMAX, :] = zeros
        acc[...] = jnp.zeros_like(acc)
        acc_side[...] = jnp.zeros_like(acc_side)
        for r in range(8):
            z_at = lax.rem(place_ref[0] + r, 8)
            for half in range(2):
                start = pl.multiple_of(HMAX + (2 * z_at + half) * rows, 8)
                for p in range(planes):
                    main[p, pl.ds(start, rows), :] = tiles[r][half, p]
                    packed = tiles[r][half, planes + p // 8]
                    back = (-(8 + 16 * (p % 8))) % LANES
                    side[p, pl.ds(start, rows), :] = roll_lanes(packed, back)

    hx = shifts_ref[step, 0]
    hy = shifts_ref[step, 1]
    block = 64
    lane = lax.broadcasted_iota(jnp.int32, (block, LANES), 1)
    wrap_s = (lane < -hx) | (lane >= LANES - hx)
    wrap_r = (lane < hx) | (lane >= LANES + hx)
    to_s = lax.rem(hx + LANES, LANES)
    to_r = lax.rem(LANES - hx, LANES)

    def rows_of(at, carry):
        z = at // (all_rows // block)
        r0 = pl.multiple_of(lax.rem(at, all_rows // block) * block, block)
        s_at = r0 + HMAX - hy
        r_at = r0 + HMAX + hy

        def shifted(plane, start, wrap, amount):
            a = main[plane, pl.ds(start, block), :]
            b = side[plane, pl.ds(start, block), :]
            return pltpu.roll(jnp.where(wrap, b, a), amount, 1)

        s1 = shifted(z, s_at, wrap_s, to_s)
        r1 = shifted(2 * depth + z, r_at, wrap_r, to_r)
        s2 = shifted(depth + z, s_at, wrap_s, to_s)
        r2 = shifted(3 * depth + z, r_at, wrap_r, to_r)
        full = s1 * r1 + s2 * r2
        image_ref[0, z, pl.ds(r0, block), :] = full.astype(jnp.bfloat16)
        observed = ref_ref[0, z, pl.ds(r0, block), :].astype(jnp.float32)
        term = pltpu.roll((full - observed) * s2, to_s, 1)
        acc[z, pl.ds(r_at, block), :] += jnp.where(wrap_r, 0.0, term)
        acc_side[z, pl.ds(r_at, block), :] += jnp.where(wrap_r, term, 0.0)
        return carry

    lax.fori_loop(0, depth * (all_rows // block), rows_of, 0)

    @pl.when(step == pl.num_programs(0) - 1)
    def _():
        lane8 = lax.broadcasted_iota(jnp.int32, (8, LANES), 1)
        for tile in range(all_rows // rows):
            strip = jnp.zeros((8, LANES), jnp.float32)
            for z in range(depth):
                at = HMAX + tile * rows
                adj_ref[tile, z * rows:(z + 1) * rows, :] = acc[z, at:at + rows, :]
                for half in range(2):
                    q = half * 4 + z
                    part = acc_side[z, at + 8 * half:at + 8 * half + 8, :]
                    part = pltpu.roll(part, (8 + 16 * q) % LANES, 1)
                    here = (lane8 >= 16 * q) & (lane8 < 16 * q + 16)
                    strip = jnp.where(here, part, strip)
            adj_ref[tile, depth * rows:, :] = strip


def total_kernel(parts_ref, core_ref, strip_ref):
    total = parts_ref[0]
    for i in range(1, parts_ref.shape[0]):
        total = total + parts_ref[i]
    n = core_ref.shape[0]
    core_ref[...] = total[:n]
    strip_ref[...] = total[n:]


def finish_kernel(core_ref, left_ref, right_ref, out_ref):
    depth, rows = out_ref.shape[0], out_ref.shape[1]
    lane = lax.broadcasted_iota(jnp.int32, (8, LANES), 1)
    for z in range(depth):
        for half in range(2):
            q = half * 4 + z
            back = (-(8 + 16 * q)) % LANES
            from_left = pltpu.roll(left_ref[...], back, 1)
            from_right = pltpu.roll(right_ref[...], back, 1)
            extra = jnp.where(lane < HMAX, from_left, 0.0)
            extra = jnp.where(lane >= LANES - HMAX, from_right, extra)
            at = z * rows + 8 * half
            out_ref[z, 8 * half:8 * half + 8, :] = (core_ref[at:at + 8, :] + extra) / OFF_SIDE


def on_device(src_prev, src_now, rcv_prev, rcv_now, velocity, shift_table, ref_image):
    depth, rows, cols = src_now.shape
    n_off = lax.axis_size("offset")
    n_space = lax.axis_size("space")
    all_rows = ref_image.shape[2]
    raw = jnp.stack([src_prev, src_now, rcv_prev, rcv_now, velocity])
    forward, backward = chain(n_space)
    low = lax.ppermute(raw[..., cols - REACH:], "space", forward)
    high = lax.ppermute(raw[..., :REACH], "space", backward)
    gap = jnp.zeros(raw.shape[:-1] + (LANES - 2 * REACH,), jnp.float32)
    wide = jnp.concatenate([raw, high, gap, low], axis=-1)
    forward, backward = chain(n_off)
    top = lax.ppermute(wide[:, :, rows - STEPS:], "offset", forward)
    bottom = lax.ppermute(wide[:, :, :STEPS], "offset", backward)
    gap = jnp.zeros(wide.shape[:2] + (8 - 2 * STEPS,) + wide.shape[3:], jnp.float32)
    wide = jnp.concatenate([wide, bottom, gap, top], axis=2)
    planes = 4 * depth + 2
    tile = pl.pallas_call(
        wave_kernel,
        out_shape=jax.ShapeDtypeStruct((planes, rows, LANES), jnp.float32),
        name="wave",
    )(wide)

    me = lax.axis_index("offset")
    other = lax.ppermute(tile, "offset", [(i, i ^ 1) for i in range(n_off)])
    is_low = (me % 2) == 0
    pair = jnp.stack([jnp.where(is_low, tile, other), jnp.where(is_low, other, tile)])

    def turn(d):
        return [(i, (i - 2 * d) % n_off) for i in range(n_off)]

    tiles = [pair] + [None] * 7
    up = down = pair
    for d in range(1, 4):
        up = lax.ppermute(up, "offset", turn(1))
        down = lax.ppermute(down, "offset", turn(-1))
        tiles[d], tiles[8 - d] = up, down
    far_a = lax.ppermute(up[0], "offset", turn(1))
    far_b = lax.ppermute(down[1], "offset", turn(-1))
    tiles[4] = jnp.stack([far_a, far_b])

    local = shift_table.shape[0]
    place = (me // 2).astype(jnp.int32)[None]
    whole = pl.BlockSpec(memory_space=pltpu.VMEM)
    scalars = pl.BlockSpec(memory_space=pltpu.SMEM)
    per_offset = pl.BlockSpec((1, depth, all_rows, cols), lambda i: (i, 0, 0, 0))
    padded_rows = all_rows + 2 * HMAX
    image, parts = pl.pallas_call(
        image_kernel,
        grid=(local,),
        in_specs=[scalars, scalars] + [whole] * 8 + [per_offset],
        out_specs=[per_offset, pl.BlockSpec((n_off, (depth * rows) + 8, LANES), lambda i: (0, 0, 0))],
        out_shape=[
            jax.ShapeDtypeStruct(ref_image.shape, jnp.bfloat16),
            jax.ShapeDtypeStruct((n_off, depth * rows + 8, LANES), jnp.float32),
        ],
        scratch_shapes=[
            pltpu.VMEM((4 * depth, padded_rows, LANES), jnp.float32),
            pltpu.VMEM((4 * depth, padded_rows, LANES), jnp.float32),
            pltpu.VMEM((depth, padded_rows, LANES), jnp.float32),
            pltpu.VMEM((depth, padded_rows, LANES), jnp.float32),
        ],
        compiler_params=pltpu.CompilerParams(vmem_limit_bytes=48 * 2**20),
        name="image",
    )(place, shift_table, *tiles, ref_image)

    parts = lax.all_to_all(parts, "offset", 0, 0)
    core, strip = pl.pallas_call(
        total_kernel,
        out_shape=[
            jax.ShapeDtypeStruct((depth * rows, LANES), jnp.float32),
            jax.ShapeDtypeStruct((8, LANES), jnp.float32),
        ],
        name="total",
    )(parts)
    forward, backward = chain(n_space)
    left = lax.ppermute(strip, "space", forward)
    right = lax.ppermute(strip, "space", backward)
    adjoint = pl.pallas_call(
        finish_kernel,
        out_shape=jax.ShapeDtypeStruct((depth, rows, cols), jnp.float32),
        name="finish",
    )(core, left, right)
    return image, adjoint


def solution(mesh):
    field = P(None, "offset", "space")
    in_specs = (field,) * 5 + (P("offset", None), P("offset", None, None, "space"))
    out_specs = (P("offset", None, None, "space"), field)
    return jax.shard_map(
        on_device, mesh=mesh, in_specs=in_specs, out_specs=out_specs, check_vma=False
    )
```

time: 650 us -> 160 us (0.25); the launches traced: 638 us -> 159 us
  waiting for transfers between devices: 257 us -> 38.4 us
  local copies, waits for them, and re-layouts: 163 us -> 4.7 us
  loops' own time: 84.1 us -> 0 us
  other arithmetic: 68.3 us -> 2.08 us
  Pallas kernels: 0 us -> 54 us
  blocking collectives: 0 us -> 21.7 us
  starting transfers between devices: 52.2 us -> 37.3 us
  between operations: 14.1 us -> 0.79 us
    psum x1 -> x0, waiting for transfers between devices: 139 us -> none  [on_device(): total = lax.psum(partial_value, 'offset')]
    all_gather x2 -> x0, waiting for transfers between devices: 113 us -> none  [on_device(): snap = lax.all_gather(now, 'offset', axis=2, tiled=True)]
    dynamic_update_slice x16 -> x0, local copies, waits for them, and re-layouts: 98.3 us -> none  [per_offset(): carry = lax.dynamic_update_slice(carry, window + term, starts)]
    another operation x1 -> x0, loops' own time: 84.1 us -> none  [on_device(): carry, image = lax.scan(per_offset, start, (shift_table, ref_image))]
    pallas_call x0 -> x4, Pallas kernels: none -> 54 us  [the longest x1 48.7 us: on_device(): pl.pallas_call(image_kernel, grid=(local,), in_specs=[scalars, scalars] +...]
    slice x43 -> x1, local copies, waits for them, and re-layouts: 52.9 us -> 0.1 us  [on_device(): high = lax.ppermute(raw[..., :REACH], 'space', backward)]
    add x20 -> x0, other arithmetic: 36.9 us -> none  [the longest x16 32.9 us: per_offset(): carry = lax.dynamic_update_slice(carry, window + term, starts)]
    ppermute x14 -> x15, waiting for transfers between devices: 3.76 us -> 38.4 us  [the longest x3 18.5 us: on_device(): down = lax.ppermute(down, 'offset', turn(-1))]
  transfers between devices with their start and end apart: 17 -> 15, of which waited for: 7 -> 9; matrix products, arithmetic and copies ran while one was open for 3% -> 0% of each run, Pallas kernels for 0% -> 0%
where the time goes in v1:
time: 160 us; the launch traced here: 159 us
  Pallas kernels  54 us (34%)
  waiting for transfers between devices  38.4 us (24%)
  starting transfers between devices  37.3 us (23%)
  blocking collectives  21.7 us (14%)
  local copies, waits for them, and re-layouts  4.7 us (3%)
  other arithmetic  2.08 us (1%)
    pallas_call x1, Pallas kernels, on_device(): pl.pallas_call(image_kernel, grid=(local,), in_specs=[scalars, scalars] +...  48.7 us
    all_to_all x1, blocking collectives, on_device(): parts = lax.all_to_all(parts, 'offset', 0, 0)  21.7 us
    ppermute x3, waiting for transfers between devices, on_device(): down = lax.ppermute(down, 'offset', turn(-1))  18.5 us
    ppermute x3, starting transfers between devices, on_device(): up = lax.ppermute(up, 'offset', turn(1))  12 us
    ppermute x1, waiting for transfers between devices, on_device(): low = lax.ppermute(raw[..., cols - REACH:], 'space', forward)  6.23 us
    ppermute x1, waiting for transfers between devices, on_device(): left = lax.ppermute(strip, 'space', forward)  5.11 us
    ppermute x1, starting transfers between devices, on_device(): top = lax.ppermute(wide[:, :, rows - STEPS:], 'offset', forward)  4.55 us
    ppermute x1, starting transfers between devices, on_device(): high = lax.ppermute(raw[..., :REACH], 'space', backward)  4.26 us
  transfers between devices with their start and end apart: 15, of which 9 were waited for; matrix products, arithmetic and copies ran while one was open for 0% of the time, Pallas kernels for 0%

profile of v1, /device:TPU:16, one launch (start us, length us, event | category | flops | bytes accessed | tf_op | source)
XLA Modules:
  0.0 159.0 jit_solution(8802361807145436047)
XLA Ops:
  0.6 0.8 bitcast_dynamic-update-slice_fusion.4
  1.4 0.8 bitcast_dynamic-update-slice_fusion.3
  2.2 0.8 bitcast_dynamic-update-slice_fusion.2
  2.9 0.8 bitcast_dynamic-update-slice_fusion.1
  4.6 4.3 %collective-permute-start = (f32[5,4,16,10]{3,2,1,0:T(8,128)S(1)}, f32[5,4,16,10]{3,2,1,0:T(8,128)S(1)}, u32[]{:S(2)}, u32[]{:S(2)}) collective-permute-start(f32[5,4,16,10]{3,2,1,0:T(8,128)S(1)} %get-tuple-element.14), channel_id=1, source_target_pairs={{16,0},{32,16},{48,32},{64,48},{80,64},{96,80},{112,96},{128,112},... | collective-permute-start | bytes 38408 | tf_op jit(solution)/shard_map/ppermute | solution.py:170
  8.8 1.9 %collective-permute-start.1 = (f32[5,4,16,10]{3,2,1,0:T(8,128)S(1)}, f32[5,4,16,10]{3,2,1,0:T(8,128)S(1)}, u32[]{:S(2)}, u32[]{:S(2)}) collective-permute-start(f32[5,4,16,10]{3,2,1,0:T(8,128)S(1)} %get-tuple-element.15), channel_id=1, source_target_pairs={{0,16},{16,32},{32,48},{48,64},{64,80},{80,96},{96,112},{112,128},... | collective-permute-start | bytes 38408 | tf_op jit(solution)/shard_map/ppermute | solution.py:169
  10.8 0.9 collective-permute-done
  11.6 6.2 %collective-permute-done.1 = f32[5,4,16,10]{3,2,1,0:T(8,128)S(1)} collective-permute-done((f32[5,4,16,10]{3,2,1,0:T(8,128)S(1)}, f32[5,4,16,10]{3,2,1,0:T(8,128)S(1)}, u32[]{:S(2)}, u32[]{:S(2)}) %collective-permute-start.1) | collective-permute-done | bytes 12832 | tf_op jit(solution)/shard_map/ppermute | solution.py:169
  18.0 1.3 collective-permute-start.2
  19.3 4.5 %collective-permute-start.3 = (f32[5,4,2,256]{3,2,1,0:T(2,128)S(1)}, f32[5,4,2,256]{3,2,1,0:T(2,128)S(1)}, u32[]{:S(2)}, u32[]{:S(2)}) collective-permute-start(f32[5,4,2,256]{3,2,1,0:T(2,128)S(1)} %get-tuple-element.11), channel_id=1, source_target_pairs={{0,1},{1,2},{2,3},{3,4},{4,5},{5,6},{6,7},{7,8},{8,9},{9,10},{10,1... | collective-permute-start | bytes 122888 | tf_op jit(solution)/shard_map/ppermute | solution.py:174
  24.0 1.6 collective-permute-done.3
  25.6 1.0 pad_maximum_fusion.u_ref
  26.5 2.1 %wave.1 = f32[18,16,128]{2,1,0:T(8,128)} custom-call(f32[5,4,24,256]{3,2,1,0:T(8,128)} %pad_maximum_fusion.u_ref), custom_call_target="tpu_custom_call" | custom-call | tf_op jit(solution)/shard_map/wave/pallas_call | solution.py:179
  28.6 2.3 %collective-permute-start.4 = (f32[18,16,128]{2,1,0:T(8,128)}, f32[18,16,128]{2,1,0:T(8,128)S(1)}, u32[]{:S(2)}, u32[]{:S(2)}) collective-permute-start(f32[18,16,128]{2,1,0:T(8,128)} %wave.1), channel_id=1, source_target_pairs={{0,1},{1,0},{2,3},{3,2},{4,5},{5,4},{6,7},{7,6},{8,9},{9,8},{10,11... | collective-permute-start | bytes 442376 | tf_op jit(solution)/shard_map/ppermute | solution.py:186
  30.9 3.3 %collective-permute-done.4 = f32[18,16,128]{2,1,0:T(8,128)S(1)} collective-permute-done((f32[18,16,128]{2,1,0:T(8,128)}, f32[18,16,128]{2,1,0:T(8,128)S(1)}, u32[]{:S(2)}, u32[]{:S(2)}) %collective-permute-start.4) | collective-permute-done | bytes 147488 | tf_op jit(solution)/shard_map/ppermute | solution.py:186
  34.3 0.9 select_bitcast_fusion.1
  35.2 3.0 %collective-permute-start.9 = (f32[2,18,16,128]{3,2,1,0:T(8,128)S(1)}, f32[2,18,16,128]{3,2,1,0:T(8,128)S(1)}, u32[]{:S(2)}, u32[]{:S(2)}) collective-permute-start(f32[2,18,16,128]{3,2,1,0:T(8,128)S(1)} %pad_maximum_fusion.1.refs_0_), channel_id=1, source_target_pairs={{0,2},{1,3},{2,4},{3,5},{4,6},{5,7},{6,8},{7,9},{8,10},{9,11},{10,... | collective-permute-start | bytes 884744 | tf_op jit(solution)/shard_map/ppermute | solution.py:197
  38.3 4.9 %collective-permute-start.5 = (f32[2,18,16,128]{3,2,1,0:T(8,128)S(1)}, f32[2,18,16,128]{3,2,1,0:T(8,128)S(1)}, u32[]{:S(2)}, u32[]{:S(2)}) collective-permute-start(f32[2,18,16,128]{3,2,1,0:T(8,128)S(1)} %pad_maximum_fusion.1.refs_0_), channel_id=1, source_target_pairs={{0,14},{1,15},{2,0},{3,1},{4,2},{5,3},{6,4},{7,5},{8,6},{9,7},{10,... | collective-permute-start | bytes 884744 | tf_op jit(solution)/shard_map/ppermute | solution.py:196
  43.2 7.5 %collective-permute-done.9.refs_7_ = f32[2,18,16,128]{3,2,1,0:T(8,128)S(1)} collective-permute-done((f32[2,18,16,128]{3,2,1,0:T(8,128)S(1)}, f32[2,18,16,128]{3,2,1,0:T(8,128)S(1)}, u32[]{:S(2)}, u32[]{:S(2)}) %collective-permute-start.9) | collective-permute-done | bytes 294944 | tf_op jit(solution)/shard_map/ppermute | solution.py:197
  50.7 3.6 %collective-permute-start.6 = (f32[2,18,16,128]{3,2,1,0:T(8,128)S(1)}, f32[2,18,16,128]{3,2,1,0:T(8,128)S(1)}, u32[]{:S(2)}, u32[]{:S(2)}) collective-permute-start(f32[2,18,16,128]{3,2,1,0:T(8,128)S(1)} %collective-permute-done.5.refs_1_), channel_id=1, source_target_pairs={{0,14},{1,15},{2,0},{3,1},{4,2},{5,3},{6,4},{7,5},{8,6},{9,7},{10,... | collective-permute-start | bytes 884744 | tf_op jit(solution)/shard_map/ppermute | solution.py:196
  54.3 6.7 %collective-permute-done.10.refs_6_ = f32[2,18,16,128]{3,2,1,0:T(8,128)S(1)} collective-permute-done((f32[2,18,16,128]{3,2,1,0:T(8,128)S(1)}, f32[2,18,16,128]{3,2,1,0:T(8,128)S(1)}, u32[]{:S(2)}, u32[]{:S(2)}) %collective-permute-start.10) | collective-permute-done | bytes 294944 | tf_op jit(solution)/shard_map/ppermute | solution.py:197
  61.0 3.6 %collective-permute-start.7 = (f32[2,18,16,128]{3,2,1,0:T(8,128)S(1)}, f32[2,18,16,128]{3,2,1,0:T(8,128)S(1)}, u32[]{:S(2)}, u32[]{:S(2)}) collective-permute-start(f32[2,18,16,128]{3,2,1,0:T(8,128)S(1)} %collective-permute-done.6.refs_2_), channel_id=1, source_target_pairs={{0,14},{1,15},{2,0},{3,1},{4,2},{5,3},{6,4},{7,5},{8,6},{9,7},{10,... | collective-permute-start | bytes 884744 | tf_op jit(solution)/shard_map/ppermute | solution.py:196
  64.5 4.4 %collective-permute-done.11.refs_5_ = f32[2,18,16,128]{3,2,1,0:T(8,128)S(1)} collective-permute-done((f32[2,18,16,128]{3,2,1,0:T(8,128)S(1)}, f32[2,18,16,128]{3,2,1,0:T(8,128)S(1)}, u32[]{:S(2)}, u32[]{:S(2)}) %collective-permute-start.11) | collective-permute-done | bytes 294944 | tf_op jit(solution)/shard_map/ppermute | solution.py:197
  69.0 3.5 %collective-permute-start.8 = (f32[18,16,128]{2,1,0:T(8,128)S(1)}, f32[18,16,128]{2,1,0:T(8,128)S(1)}, u32[]{:S(2)}, u32[]{:S(2)}) collective-permute-start(f32[18,16,128]{2,1,0:T(8,128)S(1)} %slice_bitcast_fusion.1), channel_id=1, source_target_pairs={{0,14},{1,15},{2,0},{3,1},{4,2},{5,3},{6,4},{7,5},{8,6},{9,7},{10,... | collective-permute-start | bytes 442376 | tf_op jit(solution)/shard_map/ppermute | solution.py:199
  72.6 2.7 %collective-permute-done.12 = f32[18,16,128]{2,1,0:T(8,128)S(1)} collective-permute-done((f32[18,16,128]{2,1,0:T(8,128)S(1)}, f32[18,16,128]{2,1,0:T(8,128)S(1)}, u32[]{:S(2)}, u32[]{:S(2)}) %collective-permute-start.12) | collective-permute-done | bytes 147488 | tf_op jit(solution)/shard_map/ppermute | solution.py:200
  75.4 48.7 %image.1 = (bf16[16,4,256,128]{3,2,1,0:T(8,128)(2,1)}, f32[16,72,128]{2,1,0:T(8,128)S(1)}) custom-call(s32[1]{0:T(128)} %bitcast.place_ref, s32[16,2]{1,0:T(8,128)S(1)} %copy.9.shifts_ref, f32[2,18,16,128]{3,2,1,0:T(8,128)S(1)} %pad_maximum_fusion.1.refs_0_, f32[2,18,16,128]{3,2,1,0:T(8,128)S(1)} %collective-permute-done.5.refs_1_, ...), custom_call_target="tpu_custom_call" | custom-call | tf_op jit(solution)/shard_map/image/pallas_call | solution.py:209
  124.1 21.7 %all_to_all.5.parts_ref = f32[16,72,128]{2,1,0:T(8,128)} all-to-all(f32[16,72,128]{2,1,0:T(8,128)S(1)} %get-tuple-element.7), channel_id=1, replica_groups=mesh['space'=16,'offset'=16] {'offset'}, dimensions={0} | all-to-all | bytes 1179648 | tf_op jit(solution)/shard_map/all_to_all | solution.py:228
  145.8 1.7 %total.1 = (f32[64,128]{1,0:T(8,128)}, f32[8,128]{1,0:T(8,128)}) custom-call(f32[16,72,128]{2,1,0:T(8,128)} %all_to_all.5.parts_ref), custom_call_target="tpu_custom_call" | custom-call | tf_op jit(solution)/shard_map/total/pallas_call | solution.py:229
  147.5 1.9 %collective-permute-start.14 = (f32[8,128]{1,0:T(8,128)}, f32[8,128]{1,0:T(8,128)S(1)}, u32[]{:S(2)}, u32[]{:S(2)}) collective-permute-start(f32[8,128]{1,0:T(8,128)} %get-tuple-element.9), channel_id=1, source_target_pairs={{16,0},{32,16},{48,32},{64,48},{80,64},{96,80},{112,96},{128,112},... | collective-permute-start | bytes 12296 | tf_op jit(solution)/shard_map/ppermute | solution.py:239
  149.4 2.4 %collective-permute-start.13 = (f32[8,128]{1,0:T(8,128)}, f32[8,128]{1,0:T(8,128)S(1)}, u32[]{:S(2)}, u32[]{:S(2)}) collective-permute-start(f32[8,128]{1,0:T(8,128)} %get-tuple-element.9), channel_id=1, source_target_pairs={{0,16},{16,32},{32,48},{48,64},{64,80},{80,96},{96,112},{112,128},... | collective-permute-start | bytes 12296 | tf_op jit(solution)/shard_map/ppermute | solution.py:238
  151.8 5.1 %collective-permute-done.13.left_ref = f32[8,128]{1,0:T(8,128)S(1)} collective-permute-done((f32[8,128]{1,0:T(8,128)}, f32[8,128]{1,0:T(8,128)S(1)}, u32[]{:S(2)}, u32[]{:S(2)}) %collective-permute-start.13) | collective-permute-done | bytes 4128 | tf_op jit(solution)/shard_map/ppermute | solution.py:238
  157.5 1.5 finish.1
  (26 shorter events, 2.0 us)
Async XLA Ops:
  0.6 71.9 %copy-start.2 = (s32[16,2]{0,1:T(2,128)S(1)}, s32[16,2]{0,1:T(2,128)}, u32[]{:S(2)}) copy-start(s32[16,2]{0,1:T(2,128)} %param.12) | copy-start | bytes 388
  4.6 7.1 %collective-permute-start = (f32[5,4,16,10]{3,2,1,0:T(8,128)S(1)}, f32[5,4,16,10]{3,2,1,0:T(8,128)S(1)}, u32[]{:S(2)}, u32[]{:S(2)}) collective-permute-start(f32[5,4,16,10]{3,2,1,0:T(8,128)S(1)} %get-tuple-element.14), channel_id=1, source_target_pairs={{16,0},{32,16},{48,32},{64,48},{80,64},{96,80},{112,96},{128,112},... | collective-permute-start | bytes 38408 | tf_op jit(solution)/shard_map/ppermute | solution.py:170
  8.8 9.0 %collective-permute-start.1 = (f32[5,4,16,10]{3,2,1,0:T(8,128)S(1)}, f32[5,4,16,10]{3,2,1,0:T(8,128)S(1)}, u32[]{:S(2)}, u32[]{:S(2)}) collective-permute-start(f32[5,4,16,10]{3,2,1,0:T(8,128)S(1)} %get-tuple-element.15), channel_id=1, source_target_pairs={{0,16},{16,32},{32,48},{48,64},{64,80},{80,96},{96,112},{112,128},... | collective-permute-start | bytes 38408 | tf_op jit(solution)/shard_map/ppermute | solution.py:169
  18.0 5.9 %collective-permute-start.2 = (f32[5,4,2,256]{3,2,1,0:T(2,128)S(1)}, f32[5,4,2,256]{3,2,1,0:T(2,128)S(1)}, u32[]{:S(2)}, u32[]{:S(2)}) collective-permute-start(f32[5,4,2,256]{3,2,1,0:T(2,128)S(1)} %get-tuple-element.10), channel_id=1, source_target_pairs={{1,0},{2,1},{3,2},{4,3},{5,4},{6,5},{7,6},{8,7},{9,8},{10,9},{11,1... | collective-permute-start | bytes 122888 | tf_op jit(solution)/shard_map/ppermute | solution.py:175
  19.3 6.2 %collective-permute-start.3 = (f32[5,4,2,256]{3,2,1,0:T(2,128)S(1)}, f32[5,4,2,256]{3,2,1,0:T(2,128)S(1)}, u32[]{:S(2)}, u32[]{:S(2)}) collective-permute-start(f32[5,4,2,256]{3,2,1,0:T(2,128)S(1)} %get-tuple-element.11), channel_id=1, source_target_pairs={{0,1},{1,2},{2,3},{3,4},{4,5},{5,6},{6,7},{7,8},{8,9},{9,10},{10,1... | collective-permute-start | bytes 122888 | tf_op jit(solution)/shard_map/ppermute | solution.py:174
  28.6 5.7 %collective-permute-start.4 = (f32[18,16,128]{2,1,0:T(8,128)}, f32[18,16,128]{2,1,0:T(8,128)S(1)}, u32[]{:S(2)}, u32[]{:S(2)}) collective-permute-start(f32[18,16,128]{2,1,0:T(8,128)} %wave.1), channel_id=1, source_target_pairs={{0,1},{1,0},{2,3},{3,2},{4,5},{5,4},{6,7},{7,6},{8,9},{9,8},{10,11... | collective-permute-start | bytes 442376 | tf_op jit(solution)/shard_map/ppermute | solution.py:186
  35.2 15.5 %collective-permute-start.9 = (f32[2,18,16,128]{3,2,1,0:T(8,128)S(1)}, f32[2,18,16,128]{3,2,1,0:T(8,128)S(1)}, u32[]{:S(2)}, u32[]{:S(2)}) collective-permute-start(f32[2,18,16,128]{3,2,1,0:T(8,128)S(1)} %pad_maximum_fusion.1.refs_0_), channel_id=1, source_target_pairs={{0,2},{1,3},{2,4},{3,5},{4,6},{5,7},{6,8},{7,9},{8,10},{9,11},{10,... | collective-permute-start | bytes 884744 | tf_op jit(solution)/shard_map/ppermute | solution.py:197
  38.3 12.4 %collective-permute-start.5 = (f32[2,18,16,128]{3,2,1,0:T(8,128)S(1)}, f32[2,18,16,128]{3,2,1,0:T(8,128)S(1)}, u32[]{:S(2)}, u32[]{:S(2)}) collective-permute-start(f32[2,18,16,128]{3,2,1,0:T(8,128)S(1)} %pad_maximum_fusion.1.refs_0_), channel_id=1, source_target_pairs={{0,14},{1,15},{2,0},{3,1},{4,2},{5,3},{6,4},{7,5},{8,6},{9,7},{10,... | collective-permute-start | bytes 884744 | tf_op jit(solution)/shard_map/ppermute | solution.py:196
  50.7 10.2 %collective-permute-start.10 = (f32[2,18,16,128]{3,2,1,0:T(8,128)S(1)}, f32[2,18,16,128]{3,2,1,0:T(8,128)S(1)}, u32[]{:S(2)}, u32[]{:S(2)}) collective-permute-start(f32[2,18,16,128]{3,2,1,0:T(8,128)S(1)} %collective-permute-done.9.refs_7_), channel_id=1, source_target_pairs={{0,2},{1,3},{2,4},{3,5},{4,6},{5,7},{6,8},{7,9},{8,10},{9,11},{10,... | collective-permute-start | bytes 884744 | tf_op jit(solution)/shard_map/ppermute | solution.py:197
  50.7 10.2 %collective-permute-start.6 = (f32[2,18,16,128]{3,2,1,0:T(8,128)S(1)}, f32[2,18,16,128]{3,2,1,0:T(8,128)S(1)}, u32[]{:S(2)}, u32[]{:S(2)}) collective-permute-start(f32[2,18,16,128]{3,2,1,0:T(8,128)S(1)} %collective-permute-done.5.refs_1_), channel_id=1, source_target_pairs={{0,14},{1,15},{2,0},{3,1},{4,2},{5,3},{6,4},{7,5},{8,6},{9,7},{10,... | collective-permute-start | bytes 884744 | tf_op jit(solution)/shard_map/ppermute | solution.py:196
  60.9 7.9 %collective-permute-start.11 = (f32[2,18,16,128]{3,2,1,0:T(8,128)S(1)}, f32[2,18,16,128]{3,2,1,0:T(8,128)S(1)}, u32[]{:S(2)}, u32[]{:S(2)}) collective-permute-start(f32[2,18,16,128]{3,2,1,0:T(8,128)S(1)} %collective-permute-done.10.refs_6_), channel_id=1, source_target_pairs={{0,2},{1,3},{2,4},{3,5},{4,6},{5,7},{6,8},{7,9},{8,10},{9,11},{10,... | collective-permute-start | bytes 884744 | tf_op jit(solution)/shard_map/ppermute | solution.py:197
  61.0 8.0 %collective-permute-start.7 = (f32[2,18,16,128]{3,2,1,0:T(8,128)S(1)}, f32[2,18,16,128]{3,2,1,0:T(8,128)S(1)}, u32[]{:S(2)}, u32[]{:S(2)}) collective-permute-start(f32[2,18,16,128]{3,2,1,0:T(8,128)S(1)} %collective-permute-done.6.refs_2_), channel_id=1, source_target_pairs={{0,14},{1,15},{2,0},{3,1},{4,2},{5,3},{6,4},{7,5},{8,6},{9,7},{10,... | collective-permute-start | bytes 884744 | tf_op jit(solution)/shard_map/ppermute | solution.py:196
  68.9 6.4 %collective-permute-start.12 = (f32[18,16,128]{2,1,0:T(8,128)S(1)}, f32[18,16,128]{2,1,0:T(8,128)S(1)}, u32[]{:S(2)}, u32[]{:S(2)}) collective-permute-start(f32[18,16,128]{2,1,0:T(8,128)S(1)} %slice_bitcast_fusion), channel_id=1, source_target_pairs={{0,2},{1,3},{2,4},{3,5},{4,6},{5,7},{6,8},{7,9},{8,10},{9,11},{10,... | collective-permute-start | bytes 442376 | tf_op jit(solution)/shard_map/ppermute | solution.py:200
  69.0 6.3 %collective-permute-start.8 = (f32[18,16,128]{2,1,0:T(8,128)S(1)}, f32[18,16,128]{2,1,0:T(8,128)S(1)}, u32[]{:S(2)}, u32[]{:S(2)}) collective-permute-start(f32[18,16,128]{2,1,0:T(8,128)S(1)} %slice_bitcast_fusion.1), channel_id=1, source_target_pairs={{0,14},{1,15},{2,0},{3,1},{4,2},{5,3},{6,4},{7,5},{8,6},{9,7},{10,... | collective-permute-start | bytes 442376 | tf_op jit(solution)/shard_map/ppermute | solution.py:199
  147.5 4.3 %collective-permute-start.14 = (f32[8,128]{1,0:T(8,128)}, f32[8,128]{1,0:T(8,128)S(1)}, u32[]{:S(2)}, u32[]{:S(2)}) collective-permute-start(f32[8,128]{1,0:T(8,128)} %get-tuple-element.9), channel_id=1, source_target_pairs={{16,0},{32,16},{48,32},{64,48},{80,64},{96,80},{112,96},{128,112},... | collective-permute-start | bytes 12296 | tf_op jit(solution)/shard_map/ppermute | solution.py:239
  149.4 7.5 %collective-permute-start.13 = (f32[8,128]{1,0:T(8,128)}, f32[8,128]{1,0:T(8,128)S(1)}, u32[]{:S(2)}, u32[]{:S(2)}) collective-permute-start(f32[8,128]{1,0:T(8,128)} %get-tuple-element.9), channel_id=1, source_target_pairs={{0,16},{16,32},{32,48},{48,64},{64,80},{80,96},{96,112},{112,128},... | collective-permute-start | bytes 12296 | tf_op jit(solution)/shard_map/ppermute | solution.py:238
  151.8 5.1 %copy-start = (f32[8,128]{1,0:T(8,128)}, f32[8,128]{1,0:T(8,128)S(1)}, u32[]{:S(2)}) copy-start(f32[8,128]{1,0:T(8,128)S(1)} %collective-permute-done.14.right_ref) | copy-start | bytes 12292
  157.0 0.6 copy-start.1

commit v2 on v1

v2 whole, which is shorter than its diff:
```python
import functools

import jax
import jax.numpy as jnp
from jax import lax
from jax.experimental import pallas as pl
from jax.experimental.pallas import tpu as pltpu
from jax.sharding import PartitionSpec as P

OFF_SIDE = 16
HMAX = 8
STEPS = 2
REACH = HMAX + STEPS
LANES = 128
UNROLL = 2
SMALL = pltpu.CompilerParams(vmem_limit_bytes=6 * 2**20)


def chain(count):
    forward = [(i, i + 1) for i in range(count - 1)]
    return forward, [(b, a) for a, b in forward]


def roll_lanes(x, shift):
    return pltpu.roll(x, shift, x.ndim - 1)


def stack_kernel(*refs):
    out_ref = refs[-1]
    for i, ref in enumerate(refs[:-1]):
        out_ref[i] = ref[...]


def widen_kernel(raw_ref, low_ref, high_ref, wide_ref, upper_ref, lower_ref):
    fields, depth, rows, cols = raw_ref.shape
    lane = lax.broadcasted_iota(jnp.int32, (rows, cols), 1)
    for f in range(fields):
        for z in range(depth):
            beside = jnp.where(lane >= cols - REACH, low_ref[f, z], 0.0)
            beside = jnp.where(lane < REACH, high_ref[f, z], beside)
            row = raw_ref[f, z]
            wide_ref[f, z, :, :cols] = row
            wide_ref[f, z, :, cols:] = beside
            upper_ref[f, z, :, :cols] = row[:8]
            upper_ref[f, z, :, cols:] = beside[:8]
            lower_ref[f, z, :, :cols] = row[rows - 8:]
            lower_ref[f, z, :, cols:] = beside[rows - 8:]


def wave_kernel(wide_ref, top_ref, bottom_ref, tile_ref):
    depth, rows, width = wide_ref.shape[1:]
    high_rows = rows + 8
    lane = lax.broadcasted_iota(jnp.int32, (rows, LANES), 1)
    edge_row = lax.broadcasted_iota(jnp.int32, (8, width), 0)

    def whole(f, z):
        edge = jnp.where(edge_row >= 8 - STEPS, top_ref[f, z], 0.0)
        edge = jnp.where(edge_row < STEPS, bottom_ref[f, z], edge)
        return jnp.concatenate([wide_ref[f, z], edge], axis=0)

    speed = [whole(4, z) for z in range(depth)]

    def advance(prev, now):
        out = []
        for z in range(depth):
            c = now[z]
            beside = pltpu.roll(c, 1, 0) + pltpu.roll(c, high_rows - 1, 0)
            beside = beside + roll_lanes(c, 1) + roll_lanes(c, width - 1)
            if z > 0:
                beside = beside + now[z - 1]
            if z < depth - 1:
                beside = beside + now[z + 1]
            out.append(2.0 * c - prev[z] + speed[z] * (beside - 6.0 * c))
        return out

    packed = [jnp.zeros((rows, LANES), jnp.float32) for _ in range(2)]
    for pair in range(2):
        prev = [whole(2 * pair, z) for z in range(depth)]
        now = [whole(2 * pair + 1, z) for z in range(depth)]
        for t in range(STEPS):
            prev, now = now, advance(prev, now)
            for z in range(depth):
                plane = (pair * STEPS + t) * depth + z
                tile_ref[plane] = now[z][:rows, :LANES]
                q = plane % 8
                beside = roll_lanes(now[z][:rows, LANES:], (8 + 16 * q) % LANES)
                here = (lane >= 16 * q) & (lane < 16 * q + 16)
                packed[plane // 8] = jnp.where(here, beside, packed[plane // 8])
    for k in range(2):
        tile_ref[4 * depth + k] = packed[k]


def needed(rels):
    return sorted({(r + k) % 8 for r in rels for k in (-1, 0, 1)})


def image_kernel(rels, first, last, *refs):
    refs = list(refs)
    place_ref, shifts_ref, observed_ref = refs[:3]
    del refs[:3]
    tiles = {}
    for r in needed(rels):
        tiles[r], refs = refs[:2], refs[2:]
    if not first:
        refs = refs[1:]
    earlier = {}
    if last:
        for r in range(8):
            if r not in rels:
                earlier[r], refs = refs[:2], refs[2:]
    image_hbm, core_out, side_out, main, side, image_buf, sems = refs[:7]
    if last:
        acc, acc_side, all_core, all_side = refs[7:]
    else:
        acc, acc_side = core_out, side_out
    count, depth, all_rows = observed_ref.shape[:3]
    planes = 4 * depth
    rows = all_rows // 8
    half = rows // 2
    z_of = [lax.rem(place_ref[0] + r, 8) for r in rels]

    def put(n):
        at = pl.multiple_of(z_of[n] * rows, rows)
        return pltpu.make_async_copy(
            image_buf.at[n], image_hbm.at[:, :, pl.ds(at, rows), :], sems.at[n]
        )

    acc[...] = jnp.zeros_like(acc)
    acc_side[...] = jnp.zeros_like(acc_side)
    for n, r in enumerate(rels):
        below, here, above = tiles[(r - 1) % 8], tiles[r], tiles[(r + 1) % 8]
        sources = [
            (0, below[1], slice(half - HMAX, half), z_of[n] > 0),
            (HMAX, here[0], slice(0, half), None),
            (HMAX + half, here[1], slice(0, half), None),
            (HMAX + rows, above[0], slice(0, HMAX), z_of[n] < 7),
        ]
        for at, ref, part, inside in sources:
            size = part.stop - part.start

            def load(p):
                value = ref[p, part, :]
                return value if inside is None else jnp.where(inside, value, 0.0)

            packs = [load(planes), load(planes + 1)]
            for p in range(planes):
                main[n, p, at:at + size, :] = load(p)
                back = (-(8 + 16 * (p % 8))) % LANES
                side[n, p, at:at + size, :] = roll_lanes(packs[p // 8], back)

    lane = lax.broadcasted_iota(jnp.int32, (rows, LANES), 1)

    def per_offset(o, carry):
        hx = shifts_ref[o, 0]
        hy = shifts_ref[o, 1]
        wrap_s = (lane < -hx) | (lane >= LANES - hx)
        wrap_r = (lane < hx) | (lane >= LANES + hx)
        to_s = lax.rem(hx + LANES, LANES)
        to_r = lax.rem(LANES - hx, LANES)
        s_at = HMAX - hy
        r_at = HMAX + hy

        def rotated(pieces, amount):
            turned = pltpu.roll(jnp.concatenate(pieces, axis=0), amount, 1)
            return [turned[i * rows:(i + 1) * rows] for i in range(len(pieces))]

        def piece(n, plane, start, wrap):
            a = main[n, plane, pl.ds(start, rows), :]
            return jnp.where(wrap, side[n, plane, pl.ds(start, rows), :], a)

        parts = [(n, z) for n in range(len(rels)) for z in range(depth)]
        sources, receivers = [], []
        for n, z in parts:
            for t in range(STEPS):
                sources.append(piece(n, t * depth + z, s_at, wrap_s))
                receivers.append(piece(n, (STEPS + t) * depth + z, r_at, wrap_r))
        sources = rotated(sources, to_s)
        receivers = rotated(receivers, to_r)
        terms = []
        for i, (n, z) in enumerate(parts):
            s1, s2 = sources[2 * i:2 * i + 2]
            r1, r2 = receivers[2 * i:2 * i + 2]
            full = s1 * r1 + s2 * r2
            image_buf[n, o, z] = full.astype(jnp.bfloat16)
            y_at = pl.multiple_of(z_of[n] * rows, rows)
            observed = observed_ref[o, z, pl.ds(y_at, rows), :].astype(jnp.float32)
            terms.append((full - observed) * s2)
        terms = rotated(terms, to_s)
        spots = [(n, z, pl.ds(r_at, rows)) for n, z in parts]
        sums = [acc[at] + jnp.where(wrap_r, 0.0, t) for at, t in zip(spots, terms)]
        sides = [acc_side[at] + jnp.where(wrap_r, t, 0.0) for at, t in zip(spots, terms)]
        for at, v, w in zip(spots, sums, sides):
            acc[at] = v
            acc_side[at] = w
        return carry

    lax.fori_loop(0, count, per_offset, 0, unroll=UNROLL)
    for n in range(len(rels)):
        put(n).start()

    if last:
        all_core[...] = jnp.zeros_like(all_core)
        all_side[...] = jnp.zeros_like(all_side)
        window = rows + 2 * HMAX
        for r in range(8):
            at = pl.multiple_of(lax.rem(place_ref[0] + r, 8) * rows, rows)
            if r in rels:
                c, e = acc[rels.index(r)], acc_side[rels.index(r)]
            else:
                c, e = earlier[r][0][...], earlier[r][1][...]
            all_core[:, pl.ds(at, window), :] += c
            all_side[:, pl.ds(at, window), :] += e
        lane8 = lax.broadcasted_iota(jnp.int32, (8, LANES), 1)
        for tile in range(all_rows // half):
            strip = jnp.zeros((8, LANES), jnp.float32)
            at = HMAX + tile * half
            for z in range(depth):
                core_out[tile, z * half:(z + 1) * half, :] = all_core[z, at:at + half, :]
                for k in range(2):
                    q = k * 4 + z
                    part = all_side[z, at + 8 * k:at + 8 * k + 8, :]
                    part = pltpu.roll(part, (8 + 16 * q) % LANES, 1)
                    here = (lane8 >= 16 * q) & (lane8 < 16 * q + 16)
                    strip = jnp.where(here, part, strip)
            side_out[tile] = strip
    for n in range(len(rels)):
        put(n).wait()


def merge_kernel(core_ref, left_ref, right_ref, out_ref):
    lane = lax.broadcasted_iota(jnp.int32, (8, LANES), 1)
    for tile in range(core_ref.shape[0]):
        for q in range(8):
            back = (-(8 + 16 * q)) % LANES
            extra = jnp.where(lane < HMAX, pltpu.roll(left_ref[tile], back, 1), 0.0)
            from_right = pltpu.roll(right_ref[tile], back, 1)
            extra = jnp.where(lane >= LANES - HMAX, from_right, extra)
            at = (q % 4) * 16 + (q // 4) * 8
            out_ref[tile, at:at + 8, :] = core_ref[tile, at:at + 8, :] + extra


def total_kernel(parts_ref, out_ref):
    total = parts_ref[0]
    for i in range(1, parts_ref.shape[0]):
        total = total + parts_ref[i]
    rows = out_ref.shape[1]
    for z in range(out_ref.shape[0]):
        out_ref[z] = total[z * rows:(z + 1) * rows] * (1.0 / OFF_SIDE)


def on_device(src_prev, src_now, rcv_prev, rcv_now, velocity, shift_table, ref_image):
    depth, rows, cols = src_now.shape
    n_off = lax.axis_size("offset")
    n_space = lax.axis_size("space")
    all_rows = ref_image.shape[2]
    shape = jax.ShapeDtypeStruct
    f32 = jnp.float32
    raw = pl.pallas_call(
        stack_kernel, out_shape=shape((5, depth, rows, cols), f32), name="stack"
    )(src_prev, src_now, rcv_prev, rcv_now, velocity)
    forward, backward = chain(n_space)
    low = lax.ppermute(raw, "space", forward)
    high = lax.ppermute(raw, "space", backward)
    edge = shape((5, depth, 8, 2 * LANES), f32)
    wide, upper, lower = pl.pallas_call(
        widen_kernel,
        out_shape=[shape((5, depth, rows, 2 * LANES), f32), edge, edge],
        name="widen", compiler_params=SMALL,
    )(raw, low, high)
    forward_y, backward_y = chain(n_off)
    top = lax.ppermute(lower, "offset", forward_y)
    bottom = lax.ppermute(upper, "offset", backward_y)
    planes = 4 * depth + 2
    tile = pl.pallas_call(
        wave_kernel, out_shape=shape((planes, rows, LANES), f32), name="wave", compiler_params=SMALL
    )(wide, top, bottom)

    me = lax.axis_index("offset")
    other = lax.ppermute(tile, "offset", [(i, i ^ 1) for i in range(n_off)])
    is_low = (me % 2) == 0
    pair = jnp.stack([jnp.where(is_low, tile, other), jnp.where(is_low, other, tile)])

    def turn(d):
        return [(i, (i - 2 * d) % n_off) for i in range(n_off)]

    tiles = [(pair[0], pair[1])] + [None] * 7
    up = down = pair
    for d in range(1, 4):
        up = lax.ppermute(up, "offset", turn(1))
        down = lax.ppermute(down, "offset", turn(-1))
        tiles[d], tiles[8 - d] = (up[0], up[1]), (down[0], down[1])
    tiles[4] = (
        lax.ppermute(up[0], "offset", turn(1)),
        lax.ppermute(down[1], "offset", turn(-1)),
    )

    local = shift_table.shape[0]
    place = (me // 2).astype(jnp.int32)[None]
    whole = pl.BlockSpec(memory_space=pltpu.VMEM)
    scalars = pl.BlockSpec(memory_space=pltpu.SMEM)
    anywhere = pl.BlockSpec(memory_space=pl.ANY)
    window = all_rows // 8 + 2 * HMAX
    image = None
    done = {}
    for rels in ((0,), (1, 7), (2, 6), (3, 5, 4)):
        first, last = image is None, 4 in rels
        n = len(rels)
        chunk = (n, depth, window, LANES)
        args = [place, shift_table, ref_image]
        specs = [scalars, scalars, whole]
        for r in needed(rels):
            args += tiles[r]
            specs += [whole, whole]
        aliases = {}
        if not first:
            aliases = {len(args): 0}
            args.append(image)
            specs.append(anywhere)
        scratch = [
            pltpu.VMEM((n, 4 * depth, window, LANES), f32),
            pltpu.VMEM((n, 4 * depth, window, LANES), f32),
            pltpu.VMEM((n, local, depth, all_rows // 8, LANES), jnp.bfloat16),
            pltpu.SemaphoreType.DMA((n,)),
        ]
        if last:
            for r in range(8):
                if r not in rels:
                    args += done[r]
                    specs += [whole, whole]
            scratch += [pltpu.VMEM(chunk, f32)] * 2
            scratch += [pltpu.VMEM((depth, all_rows + 2 * HMAX, LANES), f32)] * 2
            outs = [shape((n_off, depth * rows, LANES), f32), shape((n_off, 8, LANES), f32)]
        else:
            outs = [shape(chunk, f32)] * 2
        image, core, strip = pl.pallas_call(
            functools.partial(image_kernel, rels, first, last),
            in_specs=specs,
            out_specs=[anywhere, whole, whole],
            out_shape=[shape(ref_image.shape, jnp.bfloat16)] + outs,
            scratch_shapes=scratch,
            input_output_aliases=aliases,
            compiler_params=pltpu.CompilerParams(vmem_limit_bytes=16 * 2**20),
            cost_estimate=pl.CostEstimate(
                flops=n * 10_000_000, bytes_accessed=n * 4_000_000, transcendentals=0
            ),
            name="image",
        )(*args)
        if not last:
            for i, r in enumerate(rels):
                done[r] = (core[i], strip[i])

    left = lax.ppermute(strip, "space", forward)
    right = lax.ppermute(strip, "space", backward)
    parts = pl.pallas_call(
        merge_kernel, out_shape=shape(core.shape, f32), name="merge", compiler_params=SMALL
    )(core, left, right)
    parts = lax.all_to_all(parts, "offset", 0, 0)
    adjoint = pl.pallas_call(
        total_kernel, out_shape=shape((depth, rows, cols), f32), name="total", compiler_params=SMALL
    )(parts)
    return image, adjoint


def solution(mesh):
    field = P(None, "offset", "space")
    in_specs = (field,) * 5 + (P("offset", None), P("offset", None, None, "space"))
    out_specs = (P("offset", None, None, "space"), field)
    return jax.shard_map(
        on_device, mesh=mesh, in_specs=in_specs, out_specs=out_specs, check_vma=False
    )
```

time: 160 us -> 117 us (0.73)
  Pallas kernels: 54 us -> 26.6 us
  waiting for transfers between devices: 38.4 us -> 30.7 us
  starting transfers between devices: 37.3 us -> 32.5 us
  other arithmetic: 2.08 us -> 0.04 us
    pallas_call x4 -> x9, Pallas kernels: 54 us -> 26.6 us  [the longest x4 23.7 us: on_device(): pl.pallas_call(functools.partial(image_kernel, rels, first, last), in_spe...]
    ppermute x3, waiting for transfers between devices: 18.5 us -> 6.91 us  [on_device(): down = lax.ppermute(down, 'offset', turn(-1))]
    ppermute x6, waiting for transfers between devices: 11.4 us -> 15.1 us  [the longest x1 6.12 us: on_device(): low = lax.ppermute(raw, 'space', forward)]
    ppermute x6, starting transfers between devices: 15.6 us -> 13.3 us  [the longest x1 4.24 us: on_device(): high = lax.ppermute(raw, 'space', backward)]
    unnamed x11 -> x5, local copies, waits for them, and re-layouts: 3.73 us -> 3.85 us
  transfers between devices with their start and end apart: 15 -> 15, of which waited for: 9 -> 8; matrix products, arithmetic and copies ran while one was open for 0% -> 1% of each run, Pallas kernels for 0% -> 14%
where the time goes in v2:
time: 117 us; the launch traced here: 115 us
  starting transfers between devices  32.5 us (28%)
  waiting for transfers between devices  30.7 us (26%)
  Pallas kernels  26.6 us (23%)
  blocking collectives  20.4 us (17%)
  local copies, waits for them, and re-layouts  4.04 us (3%)
    pallas_call x4, Pallas kernels, on_device(): pl.pallas_call(functools.partial(image_kernel, rels, first, last), in_spe...  23.7 us
    all_to_all x1, blocking collectives, on_device(): parts = lax.all_to_all(parts, 'offset', 0, 0)  20.4 us
    ppermute x3, starting transfers between devices, on_device(): up = lax.ppermute(up, 'offset', turn(1))  10.8 us
    ppermute x3, waiting for transfers between devices, on_device(): down = lax.ppermute(down, 'offset', turn(-1))  6.91 us
    ppermute x1, waiting for transfers between devices, on_device(): low = lax.ppermute(raw, 'space', forward)  6.12 us
    ppermute x1, waiting for transfers between devices, on_device(): left = lax.ppermute(strip, 'space', forward)  5.56 us
    ppermute x1, waiting for transfers between devices, on_device(): bottom = lax.ppermute(upper, 'offset', backward_y)  4.47 us
    ppermute x1, starting transfers between devices, on_device(): high = lax.ppermute(raw, 'space', backward)  4.24 us
  transfers between devices with their start and end apart: 15, of which 8 were waited for; matrix products, arithmetic and copies ran while one was open for 1% of the time, Pallas kernels for 14%

profile of v2, /device:TPU:16, one launch (start us, length us, event | category | flops | bytes accessed | tf_op | source)
XLA Modules:
  0.0 115.2 jit_solution(8163702553343292153)
XLA Ops:
  0.6 1.5 %stack.13.raw_ref = f32[5,4,16,128]{3,2,1,0:T(8,128)} custom-call(f32[4,16,128]{2,1,0:T(8,128)} %refs_0_.1, f32[4,16,128]{2,1,0:T(8,128)} %refs_1_.5, f32[4,16,128]{2,1,0:T(8,128)} %refs_2_.5, f32[4,16,128]{2,1,0:T(8,128)} %refs_3_.1, f32[4,16,128]{2,1,0:T(8,128)} %refs_4_.1), custom_call_target="tpu_custom_call" | custom-call | tf_op jit(solution)/shard_map/stack/pallas_call | solution.py:258
  2.1 4.2 %collective-permute-start.1 = (f32[5,4,16,128]{3,2,1,0:T(8,128)}, f32[5,4,16,128]{3,2,1,0:T(8,128)S(1)}, u32[]{:S(2)}, u32[]{:S(2)}) collective-permute-start(f32[5,4,16,128]{3,2,1,0:T(8,128)} %stack.13.raw_ref), channel_id=1, source_target_pairs={{16,0},{32,16},{48,32},{64,48},{80,64},{96,80},{112,96},{128,112},... | collective-permute-start | bytes 491528 | tf_op jit(solution)/shard_map/ppermute | solution.py:263
  6.4 1.9 %collective-permute-start = (f32[5,4,16,128]{3,2,1,0:T(8,128)}, f32[5,4,16,128]{3,2,1,0:T(8,128)S(1)}, u32[]{:S(2)}, u32[]{:S(2)}) collective-permute-start(f32[5,4,16,128]{3,2,1,0:T(8,128)} %stack.13.raw_ref), channel_id=1, source_target_pairs={{0,16},{16,32},{32,48},{48,64},{64,80},{80,96},{96,112},{112,128},... | collective-permute-start | bytes 491528 | tf_op jit(solution)/shard_map/ppermute | solution.py:262
  8.3 1.2 %collective-permute-done.1.high_ref = f32[5,4,16,128]{3,2,1,0:T(8,128)S(1)} collective-permute-done((f32[5,4,16,128]{3,2,1,0:T(8,128)}, f32[5,4,16,128]{3,2,1,0:T(8,128)S(1)}, u32[]{:S(2)}, u32[]{:S(2)}) %collective-permute-start.1) | collective-permute-done | bytes 163872 | tf_op jit(solution)/shard_map/ppermute | solution.py:263
  9.5 6.1 %collective-permute-done.low_ref = f32[5,4,16,128]{3,2,1,0:T(8,128)S(1)} collective-permute-done((f32[5,4,16,128]{3,2,1,0:T(8,128)}, f32[5,4,16,128]{3,2,1,0:T(8,128)S(1)}, u32[]{:S(2)}, u32[]{:S(2)}) %collective-permute-start) | collective-permute-done | bytes 163872 | tf_op jit(solution)/shard_map/ppermute | solution.py:262
  15.6 0.9 copy-done.1
  16.6 2.5 %collective-permute-start.2 = (f32[5,4,8,256]{3,2,1,0:T(8,128)S(1)}, f32[5,4,8,256]{3,2,1,0:T(8,128)S(1)}, u32[]{:S(2)}, u32[]{:S(2)}) collective-permute-start(f32[5,4,8,256]{3,2,1,0:T(8,128)S(1)} %get-tuple-element.18), channel_id=1, source_target_pairs={{0,1},{1,2},{2,3},{3,4},{4,5},{5,6},{6,7},{7,8},{8,9},{9,10},{10,1... | collective-permute-start | bytes 491528 | tf_op jit(solution)/shard_map/ppermute | solution.py:271
  19.1 1.3 %collective-permute-start.3 = (f32[5,4,8,256]{3,2,1,0:T(8,128)S(1)}, f32[5,4,8,256]{3,2,1,0:T(8,128)S(1)}, u32[]{:S(2)}, u32[]{:S(2)}) collective-permute-start(f32[5,4,8,256]{3,2,1,0:T(8,128)S(1)} %get-tuple-element.19), channel_id=1, source_target_pairs={{1,0},{2,1},{3,2},{4,3},{5,4},{6,5},{7,6},{8,7},{9,8},{10,9},{11,1... | collective-permute-start | bytes 491528 | tf_op jit(solution)/shard_map/ppermute | solution.py:272
  20.4 3.3 %collective-permute-done.2.top_ref = f32[5,4,8,256]{3,2,1,0:T(8,128)S(1)} collective-permute-done((f32[5,4,8,256]{3,2,1,0:T(8,128)S(1)}, f32[5,4,8,256]{3,2,1,0:T(8,128)S(1)}, u32[]{:S(2)}, u32[]{:S(2)}) %collective-permute-start.2) | collective-permute-done | bytes 163872 | tf_op jit(solution)/shard_map/ppermute | solution.py:271
  23.7 4.5 %collective-permute-done.3.bottom_ref = f32[5,4,8,256]{3,2,1,0:T(8,128)S(1)} collective-permute-done((f32[5,4,8,256]{3,2,1,0:T(8,128)S(1)}, f32[5,4,8,256]{3,2,1,0:T(8,128)S(1)}, u32[]{:S(2)}, u32[]{:S(2)}) %collective-permute-start.3) | collective-permute-done | bytes 163872 | tf_op jit(solution)/shard_map/ppermute | solution.py:272
  28.2 0.4 wave.1
  28.6 2.0 %collective-permute-start.4 = (f32[18,16,128]{2,1,0:T(8,128)S(1)}, f32[18,16,128]{2,1,0:T(8,128)S(1)}, u32[]{:S(2)}, u32[]{:S(2)}) collective-permute-start(f32[18,16,128]{2,1,0:T(8,128)S(1)} %wave.1), channel_id=1, source_target_pairs={{0,1},{1,0},{2,3},{3,2},{4,5},{5,4},{6,7},{7,6},{8,9},{9,8},{10,11... | collective-permute-start | bytes 442376 | tf_op jit(solution)/shard_map/ppermute | solution.py:279
  30.6 3.2 %collective-permute-done.4 = f32[18,16,128]{2,1,0:T(8,128)S(1)} collective-permute-done((f32[18,16,128]{2,1,0:T(8,128)S(1)}, f32[18,16,128]{2,1,0:T(8,128)S(1)}, u32[]{:S(2)}, u32[]{:S(2)}) %collective-permute-start.4) | collective-permute-done | bytes 147488 | tf_op jit(solution)/shard_map/ppermute | solution.py:279
  33.9 2.0 %collective-permute-start.9 = (f32[2,18,16,128]{3,2,1,0:T(8,128)S(1)}, f32[2,18,16,128]{3,2,1,0:T(8,128)S(1)}, u32[]{:S(2)}, u32[]{:S(2)}) collective-permute-start(f32[2,18,16,128]{3,2,1,0:T(8,128)S(1)} %pad_maximum_fusion), channel_id=1, source_target_pairs={{0,2},{1,3},{2,4},{3,5},{4,6},{5,7},{6,8},{7,9},{8,10},{9,11},{10,... | collective-permute-start | bytes 884744 | tf_op jit(solution)/shard_map/ppermute | solution.py:290
  35.9 3.9 %collective-permute-start.5 = (f32[2,18,16,128]{3,2,1,0:T(8,128)S(1)}, f32[2,18,16,128]{3,2,1,0:T(8,128)S(1)}, u32[]{:S(2)}, u32[]{:S(2)}) collective-permute-start(f32[2,18,16,128]{3,2,1,0:T(8,128)S(1)} %pad_maximum_fusion), channel_id=1, source_target_pairs={{0,14},{1,15},{2,0},{3,1},{4,2},{5,3},{6,4},{7,5},{8,6},{9,7},{10,... | collective-permute-start | bytes 884744 | tf_op jit(solution)/shard_map/ppermute | solution.py:289
  39.8 0.8 copy.15.refs_1_
  40.5 6.6 %collective-permute-done.9 = f32[2,18,16,128]{3,2,1,0:T(8,128)S(1)} collective-permute-done((f32[2,18,16,128]{3,2,1,0:T(8,128)S(1)}, f32[2,18,16,128]{3,2,1,0:T(8,128)S(1)}, u32[]{:S(2)}, u32[]{:S(2)}) %collective-permute-start.9) | collective-permute-done | bytes 294944 | tf_op jit(solution)/shard_map/ppermute | solution.py:290
  47.1 3.5 %collective-permute-start.6 = (f32[2,18,16,128]{3,2,1,0:T(8,128)S(1)}, f32[2,18,16,128]{3,2,1,0:T(8,128)S(1)}, u32[]{:S(2)}, u32[]{:S(2)}) collective-permute-start(f32[2,18,16,128]{3,2,1,0:T(8,128)S(1)} %collective-permute-done.5), channel_id=1, source_target_pairs={{0,14},{1,15},{2,0},{3,1},{4,2},{5,3},{6,4},{7,5},{8,6},{9,7},{10,... | collective-permute-start | bytes 884744 | tf_op jit(solution)/shard_map/ppermute | solution.py:289
  50.6 2.2 %copy-done = bf16[16,4,256,128]{3,2,1,0:T(8,128)(2,1)S(1)} copy-done((bf16[16,4,256,128]{3,2,1,0:T(8,128)(2,1)S(1)}, bf16[16,4,256,128]{3,2,1,0:T(8,128)(2,1)}, u32[]{:S(2)}) %copy-start) | copy-done | bytes 4194328
  52.8 4.4 %image.4 = (bf16[16,4,256,128]{3,2,1,0:T(8,128)(2,1)}, f32[1,4,48,128]{3,2,1,0:T(8,128)S(1)}, f32[1,4,48,128]{3,2,1,0:T(8,128)S(1)}) custom-call(s32[1]{0:T(128)} %bitcast.refs_0_, s32[16,2]{1,0:T(8,128)S(1)} %copy.15.refs_1_, bf16[16,4,256,128]{3,2,1,0:T(8,128)(2,1)S(1)} %copy-done, f32[18,16,128]{2,1,0:T(8,128)S(1)} %get-tuple-element.44.refs_3_, ...), custom_call_target="tpu_custom_call" | custom-call | flops 10000000 | bytes 4000000 | tf_op jit(solution)/shard_map/image/pallas_call | solution.py:335
  57.2 0.3 collective-permute-done.10
  57.6 3.4 %collective-permute-start.7 = (f32[2,18,16,128]{3,2,1,0:T(8,128)S(1)}, f32[2,18,16,128]{3,2,1,0:T(8,128)S(1)}, u32[]{:S(2)}, u32[]{:S(2)}) collective-permute-start(f32[2,18,16,128]{3,2,1,0:T(8,128)S(1)} %collective-permute-done.6), channel_id=1, source_target_pairs={{0,14},{1,15},{2,0},{3,1},{4,2},{5,3},{6,4},{7,5},{8,6},{9,7},{10,... | collective-permute-start | bytes 884744 | tf_op jit(solution)/shard_map/ppermute | solution.py:289
  61.0 5.8 %image.5 = (bf16[16,4,256,128]{3,2,1,0:T(8,128)(2,1)}, f32[2,4,48,128]{3,2,1,0:T(8,128)S(1)}, f32[2,4,48,128]{3,2,1,0:T(8,128)S(1)}) custom-call(s32[1]{0:T(128)} %bitcast.refs_0_, s32[16,2]{1,0:T(8,128)S(1)} %copy.15.refs_1_, bf16[16,4,256,128]{3,2,1,0:T(8,128)(2,1)S(1)} %copy-done, ...), custom_call_target="tpu_custom_call", output_to_operand_aliasing={{0}: (13, {})} | custom-call | flops 20000000 | bytes 8000000 | tf_op jit(solution)/shard_map/image/pallas_call | solution.py:335
  67.1 3.3 %collective-permute-start.8 = (f32[18,16,128]{2,1,0:T(8,128)S(1)}, f32[18,16,128]{2,1,0:T(8,128)S(1)}, u32[]{:S(2)}, u32[]{:S(2)}) collective-permute-start(f32[18,16,128]{2,1,0:T(8,128)S(1)} %get-tuple-element.41.refs_7_.refs_5_), channel_id=1, source_target_pairs={{0,14},{1,15},{2,0},{3,1},{4,2},{5,3},{6,4},{7,5},{8,6},{9,7},{10,... | collective-permute-start | bytes 442376 | tf_op jit(solution)/shard_map/ppermute | solution.py:293
  70.4 5.8 %image.6 = (bf16[16,4,256,128]{3,2,1,0:T(8,128)(2,1)}, f32[2,4,48,128]{3,2,1,0:T(8,128)S(1)}, f32[2,4,48,128]{3,2,1,0:T(8,128)S(1)}) custom-call(s32[1]{0:T(128)} %bitcast.refs_0_, s32[16,2]{1,0:T(8,128)S(1)} %copy.15.refs_1_, bf16[16,4,256,128]{3,2,1,0:T(8,128)(2,1)S(1)} %copy-done, ...), custom_call_target="tpu_custom_call", output_to_operand_aliasing={{0}: (15, {})} | custom-call | flops 20000000 | bytes 8000000 | tf_op jit(solution)/shard_map/image/pallas_call | solution.py:335
  76.2 7.7 %image.7 = (bf16[16,4,256,128]{3,2,1,0:T(8,128)(2,1)}, f32[16,64,128]{2,1,0:T(8,128)S(1)}, f32[16,8,128]{2,1,0:T(8,128)S(1)}) custom-call(s32[1]{0:T(128)} %bitcast.refs_0_, s32[16,2]{1,0:T(8,128)S(1)} %copy.15.refs_1_, bf16[16,4,256,128]{3,2,1,0:T(8,128)(2,1)S(1)} %copy-done, ...), custom_call_target="tpu_custom_call", output_to_operand_aliasing={{0}: (13, {})} | custom-call | flops 30000000 | bytes 12000000 | tf_op jit(solution)/shard_map/image/pallas_call | solution.py:335
  83.9 1.9 %collective-permute-start.14 = (f32[16,8,128]{2,1,0:T(8,128)S(1)}, f32[16,8,128]{2,1,0:T(8,128)S(1)}, u32[]{:S(2)}, u32[]{:S(2)}) collective-permute-start(f32[16,8,128]{2,1,0:T(8,128)S(1)} %get-tuple-element.31), channel_id=1, source_target_pairs={{16,0},{32,16},{48,32},{64,48},{80,64},{96,80},{112,96},{128,112},... | collective-permute-start | bytes 196616 | tf_op jit(solution)/shard_map/ppermute | solution.py:353
  85.8 2.4 %collective-permute-start.13 = (f32[16,8,128]{2,1,0:T(8,128)S(1)}, f32[16,8,128]{2,1,0:T(8,128)S(1)}, u32[]{:S(2)}, u32[]{:S(2)}) collective-permute-start(f32[16,8,128]{2,1,0:T(8,128)S(1)} %get-tuple-element.31), channel_id=1, source_target_pairs={{0,16},{16,32},{32,48},{48,64},{64,80},{80,96},{96,112},{112,128},... | collective-permute-start | bytes 196616 | tf_op jit(solution)/shard_map/ppermute | solution.py:352
  88.2 5.6 %collective-permute-done.13.left_ref = f32[16,8,128]{2,1,0:T(8,128)S(1)} collective-permute-done((f32[16,8,128]{2,1,0:T(8,128)S(1)}, f32[16,8,128]{2,1,0:T(8,128)S(1)}, u32[]{:S(2)}, u32[]{:S(2)}) %collective-permute-start.13) | collective-permute-done | bytes 65568 | tf_op jit(solution)/shard_map/ppermute | solution.py:352
  93.8 0.3 merge.1
  94.1 20.4 %all_to_all.5.parts_ref = f32[16,64,128]{2,1,0:T(8,128)S(1)} all-to-all(f32[16,64,128]{2,1,0:T(8,128)S(1)} %merge.1), channel_id=1, replica_groups=mesh['space'=16,'offset'=16] {'offset'}, dimensions={0} | all-to-all | bytes 1048576 | tf_op jit(solution)/shard_map/all_to_all | solution.py:357
  114.5 0.6 total.1
  (23 shorter events, 0.4 us)
Async XLA Ops:
  2.1 7.4 %collective-permute-start.1 = (f32[5,4,16,128]{3,2,1,0:T(8,128)}, f32[5,4,16,128]{3,2,1,0:T(8,128)S(1)}, u32[]{:S(2)}, u32[]{:S(2)}) collective-permute-start(f32[5,4,16,128]{3,2,1,0:T(8,128)} %stack.13.raw_ref), channel_id=1, source_target_pairs={{16,0},{32,16},{48,32},{64,48},{80,64},{96,80},{112,96},{128,112},... | collective-permute-start | bytes 491528 | tf_op jit(solution)/shard_map/ppermute | solution.py:263
  6.4 9.3 %collective-permute-start = (f32[5,4,16,128]{3,2,1,0:T(8,128)}, f32[5,4,16,128]{3,2,1,0:T(8,128)S(1)}, u32[]{:S(2)}, u32[]{:S(2)}) collective-permute-start(f32[5,4,16,128]{3,2,1,0:T(8,128)} %stack.13.raw_ref), channel_id=1, source_target_pairs={{0,16},{16,32},{32,48},{48,64},{64,80},{80,96},{96,112},{112,128},... | collective-permute-start | bytes 491528 | tf_op jit(solution)/shard_map/ppermute | solution.py:262
  15.6 0.9 copy-start.1
  16.6 7.1 %collective-permute-start.2 = (f32[5,4,8,256]{3,2,1,0:T(8,128)S(1)}, f32[5,4,8,256]{3,2,1,0:T(8,128)S(1)}, u32[]{:S(2)}, u32[]{:S(2)}) collective-permute-start(f32[5,4,8,256]{3,2,1,0:T(8,128)S(1)} %get-tuple-element.18), channel_id=1, source_target_pairs={{0,1},{1,2},{2,3},{3,4},{4,5},{5,6},{6,7},{7,8},{8,9},{9,10},{10,1... | collective-permute-start | bytes 491528 | tf_op jit(solution)/shard_map/ppermute | solution.py:271
  19.1 9.0 %collective-permute-start.3 = (f32[5,4,8,256]{3,2,1,0:T(8,128)S(1)}, f32[5,4,8,256]{3,2,1,0:T(8,128)S(1)}, u32[]{:S(2)}, u32[]{:S(2)}) collective-permute-start(f32[5,4,8,256]{3,2,1,0:T(8,128)S(1)} %get-tuple-element.19), channel_id=1, source_target_pairs={{1,0},{2,1},{3,2},{4,3},{5,4},{6,5},{7,6},{8,7},{9,8},{10,9},{11,1... | collective-permute-start | bytes 491528 | tf_op jit(solution)/shard_map/ppermute | solution.py:272
  28.6 5.2 %collective-permute-start.4 = (f32[18,16,128]{2,1,0:T(8,128)S(1)}, f32[18,16,128]{2,1,0:T(8,128)S(1)}, u32[]{:S(2)}, u32[]{:S(2)}) collective-permute-start(f32[18,16,128]{2,1,0:T(8,128)S(1)} %wave.1), channel_id=1, source_target_pairs={{0,1},{1,0},{2,3},{3,2},{4,5},{5,4},{6,7},{7,6},{8,9},{9,8},{10,11... | collective-permute-start | bytes 442376 | tf_op jit(solution)/shard_map/ppermute | solution.py:279
  33.9 13.2 %collective-permute-start.9 = (f32[2,18,16,128]{3,2,1,0:T(8,128)S(1)}, f32[2,18,16,128]{3,2,1,0:T(8,128)S(1)}, u32[]{:S(2)}, u32[]{:S(2)}) collective-permute-start(f32[2,18,16,128]{3,2,1,0:T(8,128)S(1)} %pad_maximum_fusion), channel_id=1, source_target_pairs={{0,2},{1,3},{2,4},{3,5},{4,6},{5,7},{6,8},{7,9},{8,10},{9,11},{10,... | collective-permute-start | bytes 884744 | tf_op jit(solution)/shard_map/ppermute | solution.py:290
  35.9 11.3 %collective-permute-start.5 = (f32[2,18,16,128]{3,2,1,0:T(8,128)S(1)}, f32[2,18,16,128]{3,2,1,0:T(8,128)S(1)}, u32[]{:S(2)}, u32[]{:S(2)}) collective-permute-start(f32[2,18,16,128]{3,2,1,0:T(8,128)S(1)} %pad_maximum_fusion), channel_id=1, source_target_pairs={{0,14},{1,15},{2,0},{3,1},{4,2},{5,3},{6,4},{7,5},{8,6},{9,7},{10,... | collective-permute-start | bytes 884744 | tf_op jit(solution)/shard_map/ppermute | solution.py:289
  47.1 10.5 %collective-permute-start.10 = (f32[2,18,16,128]{3,2,1,0:T(8,128)S(1)}, f32[2,18,16,128]{3,2,1,0:T(8,128)S(1)}, u32[]{:S(2)}, u32[]{:S(2)}) collective-permute-start(f32[2,18,16,128]{3,2,1,0:T(8,128)S(1)} %collective-permute-done.9), channel_id=1, source_target_pairs={{0,2},{1,3},{2,4},{3,5},{4,6},{5,7},{6,8},{7,9},{8,10},{9,11},{10,... | collective-permute-start | bytes 884744 | tf_op jit(solution)/shard_map/ppermute | solution.py:290
  47.1 10.5 %collective-permute-start.6 = (f32[2,18,16,128]{3,2,1,0:T(8,128)S(1)}, f32[2,18,16,128]{3,2,1,0:T(8,128)S(1)}, u32[]{:S(2)}, u32[]{:S(2)}) collective-permute-start(f32[2,18,16,128]{3,2,1,0:T(8,128)S(1)} %collective-permute-done.5), channel_id=1, source_target_pairs={{0,14},{1,15},{2,0},{3,1},{4,2},{5,3},{6,4},{7,5},{8,6},{9,7},{10,... | collective-permute-start | bytes 884744 | tf_op jit(solution)/shard_map/ppermute | solution.py:289
  50.6 2.2 %copy-start = (bf16[16,4,256,128]{3,2,1,0:T(8,128)(2,1)S(1)}, bf16[16,4,256,128]{3,2,1,0:T(8,128)(2,1)}, u32[]{:S(2)}) copy-start(bf16[16,4,256,128]{3,2,1,0:T(8,128)(2,1)} %refs_2_.9) | copy-start | bytes 12582916
  57.6 9.3 %collective-permute-start.11 = (f32[2,18,16,128]{3,2,1,0:T(8,128)S(1)}, f32[2,18,16,128]{3,2,1,0:T(8,128)S(1)}, u32[]{:S(2)}, u32[]{:S(2)}) collective-permute-start(f32[2,18,16,128]{3,2,1,0:T(8,128)S(1)} %collective-permute-done.10), channel_id=1, source_target_pairs={{0,2},{1,3},{2,4},{3,5},{4,6},{5,7},{6,8},{7,9},{8,10},{9,11},{10,... | collective-permute-start | bytes 884744 | tf_op jit(solution)/shard_map/ppermute | solution.py:290
  57.6 9.4 %collective-permute-start.7 = (f32[2,18,16,128]{3,2,1,0:T(8,128)S(1)}, f32[2,18,16,128]{3,2,1,0:T(8,128)S(1)}, u32[]{:S(2)}, u32[]{:S(2)}) collective-permute-start(f32[2,18,16,128]{3,2,1,0:T(8,128)S(1)} %collective-permute-done.6), channel_id=1, source_target_pairs={{0,14},{1,15},{2,0},{3,1},{4,2},{5,3},{6,4},{7,5},{8,6},{9,7},{10,... | collective-permute-start | bytes 884744 | tf_op jit(solution)/shard_map/ppermute | solution.py:289
  66.9 9.3 %collective-permute-start.12 = (f32[18,16,128]{2,1,0:T(8,128)S(1)}, f32[18,16,128]{2,1,0:T(8,128)S(1)}, u32[]{:S(2)}, u32[]{:S(2)}) collective-permute-start(f32[18,16,128]{2,1,0:T(8,128)S(1)} %get-tuple-element.39.refs_10_), channel_id=1, source_target_pairs={{0,2},{1,3},{2,4},{3,5},{4,6},{5,7},{6,8},{7,9},{8,10},{9,11},{10,... | collective-permute-start | bytes 442376 | tf_op jit(solution)/shard_map/ppermute | solution.py:294
  67.1 9.1 %collective-permute-start.8 = (f32[18,16,128]{2,1,0:T(8,128)S(1)}, f32[18,16,128]{2,1,0:T(8,128)S(1)}, u32[]{:S(2)}, u32[]{:S(2)}) collective-permute-start(f32[18,16,128]{2,1,0:T(8,128)S(1)} %get-tuple-element.41.refs_7_.refs_5_), channel_id=1, source_target_pairs={{0,14},{1,15},{2,0},{3,1},{4,2},{5,3},{6,4},{7,5},{8,6},{9,7},{10,... | collective-permute-start | bytes 442376 | tf_op jit(solution)/shard_map/ppermute | solution.py:293
  83.9 4.3 %collective-permute-start.14 = (f32[16,8,128]{2,1,0:T(8,128)S(1)}, f32[16,8,128]{2,1,0:T(8,128)S(1)}, u32[]{:S(2)}, u32[]{:S(2)}) collective-permute-start(f32[16,8,128]{2,1,0:T(8,128)S(1)} %get-tuple-element.31), channel_id=1, source_target_pairs={{16,0},{32,16},{48,32},{64,48},{80,64},{96,80},{112,96},{128,112},... | collective-permute-start | bytes 196616 | tf_op jit(solution)/shard_map/ppermute | solution.py:353
  85.8 8.0 %collective-permute-start.13 = (f32[16,8,128]{2,1,0:T(8,128)S(1)}, f32[16,8,128]{2,1,0:T(8,128)S(1)}, u32[]{:S(2)}, u32[]{:S(2)}) collective-permute-start(f32[16,8,128]{2,1,0:T(8,128)S(1)} %get-tuple-element.31), channel_id=1, source_target_pairs={{0,16},{16,32},{32,48},{48,64},{64,80},{80,96},{96,112},{112,128},... | collective-permute-start | bytes 196616 | tf_op jit(solution)/shard_map/ppermute | solution.py:352

commit v3 on v2

v3 whole, which is shorter than its diff:
```python
import functools

import jax
import jax.numpy as jnp
from jax import lax
from jax.experimental import pallas as pl
from jax.experimental.pallas import tpu as pltpu
from jax.sharding import PartitionSpec as P

OFF_SIDE = 16
HMAX = 8
STEPS = 2
REACH = HMAX + STEPS
LANES = 128
UNROLL = 2
SMALL = pltpu.CompilerParams(vmem_limit_bytes=6 * 2**20)

CALLS = (
    ((7, 16, 16), (0, 0, 32), (1, 0, 16)),
    ((1, 16, 16), (2, 0, 16), (6, 16, 16), (7, 0, 16)),
    ((2, 16, 16), (3, 0, 16), (5, 16, 16), (6, 0, 16)),
    ((3, 16, 16), (4, 0, 32), (5, 0, 16)),
)


def swaps(count):
    inner = [(i, i ^ 1) for i in range(count)]
    outer = [(i, i + 1 if i % 2 else i - 1) for i in range(1, count - 1)]
    return inner, outer


def roll_lanes(x, shift):
    return pltpu.roll(x, shift % LANES, x.ndim - 1)


def edges_kernel(*refs):
    fields, raw_ref, edge_ref = refs[:-2], refs[-2], refs[-1]
    depth, rows, cols = fields[0].shape
    total = len(fields) * rows
    lane = lax.broadcasted_iota(jnp.int32, (total, LANES), 1)
    packed = jnp.zeros((total, LANES), jnp.float32)
    for z in range(depth):
        plane = jnp.concatenate([ref[z] for ref in fields], axis=0)
        for f in range(len(fields)):
            raw_ref[f, z] = plane[f * rows:(f + 1) * rows]
        first = roll_lanes(plane, 32 * z)
        last = roll_lanes(plane, 32 * z + 32)
        packed = jnp.where((lane >= 32 * z) & (lane < 32 * z + 16), first, packed)
        packed = jnp.where((lane >= 32 * z + 16) & (lane < 32 * z + 32), last, packed)
    for f in range(len(fields)):
        edge_ref[f] = packed[f * rows:(f + 1) * rows]


def touch_kernel(ref, out_ref):
    out_ref[...] = ref[0, 0, :8, :].astype(jnp.float32)


def widen_kernel(where_ref, shifts_ref, raw_ref, inner_ref, outer_ref, wide_ref, send_in_ref, send_out_ref):
    fields, depth, rows, cols = raw_ref.shape
    total = fields * rows
    lane = lax.broadcasted_iota(jnp.int32, (total, LANES), 1)
    row = lax.broadcasted_iota(jnp.int32, (8, 2 * LANES), 0)
    even_x = where_ref[1] == 0
    even_y = where_ref[2] == 0
    inner = jnp.concatenate([inner_ref[f] for f in range(fields)], axis=0)
    outer = jnp.concatenate([outer_ref[f] for f in range(fields)], axis=0)
    left = jnp.where(even_x, outer, inner)
    right = jnp.where(even_x, inner, outer)
    upper = [jnp.zeros((8, 2 * LANES), jnp.float32) for _ in range(fields)]
    lower = list(upper)
    for z in range(depth):
        beside = jnp.where(lane >= cols - REACH, roll_lanes(left, 96 - 32 * z), 0.0)
        beside = jnp.where(lane < REACH, roll_lanes(right, -32 * z), beside)
        here = (row >= 2 * z) & (row < 2 * z + 2)
        for f in range(fields):
            both = jnp.concatenate([raw_ref[f, z], beside[f * rows:(f + 1) * rows]], axis=1)
            wide_ref[f, z] = both
            upper[f] = jnp.where(here, pltpu.roll(both[:8], 2 * z, 0), upper[f])
            lower[f] = jnp.where(here, pltpu.roll(both[rows - 8:], (2 * z + 2) % 8, 0), lower[f])
    for f in range(fields):
        send_in_ref[f] = jnp.where(even_y, lower[f], upper[f])
        send_out_ref[f] = jnp.where(even_y, upper[f], lower[f])


def wave_kernel(where_ref, wide_ref, inner_ref, outer_ref, tile_ref):
    depth, rows, width = wide_ref.shape[1:]
    high_rows = rows + 8
    lane = lax.broadcasted_iota(jnp.int32, (rows, LANES), 1)
    edge_row = lax.broadcasted_iota(jnp.int32, (8, width), 0)
    even_y = where_ref[2] == 0
    top = [jnp.where(even_y, outer_ref[f], inner_ref[f]) for f in range(5)]
    bottom = [jnp.where(even_y, inner_ref[f], outer_ref[f]) for f in range(5)]

    def whole(f, z):
        edge = jnp.where(edge_row >= 6, pltpu.roll(top[f], (6 - 2 * z) % 8, 0), 0.0)
        edge = jnp.where(edge_row < 2, pltpu.roll(bottom[f], (8 - 2 * z) % 8, 0), edge)
        return jnp.concatenate([wide_ref[f, z], edge], axis=0)

    speed = [whole(4, z) for z in range(depth)]

    def advance(prev, now):
        out = []
        for z in range(depth):
            c = now[z]
            beside = pltpu.roll(c, 1, 0) + pltpu.roll(c, high_rows - 1, 0)
            beside = beside + pltpu.roll(c, 1, 1) + pltpu.roll(c, width - 1, 1)
            if z > 0:
                beside = beside + now[z - 1]
            if z < depth - 1:
                beside = beside + now[z + 1]
            out.append(2.0 * c - prev[z] + speed[z] * (beside - 6.0 * c))
        return out

    packed = [jnp.zeros((rows, LANES), jnp.float32) for _ in range(2)]
    for pair in range(2):
        prev = [whole(2 * pair, z) for z in range(depth)]
        now = [whole(2 * pair + 1, z) for z in range(depth)]
        for t in range(STEPS):
            prev, now = now, advance(prev, now)
            for z in range(depth):
                plane = (pair * STEPS + t) * depth + z
                tile_ref[plane] = now[z][:rows, :LANES]
                q = plane % 8
                beside = roll_lanes(now[z][:rows, LANES:], (8 + 16 * q) % LANES)
                here = (lane >= 16 * q) & (lane < 16 * q + 16)
                packed[plane // 8] = jnp.where(here, beside, packed[plane // 8])
    for k in range(2):
        tile_ref[4 * depth + k] = packed[k]


def needed(call):
    return sorted({r for r, _, _ in call} | {(r + k) % 8 for r, a, m in call for k in (-1, 1)
                   if (k < 0 and a == 0) or (k > 0 and a + m == 32)})


def image_kernel(call, first, last, *refs):
    refs = list(refs)
    where_ref, shifts_ref, observed_ref = refs[:3]
    del refs[:4 if first else 3]
    tiles = {}
    for r in needed(call):
        tiles[r], refs = refs[:2], refs[2:]
    if not first:
        refs = refs[1:]
    segments = list(call)
    earlier = []
    if last:
        for other in CALLS:
            if other != call:
                for segment in other:
                    earlier.append((segment, refs[0], refs[1]))
                    refs = refs[2:]
    n_seg = len(segments)
    image_hbm, refs = refs[0], refs[1:]
    if last:
        core_out, send_in, send_out = refs[:3]
        refs = refs[3:]
    sums = []
    for _ in segments:
        sums.append(refs[:2])
        refs = refs[2:]
    mains, sides, images = refs[:n_seg], refs[n_seg:2 * n_seg], refs[2 * n_seg:3 * n_seg]
    sems = refs[3 * n_seg]
    count, depth, all_rows = observed_ref.shape[:3]
    planes = 4 * depth
    rows = all_rows // 8
    half = rows // 2

    def z_of(r):
        return lax.rem(where_ref[0] + r, 8)

    def put(n, part):
        r, a, m = segments[n]
        at = pl.multiple_of(z_of(r) * rows + a, half)
        which = pl.ds(part * (count // 2), count // 2)
        return pltpu.make_async_copy(
            images[n].at[which], image_hbm.at[which, :, pl.ds(at, m), :], sems.at[n, part]
        )

    packs, homes = [], []
    for n, (r, a, m) in enumerate(segments):
        for ref in sums[n]:
            ref[...] = jnp.zeros_like(ref)
        for b in range(a - HMAX, a + m + HMAX, 8):
            step = -1 if b < 0 else (1 if b >= rows else 0)
            b_in = b - step * rows
            ref = tiles[(r + step) % 8][b_in // half]
            part = slice(b_in % half, b_in % half + 8)
            inside = {-1: z_of(r) > 0, 0: None, 1: z_of(r) < 7}[step]
            to = slice(b - a + HMAX, b - a + HMAX + 8)

            def load(p):
                value = ref[p, part, :]
                return value if inside is None else jnp.where(inside, value, 0.0)

            for p in range(planes):
                mains[n][p, to, :] = load(p)
            for k in range(2):
                packs.append(load(planes + k))
                homes.append((n, 8 * k, to))
    packs = jnp.concatenate(packs, axis=0)
    for q in range(8):
        turned = roll_lanes(packs, -(8 + 16 * q))
        for i, (n, p, to) in enumerate(homes):
            sides[n][p + q, to, :] = turned[8 * i:8 * i + 8]

    lane = lax.broadcasted_iota(jnp.int32, (rows, LANES), 1)

    def rotated(pieces, amount):
        turned = pltpu.roll(jnp.concatenate(pieces, axis=0), amount, 1)
        out, at = [], 0
        for x in pieces:
            out.append(turned[at:at + x.shape[0]])
            at += x.shape[0]
        return out

    def per_offset(o, carry):
        hx = shifts_ref[o, 0]
        hy = shifts_ref[o, 1]
        wrap_s = (lane < -hx) | (lane >= LANES - hx)
        wrap_r = (lane < hx) | (lane >= LANES + hx)
        to_s = lax.rem(hx + LANES, LANES)
        to_r = lax.rem(LANES - hx, LANES)
        s_at = HMAX - hy
        r_at = HMAX + hy

        def piece(n, plane, start, wrap):
            m = segments[n][2]
            a = mains[n][plane, pl.ds(start, m), :]
            return jnp.where(wrap[:m], sides[n][plane, pl.ds(start, m), :], a)

        parts = [(n, z) for n in range(n_seg) for z in range(depth)]
        sources, receivers = [], []
        for n, z in parts:
            for t in range(STEPS):
                sources.append(piece(n, t * depth + z, s_at, wrap_s))
                receivers.append(piece(n, (STEPS + t) * depth + z, r_at, wrap_r))
        sources = rotated(sources, to_s)
        receivers = rotated(receivers, to_r)
        terms = []
        for i, (n, z) in enumerate(parts):
            r, a, m = segments[n]
            s1, s2 = sources[2 * i:2 * i + 2]
            r1, r2 = receivers[2 * i:2 * i + 2]
            full = s1 * r1 + s2 * r2
            images[n][o, z] = full.astype(jnp.bfloat16)
            y_at = pl.multiple_of(z_of(r) * rows + a, half)
            observed = observed_ref[o, z, pl.ds(y_at, m), :].astype(jnp.float32)
            terms.append((full - observed) * s2)
        terms = rotated(terms, to_s)
        kept = []
        for (n, z), t in zip(parts, terms):
            m = segments[n][2]
            at = (z, pl.ds(r_at, m))
            inner = sums[n][0][at] + jnp.where(wrap_r[:m], 0.0, t)
            outer = sums[n][1][at] + jnp.where(wrap_r[:m], t, 0.0)
            kept.append((n, at, inner, outer))
        for n, at, inner, outer in kept:
            sums[n][0][at] = inner
            sums[n][1][at] = outer
        return carry

    for part in range(2):
        lax.fori_loop(part * (count // 2), (part + 1) * (count // 2), per_offset, 0, unroll=UNROLL)
        for n in range(n_seg):
            put(n, part).start()

    if last:
        all_core, all_side = refs[3 * n_seg + 1:]
        all_core[...] = jnp.zeros_like(all_core)
        all_side[...] = jnp.zeros_like(all_side)
        mine = [(segment, c, e) for segment, (c, e) in zip(segments, sums)]
        for (r, a, m), c, e in earlier + mine:
            at = pl.multiple_of(z_of(r) * rows + a, half)
            all_core[:, pl.ds(at, m + 2 * HMAX), :] += c[...]
            all_side[:, pl.ds(at, m + 2 * HMAX), :] += e[...]
        n_tiles = all_rows // half
        for tile in range(n_tiles):
            at = HMAX + tile * half
            for z in range(depth):
                core_out[tile, z * half:(z + 1) * half, :] = all_core[z, at:at + half, :]
        lane8 = lax.broadcasted_iota(jnp.int32, (8 * n_tiles, LANES), 1)
        strip = jnp.zeros((8 * n_tiles, LANES), jnp.float32)
        for q in range(8):
            z, k = q % 4, q // 4
            starts = [HMAX + tile * half + 8 * k for tile in range(n_tiles)]
            part = jnp.concatenate([all_side[z, at:at + 8, :] for at in starts], axis=0)
            here = (lane8 >= 16 * q) & (lane8 < 16 * q + 16)
            strip = jnp.where(here, roll_lanes(part, 8 + 16 * q), strip)
        cut = 4 * n_tiles
        low = lax.rem(lane8[:cut], 16) < HMAX
        lefts = jnp.where(low, strip[:cut], roll_lanes(strip[cut:], HMAX))
        rights = jnp.where(low, roll_lanes(strip[:cut], -HMAX), strip[cut:])
        even_x = where_ref[1] == 0
        send_in[...] = jnp.where(even_x, rights, lefts)
        send_out[...] = jnp.where(even_x, lefts, rights)
    for n in range(n_seg):
        for part in range(2):
            put(n, part).wait()


def merge_kernel(where_ref, core_ref, inner_ref, outer_ref, out_ref):
    n_tiles = core_ref.shape[0]
    cut = inner_ref.shape[0]
    even_x = where_ref[1] == 0
    from_right = jnp.where(even_x, inner_ref[...], outer_ref[...])
    from_left = jnp.where(even_x, outer_ref[...], inner_ref[...])
    lane = lax.broadcasted_iota(jnp.int32, (cut, LANES), 1)
    for group in range(2):
        for q in range(8):
            slot = 16 * q + HMAX * group
            extra = jnp.where(lane < HMAX, roll_lanes(from_left, -slot), 0.0)
            extra = jnp.where(lane >= LANES - HMAX, roll_lanes(from_right, 120 - slot), extra)
            at = (q % 4) * 16 + (q // 4) * 8
            for i in range(n_tiles // 2):
                tile = group * (n_tiles // 2) + i
                out_ref[tile, at:at + 8, :] = core_ref[tile, at:at + 8, :] + extra[8 * i:8 * i + 8]


def total_kernel(parts_ref, out_ref):
    total = parts_ref[0]
    for i in range(1, parts_ref.shape[0]):
        total = total + parts_ref[i]
    rows = out_ref.shape[1]
    for z in range(out_ref.shape[0]):
        out_ref[z] = total[z * rows:(z + 1) * rows] * (1.0 / OFF_SIDE)


def on_device(src_prev, src_now, rcv_prev, rcv_now, velocity, shift_table, ref_image):
    depth, rows, cols = src_now.shape
    n_off = lax.axis_size("offset")
    n_space = lax.axis_size("space")
    all_rows = ref_image.shape[2]
    shape = jax.ShapeDtypeStruct
    f32 = jnp.float32
    whole = pl.BlockSpec(memory_space=pltpu.VMEM)
    scalars = pl.BlockSpec(memory_space=pltpu.SMEM)
    anywhere = pl.BlockSpec(memory_space=pl.ANY)
    me = lax.axis_index("offset")
    where = jnp.stack([me // 2, lax.axis_index("space") % 2, me % 2]).astype(jnp.int32)

    raw, edge = pl.pallas_call(
        edges_kernel,
        out_shape=[shape((5, depth, rows, cols), f32), shape((5, rows, cols), f32)],
        name="edges",
    )(src_prev, src_now, rcv_prev, rcv_now, velocity)
    inner_x, outer_x = swaps(n_space)
    inner_y, outer_y = swaps(n_off)
    got_in = lax.ppermute(edge, "space", inner_x)
    got_out = lax.ppermute(edge, "space", outer_x)
    line = shape((5, 8, 2 * LANES), f32)
    wide, send_in, send_out = pl.pallas_call(
        widen_kernel,
        in_specs=[scalars] * 2 + [whole] * 3,
        out_shape=[shape((5, depth, rows, 2 * LANES), f32), line, line],
        name="widen", compiler_params=SMALL,
    )(where, shift_table, raw, got_in, got_out)
    got_in = lax.ppermute(send_in, "offset", inner_y)
    got_out = lax.ppermute(send_out, "offset", outer_y)
    planes = 4 * depth + 2
    tile = pl.pallas_call(
        wave_kernel,
        in_specs=[scalars] + [whole] * 3,
        out_shape=shape((planes, rows, LANES), f32),
        name="wave", compiler_params=SMALL,
    )(where, wide, got_in, got_out)

    other = lax.ppermute(tile, "offset", inner_y)
    is_low = (me % 2) == 0
    pair = jnp.stack([jnp.where(is_low, tile, other), jnp.where(is_low, other, tile)])

    def turn(d):
        return [(i, (i - 2 * d) % n_off) for i in range(n_off)]

    tiles = [(pair[0], pair[1])] + [None] * 7
    touched = pl.pallas_call(
        touch_kernel,
        in_specs=[whole],
        out_specs=whole,
        out_shape=shape((8, LANES), f32),
        compiler_params=SMALL,
        cost_estimate=pl.CostEstimate(flops=0, bytes_accessed=8_000_000, transcendentals=0),
        name="touch",
    )(ref_image)
    local = shift_table.shape[0]
    image = None
    done = []
    up = down = pair
    for at, call in enumerate(CALLS):
        first, last = call == CALLS[0], call == CALLS[-1]
        if first:
            up = lax.ppermute(pair, "offset", turn(1))
            down = lax.ppermute(pair, "offset", turn(-1))
            up, down, touched = lax.optimization_barrier((up, down, touched))
            tiles[1], tiles[7] = (up[0], up[1]), (down[0], down[1])
        if at < 2:
            next_up = lax.ppermute(up, "offset", turn(1))
            next_down = lax.ppermute(down, "offset", turn(-1))
        elif at == 2:
            next_up = lax.ppermute(up[0], "offset", turn(1))
            next_down = lax.ppermute(down[1], "offset", turn(-1))
        args = [where, shift_table, ref_image]
        specs = [scalars, scalars, whole]
        if first:
            args.append(touched)
            specs.append(whole)
        for r in needed(call):
            args += tiles[r]
            specs += [whole, whole]
        aliases = {}
        if not first:
            aliases = {len(args): 0}
            args.append(image)
            specs.append(anywhere)
        sums = [(depth, m + 2 * HMAX, LANES) for _, _, m in call for _ in range(2)]
        fields = [pltpu.VMEM((4 * depth, m + 2 * HMAX, LANES), f32) for _, _, m in call]
        scratch = fields + fields
        scratch += [pltpu.VMEM((local, depth, m, LANES), jnp.bfloat16) for _, _, m in call]
        scratch += [pltpu.SemaphoreType.DMA((len(call), 2))]
        if last:
            args += done
            specs += [whole] * len(done)
            scratch = [pltpu.VMEM(dims, f32) for dims in sums] + scratch
            scratch += [pltpu.VMEM((depth, all_rows + 2 * HMAX, LANES), f32)] * 2
            half_strip = shape((n_off * 4, LANES), f32)
            outs = [shape((n_off, depth * rows, LANES), f32), half_strip, half_strip]
        else:
            outs = [shape(dims, f32) for dims in sums]
        image, *rest = pl.pallas_call(
            functools.partial(image_kernel, call, first, last),
            in_specs=specs,
            out_specs=[anywhere] + [whole] * len(outs),
            out_shape=[shape(ref_image.shape, jnp.bfloat16)] + outs,
            scratch_shapes=scratch,
            input_output_aliases=aliases,
            compiler_params=pltpu.CompilerParams(vmem_limit_bytes=16 * 2**20),
            cost_estimate=pl.CostEstimate(
                flops=20_000_000, bytes_accessed=8_000_000, transcendentals=0
            ),
            name="image",
        )(*args)
        done += rest
        if not last:
            up, down, image = lax.optimization_barrier((next_up, next_down, image))
            if at < 2:
                tiles[at + 2], tiles[6 - at] = (up[0], up[1]), (down[0], down[1])
            else:
                tiles[4] = (up, down)

    core, send_in, send_out = rest
    got_in = lax.ppermute(send_in, "space", inner_x)
    got_out = lax.ppermute(send_out, "space", outer_x)
    parts = pl.pallas_call(
        merge_kernel,
        in_specs=[scalars] + [whole] * 3,
        out_shape=shape(core.shape, f32),
        name="merge", compiler_params=SMALL,
    )(where, core, got_in, got_out)
    parts = lax.all_to_all(parts, "offset", 0, 0)
    adjoint = pl.pallas_call(
        total_kernel, out_shape=shape((depth, rows, cols), f32), name="total", compiler_params=SMALL
    )(parts)
    return image, adjoint


def solution(mesh):
    field = P(None, "offset", "space")
    in_specs = (field,) * 5 + (P("offset", None), P("offset", None, None, "space"))
    out_specs = (P("offset", None, None, "space"), field)
    return jax.shard_map(
        on_device, mesh=mesh, in_specs=in_specs, out_specs=out_specs, check_vma=False
    )
```

time: 117 us -> 110 us (0.940); the launches traced: 115 us -> 110 us
  waiting for transfers between devices: 30.7 us -> 21.5 us
  blocking collectives: 20.4 us -> 24 us
  Pallas kernels: 26.6 us -> 28.8 us
  starting transfers between devices: 32.5 us -> 30.5 us
    ppermute x15, waiting for transfers between devices: 30.7 us -> 21.5 us  [the longest x2 5.92 us: on_device(): next_down = lax.ppermute(down, 'offset', turn(-1))]
    all_to_all x1, blocking collectives: 20.4 us -> 24 us  [on_device(): parts = lax.all_to_all(parts, 'offset', 0, 0)]
    pallas_call x8 -> x9, Pallas kernels: 26 us -> 28.1 us  [the longest x4 23.9 us: on_device(): pl.pallas_call(functools.partial(image_kernel, call, first, last), in_spe...]
    ppermute x15, starting transfers between devices: 32.5 us -> 30.5 us  [the longest x2 6.35 us: on_device(): next_up = lax.ppermute(up, 'offset', turn(1))]
    unnamed x5 -> x7, local copies, waits for them, and re-layouts: 3.85 us -> 3.86 us
  transfers between devices with their start and end apart: 15 -> 15, of which waited for: 8 -> 8; matrix products, arithmetic and copies ran while one was open for 1% -> 1% of each run, Pallas kernels for 14% -> 16%
where the time goes in v3:
time: 110 us
  starting transfers between devices  30.5 us (28%)
  Pallas kernels  28.8 us (26%)
  blocking collectives  24 us (22%)
  waiting for transfers between devices  21.5 us (20%)
  local copies, waits for them, and re-layouts  3.98 us (4%)
    all_to_all x1, blocking collectives, on_device(): parts = lax.all_to_all(parts, 'offset', 0, 0)  24 us
    pallas_call x4, Pallas kernels, on_device(): pl.pallas_call(functools.partial(image_kernel, call, first, last), in_spe...  23.9 us
    ppermute x2, starting transfers between devices, on_device(): next_up = lax.ppermute(up, 'offset', turn(1))  6.35 us
    ppermute x2, waiting for transfers between devices, on_device(): next_down = lax.ppermute(down, 'offset', turn(-1))  5.92 us
    ppermute x1, waiting for transfers between devices, on_device(): got_out = lax.ppermute(send_out, 'space', outer_x)  5.7 us
    ppermute x1, starting transfers between devices, on_device(): other = lax.ppermute(tile, 'offset', inner_y)  4.89 us
    ppermute x1, starting transfers between devices, on_device(): got_out = lax.ppermute(edge, 'space', outer_x)  4.24 us
    ppermute x1, starting transfers between devices, on_device(): up = lax.ppermute(pair, 'offset', turn(1))  4.03 us
  transfers between devices with their start and end apart: 15, of which 8 were waited for; matrix products, arithmetic and copies ran while one was open for 1% of the time, Pallas kernels for 16%

profile of v3, /device:TPU:16, one launch (start us, length us, event | category | flops | bytes accessed | tf_op | source)
XLA Modules:
  0.0 109.7 jit_solution(2054061630688397279)
XLA Ops:
  0.6 1.6 %edges.1 = (f32[5,4,16,128]{3,2,1,0:T(8,128)}, f32[5,16,128]{2,1,0:T(8,128)}) custom-call(f32[4,16,128]{2,1,0:T(8,128)} %refs_0_.1, f32[4,16,128]{2,1,0:T(8,128)} %refs_1_.5, f32[4,16,128]{2,1,0:T(8,128)} %refs_2_.5, f32[4,16,128]{2,1,0:T(8,128)} %refs_3_.1, f32[4,16,128]{2,1,0:T(8,128)} %refs_4_.1), custom_call_target="tpu_custom_call" | custom-call | tf_op jit(solution)/shard_map/edges/pallas_call | solution.py:342
  2.2 4.2 %collective-permute-start.1 = (f32[5,16,128]{2,1,0:T(8,128)}, f32[5,16,128]{2,1,0:T(8,128)S(1)}, u32[]{:S(2)}, u32[]{:S(2)}) collective-permute-start(f32[5,16,128]{2,1,0:T(8,128)} %get-tuple-element.49), channel_id=1, source_target_pairs={{16,32},{32,16},{48,64},{64,48},{80,96},{96,80},{112,128},{128,112... | collective-permute-start | bytes 122888 | tf_op jit(solution)/shard_map/ppermute | solution.py:350
  6.4 0.9 collective-permute-start
  7.4 0.8 copy.16.shifts_ref.refs_1_
  8.2 2.0 %collective-permute-done.1.outer_ref = f32[5,16,128]{2,1,0:T(8,128)S(1)} collective-permute-done((f32[5,16,128]{2,1,0:T(8,128)}, f32[5,16,128]{2,1,0:T(8,128)S(1)}, u32[]{:S(2)}, u32[]{:S(2)}) %collective-permute-start.1) | collective-permute-done | bytes 40992 | tf_op jit(solution)/shard_map/ppermute | solution.py:350
  10.1 0.9 copy-done.2
  11.0 0.8 widen.1
  11.9 1.6 %collective-permute-start.2 = (f32[5,8,256]{2,1,0:T(8,128)S(1)}, f32[5,8,256]{2,1,0:T(8,128)S(1)}, u32[]{:S(2)}, u32[]{:S(2)}) collective-permute-start(f32[5,8,256]{2,1,0:T(8,128)S(1)} %get-tuple-element.51), channel_id=1, source_target_pairs={{0,1},{1,0},{2,3},{3,2},{4,5},{5,4},{6,7},{7,6},{8,9},{9,8},{10,11... | collective-permute-start | bytes 122888 | tf_op jit(solution)/shard_map/ppermute | solution.py:358
  13.4 0.7 collective-permute-start.3
  14.1 1.9 %collective-permute-done.2.inner_ref = f32[5,8,256]{2,1,0:T(8,128)S(1)} collective-permute-done((f32[5,8,256]{2,1,0:T(8,128)S(1)}, f32[5,8,256]{2,1,0:T(8,128)S(1)}, u32[]{:S(2)}, u32[]{:S(2)}) %collective-permute-start.2) | collective-permute-done | bytes 40992 | tf_op jit(solution)/shard_map/ppermute | solution.py:358
  15.9 1.0 wave.1
  16.9 4.9 %collective-permute-start.4 = (f32[18,16,128]{2,1,0:T(8,128)S(1)}, f32[18,16,128]{2,1,0:T(8,128)S(1)}, u32[]{:S(2)}, u32[]{:S(2)}) collective-permute-start(f32[18,16,128]{2,1,0:T(8,128)S(1)} %wave.1), channel_id=1, source_target_pairs={{0,1},{1,0},{2,3},{3,2},{4,5},{5,4},{6,7},{7,6},{8,9},{9,8},{10,11... | collective-permute-start | bytes 442376 | tf_op jit(solution)/shard_map/ppermute | solution.py:368
  21.8 3.1 %collective-permute-done.4 = f32[18,16,128]{2,1,0:T(8,128)S(1)} collective-permute-done((f32[18,16,128]{2,1,0:T(8,128)S(1)}, f32[18,16,128]{2,1,0:T(8,128)S(1)}, u32[]{:S(2)}, u32[]{:S(2)}) %collective-permute-start.4) | collective-permute-done | bytes 147488 | tf_op jit(solution)/shard_map/ppermute | solution.py:368
  25.0 3.5 %collective-permute-start.6 = (f32[2,18,16,128]{3,2,1,0:T(8,128)S(1)}, f32[2,18,16,128]{3,2,1,0:T(8,128)S(1)}, u32[]{:S(2)}, u32[]{:S(2)}) collective-permute-start(f32[2,18,16,128]{3,2,1,0:T(8,128)S(1)} %pad_maximum_fusion), channel_id=1, source_target_pairs={{0,2},{1,3},{2,4},{3,5},{4,6},{5,7},{6,8},{7,9},{8,10},{9,11},{10,... | collective-permute-start | bytes 884744 | tf_op jit(solution)/shard_map/ppermute | solution.py:393
  28.5 4.0 %collective-permute-start.5 = (f32[2,18,16,128]{3,2,1,0:T(8,128)S(1)}, f32[2,18,16,128]{3,2,1,0:T(8,128)S(1)}, u32[]{:S(2)}, u32[]{:S(2)}) collective-permute-start(f32[2,18,16,128]{3,2,1,0:T(8,128)S(1)} %pad_maximum_fusion), channel_id=1, source_target_pairs={{0,14},{1,15},{2,0},{3,1},{4,2},{5,3},{6,4},{7,5},{8,6},{9,7},{10,... | collective-permute-start | bytes 884744 | tf_op jit(solution)/shard_map/ppermute | solution.py:392
  32.5 2.2 %copy-done = bf16[16,4,256,128]{3,2,1,0:T(8,128)(2,1)S(1)} copy-done((bf16[16,4,256,128]{3,2,1,0:T(8,128)(2,1)S(1)}, bf16[16,4,256,128]{3,2,1,0:T(8,128)(2,1)}, u32[]{:S(2)}) %copy-start) | copy-done | bytes 4194328
  34.7 2.4 %collective-permute-done.6 = f32[2,18,16,128]{3,2,1,0:T(8,128)S(1)} collective-permute-done((f32[2,18,16,128]{3,2,1,0:T(8,128)S(1)}, f32[2,18,16,128]{3,2,1,0:T(8,128)S(1)}, u32[]{:S(2)}, u32[]{:S(2)}) %collective-permute-start.6) | collective-permute-done | bytes 294944 | tf_op jit(solution)/shard_map/ppermute | solution.py:393
  37.7 3.7 %collective-permute-start.7 = (f32[2,18,16,128]{3,2,1,0:T(8,128)S(1)}, f32[2,18,16,128]{3,2,1,0:T(8,128)S(1)}, u32[]{:S(2)}, u32[]{:S(2)}) collective-permute-start(f32[2,18,16,128]{3,2,1,0:T(8,128)S(1)} %collective-permute-done.5), channel_id=1, source_target_pairs={{0,14},{1,15},{2,0},{3,1},{4,2},{5,3},{6,4},{7,5},{8,6},{9,7},{10,... | collective-permute-start | bytes 884744 | tf_op jit(solution)/shard_map/ppermute | solution.py:397
  41.4 5.8 %image.4 = (bf16[16,4,256,128]{3,2,1,0:T(8,128)(2,1)}, f32[4,32,128]{2,1,0:T(8,128)S(1)}, f32[4,32,128]{2,1,0:T(8,128)S(1)}, f32[4,48,128]{2,1,0:T(8,128)S(1)}, ...) custom-call(s32[3]{0:T(128)S(1)} %pad_add_fusion.where_ref.refs_0_, ...), custom_call_target="tpu_custom_call" | custom-call | flops 20000000 | bytes 8000000 | tf_op jit(solution)/shard_map/image/pallas_call | solution.py:429
  47.3 3.4 %collective-permute-done.8 = f32[2,18,16,128]{3,2,1,0:T(8,128)S(1)} collective-permute-done((f32[2,18,16,128]{3,2,1,0:T(8,128)S(1)}, f32[2,18,16,128]{3,2,1,0:T(8,128)S(1)}, u32[]{:S(2)}, u32[]{:S(2)}) %collective-permute-start.8) | collective-permute-done | bytes 294944 | tf_op jit(solution)/shard_map/ppermute | solution.py:398
  50.7 2.7 %collective-permute-start.9 = (f32[2,18,16,128]{3,2,1,0:T(8,128)S(1)}, f32[2,18,16,128]{3,2,1,0:T(8,128)S(1)}, u32[]{:S(2)}, u32[]{:S(2)}) collective-permute-start(f32[2,18,16,128]{3,2,1,0:T(8,128)S(1)} %collective-permute-done.7), channel_id=1, source_target_pairs={{0,14},{1,15},{2,0},{3,1},{4,2},{5,3},{6,4},{7,5},{8,6},{9,7},{10,... | collective-permute-start | bytes 884744 | tf_op jit(solution)/shard_map/ppermute | solution.py:397
  53.4 5.9 %image.5 = (bf16[16,4,256,128]{3,2,1,0:T(8,128)(2,1)}, f32[4,32,128]{2,1,0:T(8,128)S(1)}, f32[4,32,128]{2,1,0:T(8,128)S(1)}, f32[4,32,128]{2,1,0:T(8,128)S(1)}, ...) custom-call(s32[3]{0:T(128)S(1)} %pad_add_fusion.where_ref.refs_0_, ...), custom_call_target="tpu_custom_call", output_to_operand_aliasing={{0}: (11, {})} | custom-call | flops 20000000 | bytes 8000000 | tf_op jit(solution)/shard_map/image/pallas_call | solution.py:429
  59.3 2.5 %collective-permute-done.10 = f32[2,18,16,128]{3,2,1,0:T(8,128)S(1)} collective-permute-done((f32[2,18,16,128]{3,2,1,0:T(8,128)S(1)}, f32[2,18,16,128]{3,2,1,0:T(8,128)S(1)}, u32[]{:S(2)}, u32[]{:S(2)}) %collective-permute-start.10) | collective-permute-done | bytes 294944 | tf_op jit(solution)/shard_map/ppermute | solution.py:398
  61.9 0.8 collective-permute-start.11
  62.7 1.5 %collective-permute-start.12 = (f32[18,16,128]{2,1,0:T(8,128)S(1)}, f32[18,16,128]{2,1,0:T(8,128)S(1)}, u32[]{:S(2)}, u32[]{:S(2)}) collective-permute-start(f32[18,16,128]{2,1,0:T(8,128)S(1)} %get-tuple-element.95.refs_8_), channel_id=1, source_target_pairs={{0,2},{1,3},{2,4},{3,5},{4,6},{5,7},{6,8},{7,9},{8,10},{9,11},{10,... | collective-permute-start | bytes 442376 | tf_op jit(solution)/shard_map/ppermute | solution.py:401
  64.2 5.9 %image.6 = (bf16[16,4,256,128]{3,2,1,0:T(8,128)(2,1)}, f32[4,32,128]{2,1,0:T(8,128)S(1)}, f32[4,32,128]{2,1,0:T(8,128)S(1)}, f32[4,32,128]{2,1,0:T(8,128)S(1)}, ...) custom-call(s32[3]{0:T(128)S(1)} %pad_add_fusion.where_ref.refs_0_, ...), custom_call_target="tpu_custom_call", output_to_operand_aliasing={{0}: (11, {})} | custom-call | flops 20000000 | bytes 8000000 | tf_op jit(solution)/shard_map/image/pallas_call | solution.py:429
  70.2 6.2 %image.7 = (bf16[16,4,256,128]{3,2,1,0:T(8,128)(2,1)}, f32[16,64,128]{2,1,0:T(8,128)S(1)}, f32[64,128]{1,0:T(8,128)S(1)}, f32[64,128]{1,0:T(8,128)S(1)}) custom-call(s32[3]{0:T(128)S(1)} %pad_add_fusion.where_ref.refs_0_, s32[16,2]{1,0:T(8,128)S(1)} %copy.16.shifts_ref.refs_1_, ...), custom_call_target="tpu_custom_call", output_to_operand_aliasing={{0}: (9, {})} | custom-call | flops 20000000 | bytes 8000000 | tf_op jit(solution)/shard_map/image/pallas_call | solution.py:429
  76.5 1.9 %collective-permute-start.14 = (f32[64,128]{1,0:T(8,128)S(1)}, f32[64,128]{1,0:T(8,128)S(1)}, u32[]{:S(2)}, u32[]{:S(2)}) collective-permute-start(f32[64,128]{1,0:T(8,128)S(1)} %get-tuple-element.93), channel_id=1, source_target_pairs={{16,32},{32,16},{48,64},{64,48},{80,96},{96,80},{112,128},{128,112... | collective-permute-start | bytes 98312 | tf_op jit(solution)/shard_map/ppermute | solution.py:452
  78.5 5.7 %collective-permute-done.14.outer_ref = f32[64,128]{1,0:T(8,128)S(1)} collective-permute-done((f32[64,128]{1,0:T(8,128)S(1)}, f32[64,128]{1,0:T(8,128)S(1)}, u32[]{:S(2)}, u32[]{:S(2)}) %collective-permute-start.14) | collective-permute-done | bytes 32800 | tf_op jit(solution)/shard_map/ppermute | solution.py:452
  84.2 0.9 merge.1
  85.0 24.0 %all_to_all.5.parts_ref = f32[16,64,128]{2,1,0:T(8,128)S(1)} all-to-all(f32[16,64,128]{2,1,0:T(8,128)S(1)} %merge.1), channel_id=1, replica_groups=mesh['space'=16,'offset'=16] {'offset'}, dimensions={0} | all-to-all | bytes 1048576 | tf_op jit(solution)/shard_map/all_to_all | solution.py:459
  109.1 0.6 total.1
  (24 shorter events, 0.9 us)
Async XLA Ops:
  2.2 7.9 %collective-permute-start.1 = (f32[5,16,128]{2,1,0:T(8,128)}, f32[5,16,128]{2,1,0:T(8,128)S(1)}, u32[]{:S(2)}, u32[]{:S(2)}) collective-permute-start(f32[5,16,128]{2,1,0:T(8,128)} %get-tuple-element.49), channel_id=1, source_target_pairs={{16,32},{32,16},{48,64},{64,48},{80,96},{96,80},{112,128},{128,112... | collective-permute-start | bytes 122888 | tf_op jit(solution)/shard_map/ppermute | solution.py:350
  6.4 3.7 %collective-permute-start = (f32[5,16,128]{2,1,0:T(8,128)}, f32[5,16,128]{2,1,0:T(8,128)S(1)}, u32[]{:S(2)}, u32[]{:S(2)}) collective-permute-start(f32[5,16,128]{2,1,0:T(8,128)} %get-tuple-element.49), channel_id=1, source_target_pairs={{0,16},{16,0},{32,48},{48,32},{64,80},{80,64},{96,112},{112,96},{1... | collective-permute-start | bytes 122888 | tf_op jit(solution)/shard_map/ppermute | solution.py:349
  10.1 0.9 copy-start.2
  11.9 4.1 %collective-permute-start.2 = (f32[5,8,256]{2,1,0:T(8,128)S(1)}, f32[5,8,256]{2,1,0:T(8,128)S(1)}, u32[]{:S(2)}, u32[]{:S(2)}) collective-permute-start(f32[5,8,256]{2,1,0:T(8,128)S(1)} %get-tuple-element.51), channel_id=1, source_target_pairs={{0,1},{1,0},{2,3},{3,2},{4,5},{5,4},{6,7},{7,6},{8,9},{9,8},{10,11... | collective-permute-start | bytes 122888 | tf_op jit(solution)/shard_map/ppermute | solution.py:358
  13.4 2.5 %collective-permute-start.3 = (f32[5,8,256]{2,1,0:T(8,128)S(1)}, f32[5,8,256]{2,1,0:T(8,128)S(1)}, u32[]{:S(2)}, u32[]{:S(2)}) collective-permute-start(f32[5,8,256]{2,1,0:T(8,128)S(1)} %get-tuple-element.52), channel_id=1, source_target_pairs={{1,2},{2,1},{3,4},{4,3},{5,6},{6,5},{7,8},{8,7},{9,10},{10,9},{11,... | collective-permute-start | bytes 122888 | tf_op jit(solution)/shard_map/ppermute | solution.py:359
  16.9 8.0 %collective-permute-start.4 = (f32[18,16,128]{2,1,0:T(8,128)S(1)}, f32[18,16,128]{2,1,0:T(8,128)S(1)}, u32[]{:S(2)}, u32[]{:S(2)}) collective-permute-start(f32[18,16,128]{2,1,0:T(8,128)S(1)} %wave.1), channel_id=1, source_target_pairs={{0,1},{1,0},{2,3},{3,2},{4,5},{5,4},{6,7},{7,6},{8,9},{9,8},{10,11... | collective-permute-start | bytes 442376 | tf_op jit(solution)/shard_map/ppermute | solution.py:368
  25.0 12.1 %collective-permute-start.6 = (f32[2,18,16,128]{3,2,1,0:T(8,128)S(1)}, f32[2,18,16,128]{3,2,1,0:T(8,128)S(1)}, u32[]{:S(2)}, u32[]{:S(2)}) collective-permute-start(f32[2,18,16,128]{3,2,1,0:T(8,128)S(1)} %pad_maximum_fusion), channel_id=1, source_target_pairs={{0,2},{1,3},{2,4},{3,5},{4,6},{5,7},{6,8},{7,9},{8,10},{9,11},{10,... | collective-permute-start | bytes 884744 | tf_op jit(solution)/shard_map/ppermute | solution.py:393
  28.5 9.2 %collective-permute-start.5 = (f32[2,18,16,128]{3,2,1,0:T(8,128)S(1)}, f32[2,18,16,128]{3,2,1,0:T(8,128)S(1)}, u32[]{:S(2)}, u32[]{:S(2)}) collective-permute-start(f32[2,18,16,128]{3,2,1,0:T(8,128)S(1)} %pad_maximum_fusion), channel_id=1, source_target_pairs={{0,14},{1,15},{2,0},{3,1},{4,2},{5,3},{6,4},{7,5},{8,6},{9,7},{10,... | collective-permute-start | bytes 884744 | tf_op jit(solution)/shard_map/ppermute | solution.py:392
  32.5 2.2 %copy-start = (bf16[16,4,256,128]{3,2,1,0:T(8,128)(2,1)S(1)}, bf16[16,4,256,128]{3,2,1,0:T(8,128)(2,1)}, u32[]{:S(2)}) copy-start(bf16[16,4,256,128]{3,2,1,0:T(8,128)(2,1)} %refs_2_.9) | copy-start | bytes 12582916
  34.7 6.7 %copy-start.1 = (bf16[16,4,256,128]{3,2,1,0:T(8,128)(2,1)S(1)}, bf16[16,4,256,128]{3,2,1,0:T(8,128)(2,1)}, u32[]{:S(2)}) copy-start(bf16[16,4,256,128]{3,2,1,0:T(8,128)(2,1)} %refs_2_.9) | copy-start | bytes 12582916
  37.7 9.6 %collective-permute-start.7 = (f32[2,18,16,128]{3,2,1,0:T(8,128)S(1)}, f32[2,18,16,128]{3,2,1,0:T(8,128)S(1)}, u32[]{:S(2)}, u32[]{:S(2)}) collective-permute-start(f32[2,18,16,128]{3,2,1,0:T(8,128)S(1)} %collective-permute-done.5), channel_id=1, source_target_pairs={{0,14},{1,15},{2,0},{3,1},{4,2},{5,3},{6,4},{7,5},{8,6},{9,7},{10,... | collective-permute-start | bytes 884744 | tf_op jit(solution)/shard_map/ppermute | solution.py:397
  41.4 9.3 %collective-permute-start.8 = (f32[2,18,16,128]{3,2,1,0:T(8,128)S(1)}, f32[2,18,16,128]{3,2,1,0:T(8,128)S(1)}, u32[]{:S(2)}, u32[]{:S(2)}) collective-permute-start(f32[2,18,16,128]{3,2,1,0:T(8,128)S(1)} %collective-permute-done.6), channel_id=1, source_target_pairs={{0,2},{1,3},{2,4},{3,5},{4,6},{5,7},{6,8},{7,9},{8,10},{9,11},{10,... | collective-permute-start | bytes 884744 | tf_op jit(solution)/shard_map/ppermute | solution.py:398
  50.7 8.7 %collective-permute-start.9 = (f32[2,18,16,128]{3,2,1,0:T(8,128)S(1)}, f32[2,18,16,128]{3,2,1,0:T(8,128)S(1)}, u32[]{:S(2)}, u32[]{:S(2)}) collective-permute-start(f32[2,18,16,128]{3,2,1,0:T(8,128)S(1)} %collective-permute-done.7), channel_id=1, source_target_pairs={{0,14},{1,15},{2,0},{3,1},{4,2},{5,3},{6,4},{7,5},{8,6},{9,7},{10,... | collective-permute-start | bytes 884744 | tf_op jit(solution)/shard_map/ppermute | solution.py:397
  53.3 8.5 %collective-permute-start.10 = (f32[2,18,16,128]{3,2,1,0:T(8,128)S(1)}, f32[2,18,16,128]{3,2,1,0:T(8,128)S(1)}, u32[]{:S(2)}, u32[]{:S(2)}) collective-permute-start(f32[2,18,16,128]{3,2,1,0:T(8,128)S(1)} %collective-permute-done.8), channel_id=1, source_target_pairs={{0,2},{1,3},{2,4},{3,5},{4,6},{5,7},{6,8},{7,9},{8,10},{9,11},{10,... | collective-permute-start | bytes 884744 | tf_op jit(solution)/shard_map/ppermute | solution.py:398
  61.9 8.3 %collective-permute-start.11 = (f32[18,16,128]{2,1,0:T(8,128)S(1)}, f32[18,16,128]{2,1,0:T(8,128)S(1)}, u32[]{:S(2)}, u32[]{:S(2)}) collective-permute-start(f32[18,16,128]{2,1,0:T(8,128)S(1)} %get-tuple-element.97.refs_5_.refs_3_), channel_id=1, source_target_pairs={{0,14},{1,15},{2,0},{3,1},{4,2},{5,3},{6,4},{7,5},{8,6},{9,7},{10,... | collective-permute-start | bytes 442376 | tf_op jit(solution)/shard_map/ppermute | solution.py:400
  62.7 7.5 %collective-permute-start.12 = (f32[18,16,128]{2,1,0:T(8,128)S(1)}, f32[18,16,128]{2,1,0:T(8,128)S(1)}, u32[]{:S(2)}, u32[]{:S(2)}) collective-permute-start(f32[18,16,128]{2,1,0:T(8,128)S(1)} %get-tuple-element.95.refs_8_), channel_id=1, source_target_pairs={{0,2},{1,3},{2,4},{3,5},{4,6},{5,7},{6,8},{7,9},{8,10},{9,11},{10,... | collective-permute-start | bytes 442376 | tf_op jit(solution)/shard_map/ppermute | solution.py:401
  76.4 2.0 %collective-permute-start.13 = (f32[64,128]{1,0:T(8,128)S(1)}, f32[64,128]{1,0:T(8,128)S(1)}, u32[]{:S(2)}, u32[]{:S(2)}) collective-permute-start(f32[64,128]{1,0:T(8,128)S(1)} %get-tuple-element.92), channel_id=1, source_target_pairs={{0,16},{16,0},{32,48},{48,32},{64,80},{80,64},{96,112},{112,96},{1... | collective-permute-start | bytes 98312 | tf_op jit(solution)/shard_map/ppermute | solution.py:451
  76.5 7.6 %collective-permute-start.14 = (f32[64,128]{1,0:T(8,128)S(1)}, f32[64,128]{1,0:T(8,128)S(1)}, u32[]{:S(2)}, u32[]{:S(2)}) collective-permute-start(f32[64,128]{1,0:T(8,128)S(1)} %get-tuple-element.93), channel_id=1, source_target_pairs={{16,32},{32,16},{48,64},{64,48},{80,96},{96,80},{112,128},{128,112... | collective-permute-start | bytes 98312 | tf_op jit(solution)/shard_map/ppermute | solution.py:452

commit v4 on v3

--- a/solution.py
+++ b/solution.py
@@ -16,10 +16,10 @@
 SMALL = pltpu.CompilerParams(vmem_limit_bytes=6 * 2**20)
 
 CALLS = (
-    ((7, 16, 16), (0, 0, 32), (1, 0, 16)),
-    ((1, 16, 16), (2, 0, 16), (6, 16, 16), (7, 0, 16)),
-    ((2, 16, 16), (3, 0, 16), (5, 16, 16), (6, 0, 16)),
-    ((3, 16, 16), (4, 0, 32), (5, 0, 16)),
+    ((7, 8, 24), (0, 0, 32), (1, 0, 24)),
+    ((1, 24, 8), (2, 0, 24), (6, 8, 24), (7, 0, 8)),
+    ((2, 24, 8), (3, 0, 24), (5, 8, 24), (6, 0, 8)),
+    ((3, 24, 8), (4, 0, 32), (5, 0, 8)),
 )
 
 
@@ -27,6 +27,10 @@
     inner = [(i, i ^ 1) for i in range(count)]
     outer = [(i, i + 1 if i % 2 else i - 1) for i in range(1, count - 1)]
     return inner, outer
+
+
+def whole_tiles(rows):
+    return -(-rows // 16) * 16
 
 
 def roll_lanes(x, shift):
@@ -51,14 +55,23 @@
         edge_ref[f] = packed[f * rows:(f + 1) * rows]
 
 
+def hold_kernel(ref, out_ref):
+    out_ref[...] = ref[...]
+
+
 def touch_kernel(ref, out_ref):
     out_ref[...] = ref[0, 0, :8, :].astype(jnp.float32)
 
 
-def widen_kernel(where_ref, shifts_ref, raw_ref, inner_ref, outer_ref, wide_ref, send_in_ref, send_out_ref):
+def spread(packed, z):
+    lane = lax.broadcasted_iota(jnp.int32, packed.shape, 1)
+    beside = jnp.where(lane >= LANES - REACH, roll_lanes(packed, 96 - 32 * z), 0.0)
+    return jnp.where(lane < REACH, roll_lanes(packed, -32 * z), beside)
+
+
+def widen_kernel(where_ref, shifts_ref, raw_ref, inner_ref, outer_ref, own_ref, line_ref):
     fields, depth, rows, cols = raw_ref.shape
-    total = fields * rows
-    lane = lax.broadcasted_iota(jnp.int32, (total, LANES), 1)
+    lane = lax.broadcasted_iota(jnp.int32, (fields * rows, LANES), 1)
     row = lax.broadcasted_iota(jnp.int32, (8, 2 * LANES), 0)
     even_x = where_ref[1] == 0
     even_y = where_ref[2] == 0
@@ -66,35 +79,54 @@
     outer = jnp.concatenate([outer_ref[f] for f in range(fields)], axis=0)
     left = jnp.where(even_x, outer, inner)
     right = jnp.where(even_x, inner, outer)
-    upper = [jnp.zeros((8, 2 * LANES), jnp.float32) for _ in range(fields)]
-    lower = list(upper)
+    packed = jnp.where(lax.rem(lane, 32) < 16, right, left)
+    for f in range(fields):
+        own_ref[fields * depth + f] = packed[f * rows:(f + 1) * rows]
+        for z in range(depth):
+            own_ref[f * depth + z] = raw_ref[f, z]
+    lines = [jnp.zeros((8, 2 * LANES), jnp.float32) for _ in range(fields)]
     for z in range(depth):
-        beside = jnp.where(lane >= cols - REACH, roll_lanes(left, 96 - 32 * z), 0.0)
-        beside = jnp.where(lane < REACH, roll_lanes(right, -32 * z), beside)
+        beside = spread(packed, z)
         here = (row >= 2 * z) & (row < 2 * z + 2)
         for f in range(fields):
             both = jnp.concatenate([raw_ref[f, z], beside[f * rows:(f + 1) * rows]], axis=1)
-            wide_ref[f, z] = both
-            upper[f] = jnp.where(here, pltpu.roll(both[:8], 2 * z, 0), upper[f])
-            lower[f] = jnp.where(here, pltpu.roll(both[rows - 8:], (2 * z + 2) % 8, 0), lower[f])
+            upper = pltpu.roll(both[:8], 2 * z, 0)
+            lower = pltpu.roll(both[rows - 8:], (2 * z + 2) % 8, 0)
+            lines[f] = jnp.where(here, jnp.where(even_y, upper, lower), lines[f])
     for f in range(fields):
-        send_in_ref[f] = jnp.where(even_y, lower[f], upper[f])
-        send_out_ref[f] = jnp.where(even_y, upper[f], lower[f])
-
-
-def wave_kernel(where_ref, wide_ref, inner_ref, outer_ref, tile_ref):
-    depth, rows, width = wide_ref.shape[1:]
+        line_ref[f] = lines[f]
+
+
+def wave_kernel(where_ref, own_ref, other_ref, near_ref, far_ref, pair_ref):
+    fields = near_ref.shape[0]
+    depth = own_ref.shape[0] // fields - 1
+    half = own_ref.shape[1]
+    rows = 2 * half
+    width = 2 * LANES
     high_rows = rows + 8
     lane = lax.broadcasted_iota(jnp.int32, (rows, LANES), 1)
     edge_row = lax.broadcasted_iota(jnp.int32, (8, width), 0)
     even_y = where_ref[2] == 0
-    top = [jnp.where(even_y, outer_ref[f], inner_ref[f]) for f in range(5)]
-    bottom = [jnp.where(even_y, inner_ref[f], outer_ref[f]) for f in range(5)]
+
+    def ordered(mine, other):
+        return [jnp.where(even_y, mine, other), jnp.where(even_y, other, mine)]
+
+    packed_all = []
+    for f in range(fields):
+        packed_all += ordered(own_ref[fields * depth + f], other_ref[fields * depth + f])
+    packed_all = jnp.concatenate(packed_all, axis=0)
+    besides = [spread(packed_all, z) for z in range(depth)]
+    top = [jnp.where(even_y, near_ref[f], far_ref[f]) for f in range(fields)]
+    bottom = [jnp.where(even_y, far_ref[f], near_ref[f]) for f in range(fields)]
 
     def whole(f, z):
         edge = jnp.where(edge_row >= 6, pltpu.roll(top[f], (6 - 2 * z) % 8, 0), 0.0)
         edge = jnp.where(edge_row < 2, pltpu.roll(bottom[f], (8 - 2 * z) % 8, 0), edge)
-        return jnp.concatenate([wide_ref[f, z], edge], axis=0)
+        plane = f * depth + z
+        body = jnp.concatenate(ordered(own_ref[plane], other_ref[plane]), axis=0)
+        beside = besides[z][f * rows:(f + 1) * rows]
+        both = jnp.concatenate([body, beside], axis=1)
+        return jnp.concatenate([both, edge], axis=0)
 
     speed = [whole(4, z) for z in range(depth)]
 
@@ -102,13 +134,13 @@
         out = []
         for z in range(depth):
             c = now[z]
-            beside = pltpu.roll(c, 1, 0) + pltpu.roll(c, high_rows - 1, 0)
-            beside = beside + pltpu.roll(c, 1, 1) + pltpu.roll(c, width - 1, 1)
+            near = pltpu.roll(c, 1, 0) + pltpu.roll(c, high_rows - 1, 0)
+            near = near + pltpu.roll(c, 1, 1) + pltpu.roll(c, width - 1, 1)
             if z > 0:
-                beside = beside + now[z - 1]
+                near = near + now[z - 1]
             if z < depth - 1:
-                beside = beside + now[z + 1]
-            out.append(2.0 * c - prev[z] + speed[z] * (beside - 6.0 * c))
+                near = near + now[z + 1]
+            out.append(2.0 * c - prev[z] + speed[z] * (near - 6.0 * c))
         return out
 
     packed = [jnp.zeros((rows, LANES), jnp.float32) for _ in range(2)]
@@ -119,13 +151,15 @@
             prev, now = now, advance(prev, now)
             for z in range(depth):
                 plane = (pair * STEPS + t) * depth + z
-                tile_ref[plane] = now[z][:rows, :LANES]
                 q = plane % 8
-                beside = roll_lanes(now[z][:rows, LANES:], (8 + 16 * q) % LANES)
+                for k in range(2):
+                    pair_ref[k, plane] = now[z][k * half:(k + 1) * half, :LANES]
+                beside = roll_lanes(now[z][:rows, LANES:], 8 + 16 * q)
                 here = (lane >= 16 * q) & (lane < 16 * q + 16)
                 packed[plane // 8] = jnp.where(here, beside, packed[plane // 8])
-    for k in range(2):
-        tile_ref[4 * depth + k] = packed[k]
+    for j in range(2):
+        for k in range(2):
+            pair_ref[k, 4 * depth + j] = packed[j][k * half:(k + 1) * half]
 
 
 def needed(call):
@@ -171,10 +205,12 @@
 
     def put(n, part):
         r, a, m = segments[n]
-        at = pl.multiple_of(z_of(r) * rows + a, half)
+        at = pl.multiple_of(z_of(r) * rows + a, 8)
         which = pl.ds(part * (count // 2), count // 2)
         return pltpu.make_async_copy(
-            images[n].at[which], image_hbm.at[which, :, pl.ds(at, m), :], sems.at[n, part]
+            images[n].at[which, :, pl.ds(0, m), :],
+            image_hbm.at[which, :, pl.ds(at, m), :],
+            sems.at[n, part],
         )
 
     packs, homes = [], []
@@ -243,9 +279,11 @@
             s1, s2 = sources[2 * i:2 * i + 2]
             r1, r2 = receivers[2 * i:2 * i + 2]
             full = s1 * r1 + s2 * r2
-            images[n][o, z] = full.astype(jnp.bfloat16)
-            y_at = pl.multiple_of(z_of(r) * rows + a, half)
-            observed = observed_ref[o, z, pl.ds(y_at, m), :].astype(jnp.float32)
+            images[n][o, z, :m] = full.astype(jnp.bfloat16)
+            lead = a % half
+            y_at = pl.multiple_of(z_of(r) * rows + a - lead, half)
+            observed = observed_ref[o, z, pl.ds(y_at, whole_tiles(lead + m)), :]
+            observed = observed.astype(jnp.float32)[lead:lead + m]
             terms.append((full - observed) * s2)
         terms = rotated(terms, to_s)
         kept = []
@@ -271,7 +309,7 @@
         all_side[...] = jnp.zeros_like(all_side)
         mine = [(segment, c, e) for segment, (c, e) in zip(segments, sums)]
         for (r, a, m), c, e in earlier + mine:
-            at = pl.multiple_of(z_of(r) * rows + a, half)
+            at = pl.multiple_of(z_of(r) * rows + a, 8)
             all_core[:, pl.ds(at, m + 2 * HMAX), :] += c[...]
             all_side[:, pl.ds(at, m + 2 * HMAX), :] += e[...]
         n_tiles = all_rows // half
@@ -346,28 +384,35 @@
     )(src_prev, src_now, rcv_prev, rcv_now, velocity)
     inner_x, outer_x = swaps(n_space)
     inner_y, outer_y = swaps(n_off)
+    same_y = [(i, i + 2 if i % 2 else i - 2) for i in range(n_off)]
+    same_y = [(i, j) for i, j in same_y if 0 <= j < n_off]
     got_in = lax.ppermute(edge, "space", inner_x)
     got_out = lax.ppermute(edge, "space", outer_x)
-    line = shape((5, 8, 2 * LANES), f32)
-    wide, send_in, send_out = pl.pallas_call(
+    raw = pl.pallas_call(
+        hold_kernel,
+        in_specs=[whole],
+        out_specs=whole,
+        out_shape=shape(raw.shape, f32),
+        compiler_params=SMALL,
+        cost_estimate=pl.CostEstimate(flops=0, bytes_accessed=4_000_000, transcendentals=0),
+        name="hold",
+    )(raw)
+    own, line = pl.pallas_call(
         widen_kernel,
         in_specs=[scalars] * 2 + [whole] * 3,
-        out_shape=[shape((5, depth, rows, 2 * LANES), f32), line, line],
+        out_shape=[shape((5 * depth + 5, rows, cols), f32), shape((5, 8, 2 * LANES), f32)],
         name="widen", compiler_params=SMALL,
     )(where, shift_table, raw, got_in, got_out)
-    got_in = lax.ppermute(send_in, "offset", inner_y)
-    got_out = lax.ppermute(send_out, "offset", outer_y)
+    other = lax.ppermute(own, "offset", inner_y)
+    near = lax.ppermute(line, "offset", outer_y)
+    far = lax.ppermute(line, "offset", same_y)
     planes = 4 * depth + 2
-    tile = pl.pallas_call(
+    pair = pl.pallas_call(
         wave_kernel,
-        in_specs=[scalars] + [whole] * 3,
-        out_shape=shape((planes, rows, LANES), f32),
+        in_specs=[scalars] + [whole] * 4,
+        out_shape=shape((2, planes, rows, LANES), f32),
         name="wave", compiler_params=SMALL,
-    )(where, wide, got_in, got_out)
-
-    other = lax.ppermute(tile, "offset", inner_y)
-    is_low = (me % 2) == 0
-    pair = jnp.stack([jnp.where(is_low, tile, other), jnp.where(is_low, other, tile)])
+    )(where, own, other, near, far)
 
     def turn(d):
         return [(i, (i - 2 * d) % n_off) for i in range(n_off)]
@@ -415,7 +460,7 @@
         sums = [(depth, m + 2 * HMAX, LANES) for _, _, m in call for _ in range(2)]
         fields = [pltpu.VMEM((4 * depth, m + 2 * HMAX, LANES), f32) for _, _, m in call]
         scratch = fields + fields
-        scratch += [pltpu.VMEM((local, depth, m, LANES), jnp.bfloat16) for _, _, m in call]
+        scratch += [pltpu.VMEM((local, depth, whole_tiles(m), LANES), jnp.bfloat16) for _, _, m in call]
         scratch += [pltpu.SemaphoreType.DMA((len(call), 2))]
         if last:
             args += done

time: 110 us -> 104 us (0.945); the launches traced: 110 us -> 103 us
  waiting for transfers between devices: 21.5 us -> 13 us
    ppermute x3, starting transfers between devices: 7.12 us -> 3.52 us  [the longest x1 1.58 us: on_device(): other = lax.ppermute(own, 'offset', inner_y)]
    ppermute x1, waiting for transfers between devices: 5.7 us -> 2.41 us  [on_device(): got_out = lax.ppermute(send_out, 'space', outer_x)]
    ppermute x1, starting transfers between devices: 1.92 us -> 5.21 us  [on_device(): got_out = lax.ppermute(send_out, 'space', outer_x)]
    ppermute x2, waiting for transfers between devices: 5.92 us -> 3.24 us  [on_device(): next_down = lax.ppermute(down, 'offset', turn(-1))]
    ppermute x1, starting transfers between devices: 3.48 us -> 4.91 us  [on_device(): down = lax.ppermute(pair, 'offset', turn(-1))]
  transfers between devices with their start and end apart: 15 -> 15, of which waited for: 8 -> 6; matrix products, arithmetic and copies ran while one was open for 1% -> 1% of each run, Pallas kernels for 16% -> 18%
where the time goes in v4:
time: 104 us; the launch traced here: 103 us
  starting transfers between devices  31.5 us (30%)
  Pallas kernels  29.1 us (28%)
  blocking collectives  24 us (23%)
  waiting for transfers between devices  13 us (12%)
  local copies, waits for them, and re-layouts  4.01 us (4%)
    all_to_all x1, blocking collectives, on_device(): parts = lax.all_to_all(parts, 'offset', 0, 0)  24 us
    pallas_call x4, Pallas kernels, on_device(): pl.pallas_call(functools.partial(image_kernel, call, first, last), in_spe...  23.9 us
    ppermute x2, starting transfers between devices, on_device(): next_up = lax.ppermute(up, 'offset', turn(1))  5.33 us
    ppermute x1, starting transfers between devices, on_device(): got_out = lax.ppermute(send_out, 'space', outer_x)  5.21 us
    ppermute x1, starting transfers between devices, on_device(): up = lax.ppermute(pair, 'offset', turn(1))  4.92 us
    ppermute x1, starting transfers between devices, on_device(): down = lax.ppermute(pair, 'offset', turn(-1))  4.91 us
    ppermute x1, starting transfers between devices, on_device(): got_out = lax.ppermute(edge, 'space', outer_x)  4.24 us
    ppermute x1, waiting for transfers between devices, on_device(): far = lax.ppermute(line, 'offset', same_y)  3.92 us
  transfers between devices with their start and end apart: 15, of which 6 were waited for; matrix products, arithmetic and copies ran while one was open for 1% of the time, Pallas kernels for 18%

profile of v4, /device:TPU:16, one launch (start us, length us, event | category | flops | bytes accessed | tf_op | source)
XLA Modules:
  0.0 102.5 jit_solution(9822773792214012949)
XLA Ops:
  0.6 1.6 %edges.1 = (f32[5,4,16,128]{3,2,1,0:T(8,128)}, f32[5,16,128]{2,1,0:T(8,128)}) custom-call(f32[4,16,128]{2,1,0:T(8,128)} %refs_0_.1, f32[4,16,128]{2,1,0:T(8,128)} %refs_1_.5, f32[4,16,128]{2,1,0:T(8,128)} %refs_2_.5, f32[4,16,128]{2,1,0:T(8,128)} %refs_3_.1, f32[4,16,128]{2,1,0:T(8,128)} %refs_4_.1), custom_call_target="tpu_custom_call" | custom-call | tf_op jit(solution)/shard_map/edges/pallas_call | solution.py:380
  2.2 4.2 %collective-permute-start.1 = (f32[5,16,128]{2,1,0:T(8,128)}, f32[5,16,128]{2,1,0:T(8,128)S(1)}, u32[]{:S(2)}, u32[]{:S(2)}) collective-permute-start(f32[5,16,128]{2,1,0:T(8,128)} %get-tuple-element.48), channel_id=1, source_target_pairs={{16,32},{32,16},{48,64},{64,48},{80,96},{96,80},{112,128},{128,112... | collective-permute-start | bytes 122888 | tf_op jit(solution)/shard_map/ppermute | solution.py:390
  6.4 0.9 collective-permute-start
  7.4 0.8 copy.16.shifts_ref.refs_1_
  8.2 0.9 copy-done.2
  9.1 1.0 %collective-permute-done.1.outer_ref = f32[5,16,128]{2,1,0:T(8,128)S(1)} collective-permute-done((f32[5,16,128]{2,1,0:T(8,128)}, f32[5,16,128]{2,1,0:T(8,128)S(1)}, u32[]{:S(2)}, u32[]{:S(2)}) %collective-permute-start.1) | collective-permute-done | bytes 40992 | tf_op jit(solution)/shard_map/ppermute | solution.py:390
  10.1 0.8 widen.1
  10.9 1.6 %collective-permute-start.2 = (f32[25,16,128]{2,1,0:T(8,128)S(1)}, f32[25,16,128]{2,1,0:T(8,128)S(1)}, u32[]{:S(2)}, u32[]{:S(2)}) collective-permute-start(f32[25,16,128]{2,1,0:T(8,128)S(1)} %get-tuple-element.49.own_ref), channel_id=1, source_target_pairs={{0,1},{1,0},{2,3},{3,2},{4,5},{5,4},{6,7},{7,6},{8,9},{9,8},{10,11... | collective-permute-start | bytes 614408 | tf_op jit(solution)/shard_map/ppermute | solution.py:406
  12.5 1.3 %collective-permute-start.4 = (f32[5,8,256]{2,1,0:T(8,128)S(1)}, f32[5,8,256]{2,1,0:T(8,128)S(1)}, u32[]{:S(2)}, u32[]{:S(2)}) collective-permute-start(f32[5,8,256]{2,1,0:T(8,128)S(1)} %get-tuple-element.50), channel_id=1, source_target_pairs={{1,3},{2,0},{3,5},{4,2},{5,7},{6,4},{7,9},{8,6},{9,11},{10,8},{11,... | collective-permute-start | bytes 122888 | tf_op jit(solution)/shard_map/ppermute | solution.py:408
  13.8 0.7 collective-permute-start.3
  14.4 3.9 %collective-permute-done.4.far_ref = f32[5,8,256]{2,1,0:T(8,128)S(1)} collective-permute-done((f32[5,8,256]{2,1,0:T(8,128)S(1)}, f32[5,8,256]{2,1,0:T(8,128)S(1)}, u32[]{:S(2)}, u32[]{:S(2)}) %collective-permute-start.4) | collective-permute-done | bytes 40992 | tf_op jit(solution)/shard_map/ppermute | solution.py:408
  18.4 1.3 %wave.1 = f32[2,18,16,128]{3,2,1,0:T(8,128)S(1)} custom-call(s32[3]{0:T(128)S(1)} %pad_add_fusion.where_ref.refs_0_, f32[25,16,128]{2,1,0:T(8,128)S(1)} %get-tuple-element.49.own_ref, f32[25,16,128]{2,1,0:T(8,128)S(1)} %collective-permute-done.2.other_ref, f32[5,8,256]{2,1,0:T(8,128)S(1)} %collective-permute-done.3.near_ref, ...), custom_call_target="tpu_custom_call" | custom-call | tf_op jit(solution)/shard_map/wave/pallas_call | solution.py:410
  19.7 4.9 %collective-permute-start.6 = (f32[2,18,16,128]{3,2,1,0:T(8,128)S(1)}, f32[2,18,16,128]{3,2,1,0:T(8,128)S(1)}, u32[]{:S(2)}, u32[]{:S(2)}) collective-permute-start(f32[2,18,16,128]{3,2,1,0:T(8,128)S(1)} %wave.1), channel_id=1, source_target_pairs={{0,2},{1,3},{2,4},{3,5},{4,6},{5,7},{6,8},{7,9},{8,10},{9,11},{10,... | collective-permute-start | bytes 884744 | tf_op jit(solution)/shard_map/ppermute | solution.py:438
  24.6 4.9 %collective-permute-start.5 = (f32[2,18,16,128]{3,2,1,0:T(8,128)S(1)}, f32[2,18,16,128]{3,2,1,0:T(8,128)S(1)}, u32[]{:S(2)}, u32[]{:S(2)}) collective-permute-start(f32[2,18,16,128]{3,2,1,0:T(8,128)S(1)} %wave.1), channel_id=1, source_target_pairs={{0,14},{1,15},{2,0},{3,1},{4,2},{5,3},{6,4},{7,5},{8,6},{9,7},{10,... | collective-permute-start | bytes 884744 | tf_op jit(solution)/shard_map/ppermute | solution.py:437
  29.5 2.2 %copy-done = bf16[16,4,256,128]{3,2,1,0:T(8,128)(2,1)S(1)} copy-done((bf16[16,4,256,128]{3,2,1,0:T(8,128)(2,1)S(1)}, bf16[16,4,256,128]{3,2,1,0:T(8,128)(2,1)}, u32[]{:S(2)}) %copy-start) | copy-done | bytes 4194328
  31.7 2.4 %collective-permute-done.6 = f32[2,18,16,128]{3,2,1,0:T(8,128)S(1)} collective-permute-done((f32[2,18,16,128]{3,2,1,0:T(8,128)S(1)}, f32[2,18,16,128]{3,2,1,0:T(8,128)S(1)}, u32[]{:S(2)}, u32[]{:S(2)}) %collective-permute-start.6) | collective-permute-done | bytes 294944 | tf_op jit(solution)/shard_map/ppermute | solution.py:438
  34.1 3.4 %collective-permute-start.7 = (f32[2,18,16,128]{3,2,1,0:T(8,128)S(1)}, f32[2,18,16,128]{3,2,1,0:T(8,128)S(1)}, u32[]{:S(2)}, u32[]{:S(2)}) collective-permute-start(f32[2,18,16,128]{3,2,1,0:T(8,128)S(1)} %collective-permute-done.5), channel_id=1, source_target_pairs={{0,14},{1,15},{2,0},{3,1},{4,2},{5,3},{6,4},{7,5},{8,6},{9,7},{10,... | collective-permute-start | bytes 884744 | tf_op jit(solution)/shard_map/ppermute | solution.py:442
  37.6 6.5 %image.4 = (bf16[16,4,256,128]{3,2,1,0:T(8,128)(2,1)}, f32[4,40,128]{2,1,0:T(8,128)S(1)}, f32[4,40,128]{2,1,0:T(8,128)S(1)}, f32[4,48,128]{2,1,0:T(8,128)S(1)}, ...) custom-call(s32[3]{0:T(128)S(1)} %pad_add_fusion.where_ref.refs_0_, ...), custom_call_target="tpu_custom_call" | custom-call | flops 20000000 | bytes 8000000 | tf_op jit(solution)/shard_map/image/pallas_call | solution.py:474
  44.1 1.3 %collective-permute-done.8 = f32[2,18,16,128]{3,2,1,0:T(8,128)S(1)} collective-permute-done((f32[2,18,16,128]{3,2,1,0:T(8,128)S(1)}, f32[2,18,16,128]{3,2,1,0:T(8,128)S(1)}, u32[]{:S(2)}, u32[]{:S(2)}) %collective-permute-start.8) | collective-permute-done | bytes 294944 | tf_op jit(solution)/shard_map/ppermute | solution.py:443
  45.4 2.0 %collective-permute-start.9 = (f32[2,18,16,128]{3,2,1,0:T(8,128)S(1)}, f32[2,18,16,128]{3,2,1,0:T(8,128)S(1)}, u32[]{:S(2)}, u32[]{:S(2)}) collective-permute-start(f32[2,18,16,128]{3,2,1,0:T(8,128)S(1)} %collective-permute-done.7), channel_id=1, source_target_pairs={{0,14},{1,15},{2,0},{3,1},{4,2},{5,3},{6,4},{7,5},{8,6},{9,7},{10,... | collective-permute-start | bytes 884744 | tf_op jit(solution)/shard_map/ppermute | solution.py:442
  47.5 5.9 %image.5 = (bf16[16,4,256,128]{3,2,1,0:T(8,128)(2,1)}, f32[4,24,128]{2,1,0:T(8,128)S(1)}, f32[4,24,128]{2,1,0:T(8,128)S(1)}, f32[4,40,128]{2,1,0:T(8,128)S(1)}, ...) custom-call(s32[3]{0:T(128)S(1)} %pad_add_fusion.where_ref.refs_0_, ...), custom_call_target="tpu_custom_call", output_to_operand_aliasing={{0}: (11, {})} | custom-call | flops 20000000 | bytes 8000000 | tf_op jit(solution)/shard_map/image/pallas_call | solution.py:474
  53.4 1.9 %collective-permute-done.10 = f32[2,18,16,128]{3,2,1,0:T(8,128)S(1)} collective-permute-done((f32[2,18,16,128]{3,2,1,0:T(8,128)S(1)}, f32[2,18,16,128]{3,2,1,0:T(8,128)S(1)}, u32[]{:S(2)}, u32[]{:S(2)}) %collective-permute-start.10) | collective-permute-done | bytes 294944 | tf_op jit(solution)/shard_map/ppermute | solution.py:443
  55.4 1.4 %collective-permute-start.11 = (f32[18,16,128]{2,1,0:T(8,128)S(1)}, f32[18,16,128]{2,1,0:T(8,128)S(1)}, u32[]{:S(2)}, u32[]{:S(2)}) collective-permute-start(f32[18,16,128]{2,1,0:T(8,128)S(1)} %get-tuple-element.95.refs_5_.refs_3_), channel_id=1, source_target_pairs={{0,14},{1,15},{2,0},{3,1},{4,2},{5,3},{6,4},{7,5},{8,6},{9,7},{10,... | collective-permute-start | bytes 442376 | tf_op jit(solution)/shard_map/ppermute | solution.py:445
  56.7 1.0 collective-permute-start.12
  57.7 5.9 %image.6 = (bf16[16,4,256,128]{3,2,1,0:T(8,128)(2,1)}, f32[4,24,128]{2,1,0:T(8,128)S(1)}, f32[4,24,128]{2,1,0:T(8,128)S(1)}, f32[4,40,128]{2,1,0:T(8,128)S(1)}, ...) custom-call(s32[3]{0:T(128)S(1)} %pad_add_fusion.where_ref.refs_0_, ...), custom_call_target="tpu_custom_call", output_to_operand_aliasing={{0}: (11, {})} | custom-call | flops 20000000 | bytes 8000000 | tf_op jit(solution)/shard_map/image/pallas_call | solution.py:474
  63.7 5.6 %image.7 = (bf16[16,4,256,128]{3,2,1,0:T(8,128)(2,1)}, f32[16,64,128]{2,1,0:T(8,128)S(1)}, f32[64,128]{1,0:T(8,128)S(1)}, f32[64,128]{1,0:T(8,128)S(1)}) custom-call(s32[3]{0:T(128)S(1)} %pad_add_fusion.where_ref.refs_0_, s32[16,2]{1,0:T(8,128)S(1)} %copy.16.shifts_ref.refs_1_, ...), custom_call_target="tpu_custom_call", output_to_operand_aliasing={{0}: (9, {})} | custom-call | flops 20000000 | bytes 8000000 | tf_op jit(solution)/shard_map/image/pallas_call | solution.py:474
  69.3 0.1 collective-permute-start.13
  69.4 5.2 %collective-permute-start.14 = (f32[64,128]{1,0:T(8,128)S(1)}, f32[64,128]{1,0:T(8,128)S(1)}, u32[]{:S(2)}, u32[]{:S(2)}) collective-permute-start(f32[64,128]{1,0:T(8,128)S(1)} %get-tuple-element.91), channel_id=1, source_target_pairs={{16,32},{32,16},{48,64},{64,48},{80,96},{96,80},{112,128},{128,112... | collective-permute-start | bytes 98312 | tf_op jit(solution)/shard_map/ppermute | solution.py:497
  74.6 2.4 %collective-permute-done.14.outer_ref = f32[64,128]{1,0:T(8,128)S(1)} collective-permute-done((f32[64,128]{1,0:T(8,128)S(1)}, f32[64,128]{1,0:T(8,128)S(1)}, u32[]{:S(2)}, u32[]{:S(2)}) %collective-permute-start.14) | collective-permute-done | bytes 32800 | tf_op jit(solution)/shard_map/ppermute | solution.py:497
  77.0 0.9 merge.1
  77.9 24.0 %all_to_all.5.parts_ref = f32[16,64,128]{2,1,0:T(8,128)S(1)} all-to-all(f32[16,64,128]{2,1,0:T(8,128)S(1)} %merge.1), channel_id=1, replica_groups=mesh['space'=16,'offset'=16] {'offset'}, dimensions={0} | all-to-all | bytes 1048576 | tf_op jit(solution)/shard_map/all_to_all | solution.py:504
  101.9 0.6 total.1
  (24 shorter events, 0.3 us)
Async XLA Ops:
  2.2 7.9 %collective-permute-start.1 = (f32[5,16,128]{2,1,0:T(8,128)}, f32[5,16,128]{2,1,0:T(8,128)S(1)}, u32[]{:S(2)}, u32[]{:S(2)}) collective-permute-start(f32[5,16,128]{2,1,0:T(8,128)} %get-tuple-element.48), channel_id=1, source_target_pairs={{16,32},{32,16},{48,64},{64,48},{80,96},{96,80},{112,128},{128,112... | collective-permute-start | bytes 122888 | tf_op jit(solution)/shard_map/ppermute | solution.py:390
  6.4 3.7 %collective-permute-start = (f32[5,16,128]{2,1,0:T(8,128)}, f32[5,16,128]{2,1,0:T(8,128)S(1)}, u32[]{:S(2)}, u32[]{:S(2)}) collective-permute-start(f32[5,16,128]{2,1,0:T(8,128)} %get-tuple-element.48), channel_id=1, source_target_pairs={{0,16},{16,0},{32,48},{48,32},{64,80},{80,64},{96,112},{112,96},{1... | collective-permute-start | bytes 122888 | tf_op jit(solution)/shard_map/ppermute | solution.py:389
  8.2 0.9 copy-start.2
  10.9 7.5 %collective-permute-start.2 = (f32[25,16,128]{2,1,0:T(8,128)S(1)}, f32[25,16,128]{2,1,0:T(8,128)S(1)}, u32[]{:S(2)}, u32[]{:S(2)}) collective-permute-start(f32[25,16,128]{2,1,0:T(8,128)S(1)} %get-tuple-element.49.own_ref), channel_id=1, source_target_pairs={{0,1},{1,0},{2,3},{3,2},{4,5},{5,4},{6,7},{7,6},{8,9},{9,8},{10,11... | collective-permute-start | bytes 614408 | tf_op jit(solution)/shard_map/ppermute | solution.py:406
  12.5 5.9 %collective-permute-start.4 = (f32[5,8,256]{2,1,0:T(8,128)S(1)}, f32[5,8,256]{2,1,0:T(8,128)S(1)}, u32[]{:S(2)}, u32[]{:S(2)}) collective-permute-start(f32[5,8,256]{2,1,0:T(8,128)S(1)} %get-tuple-element.50), channel_id=1, source_target_pairs={{1,3},{2,0},{3,5},{4,2},{5,7},{6,4},{7,9},{8,6},{9,11},{10,8},{11,... | collective-permute-start | bytes 122888 | tf_op jit(solution)/shard_map/ppermute | solution.py:408
  13.8 4.6 %collective-permute-start.3 = (f32[5,8,256]{2,1,0:T(8,128)S(1)}, f32[5,8,256]{2,1,0:T(8,128)S(1)}, u32[]{:S(2)}, u32[]{:S(2)}) collective-permute-start(f32[5,8,256]{2,1,0:T(8,128)S(1)} %get-tuple-element.50), channel_id=1, source_target_pairs={{1,2},{2,1},{3,4},{4,3},{5,6},{6,5},{7,8},{8,7},{9,10},{10,9},{11,... | collective-permute-start | bytes 122888 | tf_op jit(solution)/shard_map/ppermute | solution.py:407
  19.7 14.4 %collective-permute-start.6 = (f32[2,18,16,128]{3,2,1,0:T(8,128)S(1)}, f32[2,18,16,128]{3,2,1,0:T(8,128)S(1)}, u32[]{:S(2)}, u32[]{:S(2)}) collective-permute-start(f32[2,18,16,128]{3,2,1,0:T(8,128)S(1)} %wave.1), channel_id=1, source_target_pairs={{0,2},{1,3},{2,4},{3,5},{4,6},{5,7},{6,8},{7,9},{8,10},{9,11},{10,... | collective-permute-start | bytes 884744 | tf_op jit(solution)/shard_map/ppermute | solution.py:438
  24.6 9.5 %collective-permute-start.5 = (f32[2,18,16,128]{3,2,1,0:T(8,128)S(1)}, f32[2,18,16,128]{3,2,1,0:T(8,128)S(1)}, u32[]{:S(2)}, u32[]{:S(2)}) collective-permute-start(f32[2,18,16,128]{3,2,1,0:T(8,128)S(1)} %wave.1), channel_id=1, source_target_pairs={{0,14},{1,15},{2,0},{3,1},{4,2},{5,3},{6,4},{7,5},{8,6},{9,7},{10,... | collective-permute-start | bytes 884744 | tf_op jit(solution)/shard_map/ppermute | solution.py:437
  29.5 2.2 %copy-start = (bf16[16,4,256,128]{3,2,1,0:T(8,128)(2,1)S(1)}, bf16[16,4,256,128]{3,2,1,0:T(8,128)(2,1)}, u32[]{:S(2)}) copy-start(bf16[16,4,256,128]{3,2,1,0:T(8,128)(2,1)} %refs_2_.9) | copy-start | bytes 12582916
  31.7 5.9 %copy-start.1 = (bf16[16,4,256,128]{3,2,1,0:T(8,128)(2,1)S(1)}, bf16[16,4,256,128]{3,2,1,0:T(8,128)(2,1)}, u32[]{:S(2)}) copy-start(bf16[16,4,256,128]{3,2,1,0:T(8,128)(2,1)} %refs_2_.9) | copy-start | bytes 12582916
  34.1 10.0 %collective-permute-start.7 = (f32[2,18,16,128]{3,2,1,0:T(8,128)S(1)}, f32[2,18,16,128]{3,2,1,0:T(8,128)S(1)}, u32[]{:S(2)}, u32[]{:S(2)}) collective-permute-start(f32[2,18,16,128]{3,2,1,0:T(8,128)S(1)} %collective-permute-done.5), channel_id=1, source_target_pairs={{0,14},{1,15},{2,0},{3,1},{4,2},{5,3},{6,4},{7,5},{8,6},{9,7},{10,... | collective-permute-start | bytes 884744 | tf_op jit(solution)/shard_map/ppermute | solution.py:442
  37.5 7.9 %collective-permute-start.8 = (f32[2,18,16,128]{3,2,1,0:T(8,128)S(1)}, f32[2,18,16,128]{3,2,1,0:T(8,128)S(1)}, u32[]{:S(2)}, u32[]{:S(2)}) collective-permute-start(f32[2,18,16,128]{3,2,1,0:T(8,128)S(1)} %collective-permute-done.6), channel_id=1, source_target_pairs={{0,2},{1,3},{2,4},{3,5},{4,6},{5,7},{6,8},{7,9},{8,10},{9,11},{10,... | collective-permute-start | bytes 884744 | tf_op jit(solution)/shard_map/ppermute | solution.py:443
  45.4 8.0 %collective-permute-start.9 = (f32[2,18,16,128]{3,2,1,0:T(8,128)S(1)}, f32[2,18,16,128]{3,2,1,0:T(8,128)S(1)}, u32[]{:S(2)}, u32[]{:S(2)}) collective-permute-start(f32[2,18,16,128]{3,2,1,0:T(8,128)S(1)} %collective-permute-done.7), channel_id=1, source_target_pairs={{0,14},{1,15},{2,0},{3,1},{4,2},{5,3},{6,4},{7,5},{8,6},{9,7},{10,... | collective-permute-start | bytes 884744 | tf_op jit(solution)/shard_map/ppermute | solution.py:442
  47.4 7.9 %collective-permute-start.10 = (f32[2,18,16,128]{3,2,1,0:T(8,128)S(1)}, f32[2,18,16,128]{3,2,1,0:T(8,128)S(1)}, u32[]{:S(2)}, u32[]{:S(2)}) collective-permute-start(f32[2,18,16,128]{3,2,1,0:T(8,128)S(1)} %collective-permute-done.8), channel_id=1, source_target_pairs={{0,2},{1,3},{2,4},{3,5},{4,6},{5,7},{6,8},{7,9},{8,10},{9,11},{10,... | collective-permute-start | bytes 884744 | tf_op jit(solution)/shard_map/ppermute | solution.py:443
  55.4 8.3 %collective-permute-start.11 = (f32[18,16,128]{2,1,0:T(8,128)S(1)}, f32[18,16,128]{2,1,0:T(8,128)S(1)}, u32[]{:S(2)}, u32[]{:S(2)}) collective-permute-start(f32[18,16,128]{2,1,0:T(8,128)S(1)} %get-tuple-element.95.refs_5_.refs_3_), channel_id=1, source_target_pairs={{0,14},{1,15},{2,0},{3,1},{4,2},{5,3},{6,4},{7,5},{8,6},{9,7},{10,... | collective-permute-start | bytes 442376 | tf_op jit(solution)/shard_map/ppermute | solution.py:445
  56.7 6.9 %collective-permute-start.12 = (f32[18,16,128]{2,1,0:T(8,128)S(1)}, f32[18,16,128]{2,1,0:T(8,128)S(1)}, u32[]{:S(2)}, u32[]{:S(2)}) collective-permute-start(f32[18,16,128]{2,1,0:T(8,128)S(1)} %get-tuple-element.93.refs_8_), channel_id=1, source_target_pairs={{0,2},{1,3},{2,4},{3,5},{4,6},{5,7},{6,8},{7,9},{8,10},{9,11},{10,... | collective-permute-start | bytes 442376 | tf_op jit(solution)/shard_map/ppermute | solution.py:446
  69.3 5.3 %collective-permute-start.13 = (f32[64,128]{1,0:T(8,128)S(1)}, f32[64,128]{1,0:T(8,128)S(1)}, u32[]{:S(2)}, u32[]{:S(2)}) collective-permute-start(f32[64,128]{1,0:T(8,128)S(1)} %get-tuple-element.90), channel_id=1, source_target_pairs={{0,16},{16,0},{32,48},{48,32},{64,80},{80,64},{96,112},{112,96},{1... | collective-permute-start | bytes 98312 | tf_op jit(solution)/shard_map/ppermute | solution.py:496
  69.4 7.6 %collective-permute-start.14 = (f32[64,128]{1,0:T(8,128)S(1)}, f32[64,128]{1,0:T(8,128)S(1)}, u32[]{:S(2)}, u32[]{:S(2)}) collective-permute-start(f32[64,128]{1,0:T(8,128)S(1)} %get-tuple-element.91), channel_id=1, source_target_pairs={{16,32},{32,16},{48,64},{64,48},{80,96},{96,80},{112,128},{128,112... | collective-permute-start | bytes 98312 | tf_op jit(solution)/shard_map/ppermute | solution.py:497

commit v5 on v4

--- a/solution.py
+++ b/solution.py
@@ -12,7 +12,7 @@
 STEPS = 2
 REACH = HMAX + STEPS
 LANES = 128
-UNROLL = 2
+GROUP = 4
 SMALL = pltpu.CompilerParams(vmem_limit_bytes=6 * 2**20)
 
 CALLS = (
@@ -206,7 +206,7 @@
     def put(n, part):
         r, a, m = segments[n]
         at = pl.multiple_of(z_of(r) * rows + a, 8)
-        which = pl.ds(part * (count // 2), count // 2)
+        which = pl.ds(part * GROUP, GROUP)
         return pltpu.make_async_copy(
             images[n].at[which, :, pl.ds(0, m), :],
             image_hbm.at[which, :, pl.ds(at, m), :],
@@ -250,7 +250,7 @@
             at += x.shape[0]
         return out
 
-    def per_offset(o, carry):
+    def per_offset(o):
         hx = shifts_ref[o, 0]
         hy = shifts_ref[o, 1]
         wrap_s = (lane < -hx) | (lane >= LANES - hx)
@@ -266,26 +266,27 @@
             return jnp.where(wrap[:m], sides[n][plane, pl.ds(start, m), :], a)
 
         parts = [(n, z) for n in range(n_seg) for z in range(depth)]
-        sources, receivers = [], []
+        sources, receivers, observed = [], [], []
         for n, z in parts:
+            r, a, m = segments[n]
             for t in range(STEPS):
                 sources.append(piece(n, t * depth + z, s_at, wrap_s))
                 receivers.append(piece(n, (STEPS + t) * depth + z, r_at, wrap_r))
-        sources = rotated(sources, to_s)
-        receivers = rotated(receivers, to_r)
-        terms = []
-        for i, (n, z) in enumerate(parts):
-            r, a, m = segments[n]
+            lead = a % half
+            y_at = pl.multiple_of(z_of(r) * rows + a - lead, half)
+            seen = observed_ref[o, z, pl.ds(y_at, whole_tiles(lead + m)), :]
+            observed.append(seen.astype(jnp.float32)[lead:lead + m])
+        sources = rotated(sources, lax.rem(2 * hx + LANES, LANES))
+        observed = rotated(observed, to_s)
+        fulls, terms = [], []
+        for i in range(len(parts)):
             s1, s2 = sources[2 * i:2 * i + 2]
             r1, r2 = receivers[2 * i:2 * i + 2]
             full = s1 * r1 + s2 * r2
-            images[n][o, z, :m] = full.astype(jnp.bfloat16)
-            lead = a % half
-            y_at = pl.multiple_of(z_of(r) * rows + a - lead, half)
-            observed = observed_ref[o, z, pl.ds(y_at, whole_tiles(lead + m)), :]
-            observed = observed.astype(jnp.float32)[lead:lead + m]
-            terms.append((full - observed) * s2)
-        terms = rotated(terms, to_s)
+            fulls.append(full)
+            terms.append((full - observed[i]) * s2)
+        for (n, z), full in zip(parts, rotated(fulls, to_r)):
+            images[n][o, z, :segments[n][2]] = full.astype(jnp.bfloat16)
         kept = []
         for (n, z), t in zip(parts, terms):
             m = segments[n][2]
@@ -296,12 +297,15 @@
         for n, at, inner, outer in kept:
             sums[n][0][at] = inner
             sums[n][1][at] = outer
-        return carry
-
-    for part in range(2):
-        lax.fori_loop(part * (count // 2), (part + 1) * (count // 2), per_offset, 0, unroll=UNROLL)
+
+    def per_group(part, carry):
+        for k in range(GROUP):
+            per_offset(part * GROUP + k)
         for n in range(n_seg):
             put(n, part).start()
+        return carry
+
+    lax.fori_loop(0, count // GROUP, per_group, 0)
 
     if last:
         all_core, all_side = refs[3 * n_seg + 1:]
@@ -333,7 +337,7 @@
         send_in[...] = jnp.where(even_x, rights, lefts)
         send_out[...] = jnp.where(even_x, lefts, rights)
     for n in range(n_seg):
-        for part in range(2):
+        for part in range(count // GROUP):
             put(n, part).wait()
 
 
@@ -461,7 +465,7 @@
         fields = [pltpu.VMEM((4 * depth, m + 2 * HMAX, LANES), f32) for _, _, m in call]
         scratch = fields + fields
         scratch += [pltpu.VMEM((local, depth, whole_tiles(m), LANES), jnp.bfloat16) for _, _, m in call]
-        scratch += [pltpu.SemaphoreType.DMA((len(call), 2))]
+        scratch += [pltpu.SemaphoreType.DMA((len(call), local // GROUP))]
         if last:
             args += done
             specs += [whole] * len(done)

time: 104 us -> 102 us (0.981); the launches traced: 103 us -> 102 us
  waiting for transfers between devices: 13 us -> 21.4 us
  Pallas kernels: 29.1 us -> 23.3 us
  starting transfers between devices: 31.5 us -> 28.5 us
    pallas_call x4, Pallas kernels: 23.9 us -> 18.1 us  [on_device(): pl.pallas_call(functools.partial(image_kernel, call, first, last), in_spe...]
    ppermute x2, waiting for transfers between devices: 3.24 us -> 7 us  [on_device(): next_down = lax.ppermute(down, 'offset', turn(-1))]
    ppermute x1, starting transfers between devices: 5.21 us -> 1.92 us  [on_device(): got_out = lax.ppermute(send_out, 'space', outer_x)]
    ppermute x1, waiting for transfers between devices: 2.41 us -> 5.7 us  [on_device(): got_out = lax.ppermute(send_out, 'space', outer_x)]
    ppermute x2, waiting for transfers between devices: 0.01 us -> 1.3 us  [on_device(): next_up = lax.ppermute(up, 'offset', turn(1))]
    ppermute x1, starting transfers between devices: 1.36 us -> 0.08 us  [on_device(): next_up = lax.ppermute(up[0], 'offset', turn(1))]
    ppermute x1, starting transfers between devices: 1 us -> 2.26 us  [on_device(): next_down = lax.ppermute(down[1], 'offset', turn(-1))]
  transfers between devices with their start and end apart: 15 -> 15, of which waited for: 6 -> 7; matrix products, arithmetic and copies ran while one was open for 1% -> 1% of each run, Pallas kernels for 18% -> 14%
where the time goes in v5:
time: 102 us
  starting transfers between devices  28.5 us (28%)
  blocking collectives  24 us (24%)
  Pallas kernels  23.3 us (23%)
  waiting for transfers between devices  21.4 us (21%)
  local copies, waits for them, and re-layouts  4.01 us (4%)
    all_to_all x1, blocking collectives, on_device(): parts = lax.all_to_all(parts, 'offset', 0, 0)  24 us
    pallas_call x4, Pallas kernels, on_device(): pl.pallas_call(functools.partial(image_kernel, call, first, last), in_spe...  18.1 us
    ppermute x2, waiting for transfers between devices, on_device(): next_down = lax.ppermute(down, 'offset', turn(-1))  7 us
    ppermute x1, waiting for transfers between devices, on_device(): got_out = lax.ppermute(send_out, 'space', outer_x)  5.7 us
    ppermute x2, starting transfers between devices, on_device(): next_up = lax.ppermute(up, 'offset', turn(1))  5.68 us
    ppermute x1, starting transfers between devices, on_device(): up = lax.ppermute(pair, 'offset', turn(1))  4.92 us
    ppermute x1, starting transfers between devices, on_device(): down = lax.ppermute(pair, 'offset', turn(-1))  4.91 us
    ppermute x1, starting transfers between devices, on_device(): got_out = lax.ppermute(edge, 'space', outer_x)  4.24 us
  transfers between devices with their start and end apart: 15, of which 7 were waited for; matrix products, arithmetic and copies ran while one was open for 1% of the time, Pallas kernels for 14%

profile of v5, /device:TPU:16, one launch (start us, length us, event | category | flops | bytes accessed | tf_op | source)
XLA Modules:
  0.0 102.1 jit_solution(5179320005930162335)
XLA Ops:
  0.6 1.6 %edges.1 = (f32[5,4,16,128]{3,2,1,0:T(8,128)}, f32[5,16,128]{2,1,0:T(8,128)}) custom-call(f32[4,16,128]{2,1,0:T(8,128)} %refs_0_.1, f32[4,16,128]{2,1,0:T(8,128)} %refs_1_.5, f32[4,16,128]{2,1,0:T(8,128)} %refs_2_.5, f32[4,16,128]{2,1,0:T(8,128)} %refs_3_.1, f32[4,16,128]{2,1,0:T(8,128)} %refs_4_.1), custom_call_target="tpu_custom_call" | custom-call | tf_op jit(solution)/shard_map/edges/pallas_call | solution.py:384
  2.2 4.2 %collective-permute-start.1 = (f32[5,16,128]{2,1,0:T(8,128)}, f32[5,16,128]{2,1,0:T(8,128)S(1)}, u32[]{:S(2)}, u32[]{:S(2)}) collective-permute-start(f32[5,16,128]{2,1,0:T(8,128)} %get-tuple-element.48), channel_id=1, source_target_pairs={{16,32},{32,16},{48,64},{64,48},{80,96},{96,80},{112,128},{128,112... | collective-permute-start | bytes 122888 | tf_op jit(solution)/shard_map/ppermute | solution.py:394
  6.4 0.9 collective-permute-start
  7.4 0.8 copy.16.shifts_ref.refs_1_
  8.2 0.9 copy-done.2
  9.1 1.0 %collective-permute-done.1.outer_ref = f32[5,16,128]{2,1,0:T(8,128)S(1)} collective-permute-done((f32[5,16,128]{2,1,0:T(8,128)}, f32[5,16,128]{2,1,0:T(8,128)S(1)}, u32[]{:S(2)}, u32[]{:S(2)}) %collective-permute-start.1) | collective-permute-done | bytes 40992 | tf_op jit(solution)/shard_map/ppermute | solution.py:394
  10.1 0.8 widen.1
  10.9 1.6 %collective-permute-start.2 = (f32[25,16,128]{2,1,0:T(8,128)S(1)}, f32[25,16,128]{2,1,0:T(8,128)S(1)}, u32[]{:S(2)}, u32[]{:S(2)}) collective-permute-start(f32[25,16,128]{2,1,0:T(8,128)S(1)} %get-tuple-element.49.own_ref), channel_id=1, source_target_pairs={{0,1},{1,0},{2,3},{3,2},{4,5},{5,4},{6,7},{7,6},{8,9},{9,8},{10,11... | collective-permute-start | bytes 614408 | tf_op jit(solution)/shard_map/ppermute | solution.py:410
  12.5 1.3 %collective-permute-start.4 = (f32[5,8,256]{2,1,0:T(8,128)S(1)}, f32[5,8,256]{2,1,0:T(8,128)S(1)}, u32[]{:S(2)}, u32[]{:S(2)}) collective-permute-start(f32[5,8,256]{2,1,0:T(8,128)S(1)} %get-tuple-element.50), channel_id=1, source_target_pairs={{1,3},{2,0},{3,5},{4,2},{5,7},{6,4},{7,9},{8,6},{9,11},{10,8},{11,... | collective-permute-start | bytes 122888 | tf_op jit(solution)/shard_map/ppermute | solution.py:412
  13.8 0.7 collective-permute-start.3
  14.4 3.9 %collective-permute-done.4.far_ref = f32[5,8,256]{2,1,0:T(8,128)S(1)} collective-permute-done((f32[5,8,256]{2,1,0:T(8,128)S(1)}, f32[5,8,256]{2,1,0:T(8,128)S(1)}, u32[]{:S(2)}, u32[]{:S(2)}) %collective-permute-start.4) | collective-permute-done | bytes 40992 | tf_op jit(solution)/shard_map/ppermute | solution.py:412
  18.4 1.3 %wave.1 = f32[2,18,16,128]{3,2,1,0:T(8,128)S(1)} custom-call(s32[3]{0:T(128)S(1)} %pad_add_fusion.where_ref.refs_0_, f32[25,16,128]{2,1,0:T(8,128)S(1)} %get-tuple-element.49.own_ref, f32[25,16,128]{2,1,0:T(8,128)S(1)} %collective-permute-done.2.other_ref, f32[5,8,256]{2,1,0:T(8,128)S(1)} %collective-permute-done.3.near_ref, ...), custom_call_target="tpu_custom_call" | custom-call | tf_op jit(solution)/shard_map/wave/pallas_call | solution.py:414
  19.7 4.9 %collective-permute-start.6 = (f32[2,18,16,128]{3,2,1,0:T(8,128)S(1)}, f32[2,18,16,128]{3,2,1,0:T(8,128)S(1)}, u32[]{:S(2)}, u32[]{:S(2)}) collective-permute-start(f32[2,18,16,128]{3,2,1,0:T(8,128)S(1)} %wave.1), channel_id=1, source_target_pairs={{0,2},{1,3},{2,4},{3,5},{4,6},{5,7},{6,8},{7,9},{8,10},{9,11},{10,... | collective-permute-start | bytes 884744 | tf_op jit(solution)/shard_map/ppermute | solution.py:442
  24.6 4.9 %collective-permute-start.5 = (f32[2,18,16,128]{3,2,1,0:T(8,128)S(1)}, f32[2,18,16,128]{3,2,1,0:T(8,128)S(1)}, u32[]{:S(2)}, u32[]{:S(2)}) collective-permute-start(f32[2,18,16,128]{3,2,1,0:T(8,128)S(1)} %wave.1), channel_id=1, source_target_pairs={{0,14},{1,15},{2,0},{3,1},{4,2},{5,3},{6,4},{7,5},{8,6},{9,7},{10,... | collective-permute-start | bytes 884744 | tf_op jit(solution)/shard_map/ppermute | solution.py:441
  29.5 2.2 %copy-done = bf16[16,4,256,128]{3,2,1,0:T(8,128)(2,1)S(1)} copy-done((bf16[16,4,256,128]{3,2,1,0:T(8,128)(2,1)S(1)}, bf16[16,4,256,128]{3,2,1,0:T(8,128)(2,1)}, u32[]{:S(2)}) %copy-start) | copy-done | bytes 4194328
  31.7 2.4 %collective-permute-done.6 = f32[2,18,16,128]{3,2,1,0:T(8,128)S(1)} collective-permute-done((f32[2,18,16,128]{3,2,1,0:T(8,128)S(1)}, f32[2,18,16,128]{3,2,1,0:T(8,128)S(1)}, u32[]{:S(2)}, u32[]{:S(2)}) %collective-permute-start.6) | collective-permute-done | bytes 294944 | tf_op jit(solution)/shard_map/ppermute | solution.py:442
  34.1 3.4 %collective-permute-start.7 = (f32[2,18,16,128]{3,2,1,0:T(8,128)S(1)}, f32[2,18,16,128]{3,2,1,0:T(8,128)S(1)}, u32[]{:S(2)}, u32[]{:S(2)}) collective-permute-start(f32[2,18,16,128]{3,2,1,0:T(8,128)S(1)} %collective-permute-done.5), channel_id=1, source_target_pairs={{0,14},{1,15},{2,0},{3,1},{4,2},{5,3},{6,4},{7,5},{8,6},{9,7},{10,... | collective-permute-start | bytes 884744 | tf_op jit(solution)/shard_map/ppermute | solution.py:446
  37.6 5.0 %image.4 = (bf16[16,4,256,128]{3,2,1,0:T(8,128)(2,1)}, f32[4,40,128]{2,1,0:T(8,128)S(1)}, f32[4,40,128]{2,1,0:T(8,128)S(1)}, f32[4,48,128]{2,1,0:T(8,128)S(1)}, ...) custom-call(s32[3]{0:T(128)S(1)} %pad_add_fusion.where_ref.refs_0_, ...), custom_call_target="tpu_custom_call" | custom-call | flops 20000000 | bytes 8000000 | tf_op jit(solution)/shard_map/image/pallas_call | solution.py:478
  42.6 3.4 %collective-permute-done.8 = f32[2,18,16,128]{3,2,1,0:T(8,128)S(1)} collective-permute-done((f32[2,18,16,128]{3,2,1,0:T(8,128)S(1)}, f32[2,18,16,128]{3,2,1,0:T(8,128)S(1)}, u32[]{:S(2)}, u32[]{:S(2)}) %collective-permute-start.8) | collective-permute-done | bytes 294944 | tf_op jit(solution)/shard_map/ppermute | solution.py:447
  45.9 2.3 %collective-permute-start.9 = (f32[2,18,16,128]{3,2,1,0:T(8,128)S(1)}, f32[2,18,16,128]{3,2,1,0:T(8,128)S(1)}, u32[]{:S(2)}, u32[]{:S(2)}) collective-permute-start(f32[2,18,16,128]{3,2,1,0:T(8,128)S(1)} %collective-permute-done.7), channel_id=1, source_target_pairs={{0,14},{1,15},{2,0},{3,1},{4,2},{5,3},{6,4},{7,5},{8,6},{9,7},{10,... | collective-permute-start | bytes 884744 | tf_op jit(solution)/shard_map/ppermute | solution.py:446
  48.3 4.5 %image.5 = (bf16[16,4,256,128]{3,2,1,0:T(8,128)(2,1)}, f32[4,24,128]{2,1,0:T(8,128)S(1)}, f32[4,24,128]{2,1,0:T(8,128)S(1)}, f32[4,40,128]{2,1,0:T(8,128)S(1)}, ...) custom-call(s32[3]{0:T(128)S(1)} %pad_add_fusion.where_ref.refs_0_, ...), custom_call_target="tpu_custom_call", output_to_operand_aliasing={{0}: (11, {})} | custom-call | flops 20000000 | bytes 8000000 | tf_op jit(solution)/shard_map/image/pallas_call | solution.py:478
  52.8 1.3 %collective-permute-done.9 = f32[2,18,16,128]{3,2,1,0:T(8,128)S(1)} collective-permute-done((f32[2,18,16,128]{3,2,1,0:T(8,128)S(1)}, f32[2,18,16,128]{3,2,1,0:T(8,128)S(1)}, u32[]{:S(2)}, u32[]{:S(2)}) %collective-permute-start.9) | collective-permute-done | bytes 294944 | tf_op jit(solution)/shard_map/ppermute | solution.py:446
  54.1 3.6 %collective-permute-done.10 = f32[2,18,16,128]{3,2,1,0:T(8,128)S(1)} collective-permute-done((f32[2,18,16,128]{3,2,1,0:T(8,128)S(1)}, f32[2,18,16,128]{3,2,1,0:T(8,128)S(1)}, u32[]{:S(2)}, u32[]{:S(2)}) %collective-permute-start.10) | collective-permute-done | bytes 294944 | tf_op jit(solution)/shard_map/ppermute | solution.py:447
  57.9 2.3 %collective-permute-start.12 = (f32[18,16,128]{2,1,0:T(8,128)S(1)}, f32[18,16,128]{2,1,0:T(8,128)S(1)}, u32[]{:S(2)}, u32[]{:S(2)}) collective-permute-start(f32[18,16,128]{2,1,0:T(8,128)S(1)} %get-tuple-element.93.refs_8_), channel_id=1, source_target_pairs={{0,2},{1,3},{2,4},{3,5},{4,6},{5,7},{6,8},{7,9},{8,10},{9,11},{10,... | collective-permute-start | bytes 442376 | tf_op jit(solution)/shard_map/ppermute | solution.py:450
  60.2 4.5 %image.6 = (bf16[16,4,256,128]{3,2,1,0:T(8,128)(2,1)}, f32[4,24,128]{2,1,0:T(8,128)S(1)}, f32[4,24,128]{2,1,0:T(8,128)S(1)}, f32[4,40,128]{2,1,0:T(8,128)S(1)}, ...) custom-call(s32[3]{0:T(128)S(1)} %pad_add_fusion.where_ref.refs_0_, ...), custom_call_target="tpu_custom_call", output_to_operand_aliasing={{0}: (11, {})} | custom-call | flops 20000000 | bytes 8000000 | tf_op jit(solution)/shard_map/image/pallas_call | solution.py:478
  64.7 4.1 %image.7 = (bf16[16,4,256,128]{3,2,1,0:T(8,128)(2,1)}, f32[16,64,128]{2,1,0:T(8,128)S(1)}, f32[64,128]{1,0:T(8,128)S(1)}, f32[64,128]{1,0:T(8,128)S(1)}) custom-call(s32[3]{0:T(128)S(1)} %pad_add_fusion.where_ref.refs_0_, s32[16,2]{1,0:T(8,128)S(1)} %copy.16.shifts_ref.refs_1_, ...), custom_call_target="tpu_custom_call", output_to_operand_aliasing={{0}: (9, {})} | custom-call | flops 20000000 | bytes 8000000 | tf_op jit(solution)/shard_map/image/pallas_call | solution.py:478
  68.8 0.1 collective-permute-start.13
  68.9 1.9 %collective-permute-start.14 = (f32[64,128]{1,0:T(8,128)S(1)}, f32[64,128]{1,0:T(8,128)S(1)}, u32[]{:S(2)}, u32[]{:S(2)}) collective-permute-start(f32[64,128]{1,0:T(8,128)S(1)} %get-tuple-element.91), channel_id=1, source_target_pairs={{16,32},{32,16},{48,64},{64,48},{80,96},{96,80},{112,128},{128,112... | collective-permute-start | bytes 98312 | tf_op jit(solution)/shard_map/ppermute | solution.py:501
  70.9 5.7 %collective-permute-done.14.outer_ref = f32[64,128]{1,0:T(8,128)S(1)} collective-permute-done((f32[64,128]{1,0:T(8,128)S(1)}, f32[64,128]{1,0:T(8,128)S(1)}, u32[]{:S(2)}, u32[]{:S(2)}) %collective-permute-start.14) | collective-permute-done | bytes 32800 | tf_op jit(solution)/shard_map/ppermute | solution.py:501
  76.6 0.9 merge.1
  77.4 24.0 %all_to_all.5.parts_ref = f32[16,64,128]{2,1,0:T(8,128)S(1)} all-to-all(f32[16,64,128]{2,1,0:T(8,128)S(1)} %merge.1), channel_id=1, replica_groups=mesh['space'=16,'offset'=16] {'offset'}, dimensions={0} | all-to-all | bytes 1048576 | tf_op jit(solution)/shard_map/all_to_all | solution.py:508
  101.5 0.6 total.1
  (24 shorter events, 0.3 us)
Async XLA Ops:
  2.2 7.9 %collective-permute-start.1 = (f32[5,16,128]{2,1,0:T(8,128)}, f32[5,16,128]{2,1,0:T(8,128)S(1)}, u32[]{:S(2)}, u32[]{:S(2)}) collective-permute-start(f32[5,16,128]{2,1,0:T(8,128)} %get-tuple-element.48), channel_id=1, source_target_pairs={{16,32},{32,16},{48,64},{64,48},{80,96},{96,80},{112,128},{128,112... | collective-permute-start | bytes 122888 | tf_op jit(solution)/shard_map/ppermute | solution.py:394
  6.4 3.7 %collective-permute-start = (f32[5,16,128]{2,1,0:T(8,128)}, f32[5,16,128]{2,1,0:T(8,128)S(1)}, u32[]{:S(2)}, u32[]{:S(2)}) collective-permute-start(f32[5,16,128]{2,1,0:T(8,128)} %get-tuple-element.48), channel_id=1, source_target_pairs={{0,16},{16,0},{32,48},{48,32},{64,80},{80,64},{96,112},{112,96},{1... | collective-permute-start | bytes 122888 | tf_op jit(solution)/shard_map/ppermute | solution.py:393
  8.2 0.9 copy-start.2
  10.9 7.5 %collective-permute-start.2 = (f32[25,16,128]{2,1,0:T(8,128)S(1)}, f32[25,16,128]{2,1,0:T(8,128)S(1)}, u32[]{:S(2)}, u32[]{:S(2)}) collective-permute-start(f32[25,16,128]{2,1,0:T(8,128)S(1)} %get-tuple-element.49.own_ref), channel_id=1, source_target_pairs={{0,1},{1,0},{2,3},{3,2},{4,5},{5,4},{6,7},{7,6},{8,9},{9,8},{10,11... | collective-permute-start | bytes 614408 | tf_op jit(solution)/shard_map/ppermute | solution.py:410
  12.5 5.9 %collective-permute-start.4 = (f32[5,8,256]{2,1,0:T(8,128)S(1)}, f32[5,8,256]{2,1,0:T(8,128)S(1)}, u32[]{:S(2)}, u32[]{:S(2)}) collective-permute-start(f32[5,8,256]{2,1,0:T(8,128)S(1)} %get-tuple-element.50), channel_id=1, source_target_pairs={{1,3},{2,0},{3,5},{4,2},{5,7},{6,4},{7,9},{8,6},{9,11},{10,8},{11,... | collective-permute-start | bytes 122888 | tf_op jit(solution)/shard_map/ppermute | solution.py:412
  13.8 4.6 %collective-permute-start.3 = (f32[5,8,256]{2,1,0:T(8,128)S(1)}, f32[5,8,256]{2,1,0:T(8,128)S(1)}, u32[]{:S(2)}, u32[]{:S(2)}) collective-permute-start(f32[5,8,256]{2,1,0:T(8,128)S(1)} %get-tuple-element.50), channel_id=1, source_target_pairs={{1,2},{2,1},{3,4},{4,3},{5,6},{6,5},{7,8},{8,7},{9,10},{10,9},{11,... | collective-permute-start | bytes 122888 | tf_op jit(solution)/shard_map/ppermute | solution.py:411
  19.7 14.4 %collective-permute-start.6 = (f32[2,18,16,128]{3,2,1,0:T(8,128)S(1)}, f32[2,18,16,128]{3,2,1,0:T(8,128)S(1)}, u32[]{:S(2)}, u32[]{:S(2)}) collective-permute-start(f32[2,18,16,128]{3,2,1,0:T(8,128)S(1)} %wave.1), channel_id=1, source_target_pairs={{0,2},{1,3},{2,4},{3,5},{4,6},{5,7},{6,8},{7,9},{8,10},{9,11},{10,... | collective-permute-start | bytes 884744 | tf_op jit(solution)/shard_map/ppermute | solution.py:442
  24.6 9.5 %collective-permute-start.5 = (f32[2,18,16,128]{3,2,1,0:T(8,128)S(1)}, f32[2,18,16,128]{3,2,1,0:T(8,128)S(1)}, u32[]{:S(2)}, u32[]{:S(2)}) collective-permute-start(f32[2,18,16,128]{3,2,1,0:T(8,128)S(1)} %wave.1), channel_id=1, source_target_pairs={{0,14},{1,15},{2,0},{3,1},{4,2},{5,3},{6,4},{7,5},{8,6},{9,7},{10,... | collective-permute-start | bytes 884744 | tf_op jit(solution)/shard_map/ppermute | solution.py:441
  29.5 2.2 %copy-start = (bf16[16,4,256,128]{3,2,1,0:T(8,128)(2,1)S(1)}, bf16[16,4,256,128]{3,2,1,0:T(8,128)(2,1)}, u32[]{:S(2)}) copy-start(bf16[16,4,256,128]{3,2,1,0:T(8,128)(2,1)} %refs_2_.9) | copy-start | bytes 12582916
  31.7 5.9 %copy-start.1 = (bf16[16,4,256,128]{3,2,1,0:T(8,128)(2,1)S(1)}, bf16[16,4,256,128]{3,2,1,0:T(8,128)(2,1)}, u32[]{:S(2)}) copy-start(bf16[16,4,256,128]{3,2,1,0:T(8,128)(2,1)} %refs_2_.9) | copy-start | bytes 12582916
  34.1 8.4 %collective-permute-start.7 = (f32[2,18,16,128]{3,2,1,0:T(8,128)S(1)}, f32[2,18,16,128]{3,2,1,0:T(8,128)S(1)}, u32[]{:S(2)}, u32[]{:S(2)}) collective-permute-start(f32[2,18,16,128]{3,2,1,0:T(8,128)S(1)} %collective-permute-done.5), channel_id=1, source_target_pairs={{0,14},{1,15},{2,0},{3,1},{4,2},{5,3},{6,4},{7,5},{8,6},{9,7},{10,... | collective-permute-start | bytes 884744 | tf_op jit(solution)/shard_map/ppermute | solution.py:446
  37.5 8.4 %collective-permute-start.8 = (f32[2,18,16,128]{3,2,1,0:T(8,128)S(1)}, f32[2,18,16,128]{3,2,1,0:T(8,128)S(1)}, u32[]{:S(2)}, u32[]{:S(2)}) collective-permute-start(f32[2,18,16,128]{3,2,1,0:T(8,128)S(1)} %collective-permute-done.6), channel_id=1, source_target_pairs={{0,2},{1,3},{2,4},{3,5},{4,6},{5,7},{6,8},{7,9},{8,10},{9,11},{10,... | collective-permute-start | bytes 884744 | tf_op jit(solution)/shard_map/ppermute | solution.py:447
  45.9 8.2 %collective-permute-start.9 = (f32[2,18,16,128]{3,2,1,0:T(8,128)S(1)}, f32[2,18,16,128]{3,2,1,0:T(8,128)S(1)}, u32[]{:S(2)}, u32[]{:S(2)}) collective-permute-start(f32[2,18,16,128]{3,2,1,0:T(8,128)S(1)} %collective-permute-done.7), channel_id=1, source_target_pairs={{0,14},{1,15},{2,0},{3,1},{4,2},{5,3},{6,4},{7,5},{8,6},{9,7},{10,... | collective-permute-start | bytes 884744 | tf_op jit(solution)/shard_map/ppermute | solution.py:446
  48.2 9.5 %collective-permute-start.10 = (f32[2,18,16,128]{3,2,1,0:T(8,128)S(1)}, f32[2,18,16,128]{3,2,1,0:T(8,128)S(1)}, u32[]{:S(2)}, u32[]{:S(2)}) collective-permute-start(f32[2,18,16,128]{3,2,1,0:T(8,128)S(1)} %collective-permute-done.8), channel_id=1, source_target_pairs={{0,2},{1,3},{2,4},{3,5},{4,6},{5,7},{6,8},{7,9},{8,10},{9,11},{10,... | collective-permute-start | bytes 884744 | tf_op jit(solution)/shard_map/ppermute | solution.py:447
  57.8 6.9 %collective-permute-start.11 = (f32[18,16,128]{2,1,0:T(8,128)S(1)}, f32[18,16,128]{2,1,0:T(8,128)S(1)}, u32[]{:S(2)}, u32[]{:S(2)}) collective-permute-start(f32[18,16,128]{2,1,0:T(8,128)S(1)} %get-tuple-element.95.refs_5_.refs_3_), channel_id=1, source_target_pairs={{0,14},{1,15},{2,0},{3,1},{4,2},{5,3},{6,4},{7,5},{8,6},{9,7},{10,... | collective-permute-start | bytes 442376 | tf_op jit(solution)/shard_map/ppermute | solution.py:449
  57.9 6.8 %collective-permute-start.12 = (f32[18,16,128]{2,1,0:T(8,128)S(1)}, f32[18,16,128]{2,1,0:T(8,128)S(1)}, u32[]{:S(2)}, u32[]{:S(2)}) collective-permute-start(f32[18,16,128]{2,1,0:T(8,128)S(1)} %get-tuple-element.93.refs_8_), channel_id=1, source_target_pairs={{0,2},{1,3},{2,4},{3,5},{4,6},{5,7},{6,8},{7,9},{8,10},{9,11},{10,... | collective-permute-start | bytes 442376 | tf_op jit(solution)/shard_map/ppermute | solution.py:450
  68.8 2.0 %collective-permute-start.13 = (f32[64,128]{1,0:T(8,128)S(1)}, f32[64,128]{1,0:T(8,128)S(1)}, u32[]{:S(2)}, u32[]{:S(2)}) collective-permute-start(f32[64,128]{1,0:T(8,128)S(1)} %get-tuple-element.90), channel_id=1, source_target_pairs={{0,16},{16,0},{32,48},{48,32},{64,80},{80,64},{96,112},{112,96},{1... | collective-permute-start | bytes 98312 | tf_op jit(solution)/shard_map/ppermute | solution.py:500
  68.9 7.6 %collective-permute-start.14 = (f32[64,128]{1,0:T(8,128)S(1)}, f32[64,128]{1,0:T(8,128)S(1)}, u32[]{:S(2)}, u32[]{:S(2)}) collective-permute-start(f32[64,128]{1,0:T(8,128)S(1)} %get-tuple-element.91), channel_id=1, source_target_pairs={{16,32},{32,16},{48,64},{64,48},{80,96},{96,80},{112,128},{128,112... | collective-permute-start | bytes 98312 | tf_op jit(solution)/shard_map/ppermute | solution.py:501

commit v6 on v5

--- a/solution.py
+++ b/solution.py
@@ -12,7 +12,7 @@
 STEPS = 2
 REACH = HMAX + STEPS
 LANES = 128
-GROUP = 4
+GROUP = 8
 SMALL = pltpu.CompilerParams(vmem_limit_bytes=6 * 2**20)
 
 CALLS = (
@@ -59,7 +59,7 @@
     out_ref[...] = ref[...]
 
 
-def touch_kernel(ref, out_ref):
+def touch_kernel(shifts_ref, ref, out_ref):
     out_ref[...] = ref[0, 0, :8, :].astype(jnp.float32)
 
 
@@ -69,7 +69,7 @@
     return jnp.where(lane < REACH, roll_lanes(packed, -32 * z), beside)
 
 
-def widen_kernel(where_ref, shifts_ref, raw_ref, inner_ref, outer_ref, own_ref, line_ref):
+def widen_kernel(where_ref, raw_ref, inner_ref, outer_ref, own_ref, line_ref):
     fields, depth, rows, cols = raw_ref.shape
     lane = lax.broadcasted_iota(jnp.int32, (fields * rows, LANES), 1)
     row = lax.broadcasted_iota(jnp.int32, (8, 2 * LANES), 0)
@@ -85,14 +85,19 @@
         for z in range(depth):
             own_ref[f * depth + z] = raw_ref[f, z]
     lines = [jnp.zeros((8, 2 * LANES), jnp.float32) for _ in range(fields)]
+    first = jnp.concatenate([packed[f * rows:f * rows + 8] for f in range(fields)], axis=0)
+    last = jnp.concatenate([packed[(f + 1) * rows - 8:(f + 1) * rows] for f in range(fields)], axis=0)
+    packed = jnp.where(even_y, first, last)
     for z in range(depth):
         beside = spread(packed, z)
         here = (row >= 2 * z) & (row < 2 * z + 2)
+        to = jnp.where(even_y, 2 * z, (2 * z + 2) % 8)
+        both = []
         for f in range(fields):
-            both = jnp.concatenate([raw_ref[f, z], beside[f * rows:(f + 1) * rows]], axis=1)
-            upper = pltpu.roll(both[:8], 2 * z, 0)
-            lower = pltpu.roll(both[rows - 8:], (2 * z + 2) % 8, 0)
-            lines[f] = jnp.where(here, jnp.where(even_y, upper, lower), lines[f])
+            edge = jnp.where(even_y, raw_ref[f, z, :8], raw_ref[f, z, rows - 8:])
+            both.append(jnp.concatenate([edge, beside[8 * f:8 * f + 8]], axis=1))
+        for f in range(fields):
+            lines[f] = jnp.where(here, pltpu.roll(both[f], to, 0), lines[f])
     for f in range(fields):
         line_ref[f] = lines[f]
 
@@ -347,12 +352,13 @@
     even_x = where_ref[1] == 0
     from_right = jnp.where(even_x, inner_ref[...], outer_ref[...])
     from_left = jnp.where(even_x, outer_ref[...], inner_ref[...])
+    both = jnp.concatenate([from_left, roll_lanes(from_right, LANES - HMAX)], axis=0)
     lane = lax.broadcasted_iota(jnp.int32, (cut, LANES), 1)
     for group in range(2):
         for q in range(8):
-            slot = 16 * q + HMAX * group
-            extra = jnp.where(lane < HMAX, roll_lanes(from_left, -slot), 0.0)
-            extra = jnp.where(lane >= LANES - HMAX, roll_lanes(from_right, 120 - slot), extra)
+            turned = roll_lanes(both, -(16 * q + HMAX * group))
+            extra = jnp.where(lane < HMAX, turned[:cut], 0.0)
+            extra = jnp.where(lane >= LANES - HMAX, turned[cut:], extra)
             at = (q % 4) * 16 + (q // 4) * 8
             for i in range(n_tiles // 2):
                 tile = group * (n_tiles // 2) + i
@@ -403,10 +409,10 @@
     )(raw)
     own, line = pl.pallas_call(
         widen_kernel,
-        in_specs=[scalars] * 2 + [whole] * 3,
+        in_specs=[scalars] + [whole] * 3,
         out_shape=[shape((5 * depth + 5, rows, cols), f32), shape((5, 8, 2 * LANES), f32)],
         name="widen", compiler_params=SMALL,
-    )(where, shift_table, raw, got_in, got_out)
+    )(where, raw, got_in, got_out)
     other = lax.ppermute(own, "offset", inner_y)
     near = lax.ppermute(line, "offset", outer_y)
     far = lax.ppermute(line, "offset", same_y)
@@ -424,13 +430,13 @@
     tiles = [(pair[0], pair[1])] + [None] * 7
     touched = pl.pallas_call(
         touch_kernel,
-        in_specs=[whole],
+        in_specs=[scalars, whole],
         out_specs=whole,
         out_shape=shape((8, LANES), f32),
         compiler_params=SMALL,
         cost_estimate=pl.CostEstimate(flops=0, bytes_accessed=8_000_000, transcendentals=0),
         name="touch",
-    )(ref_image)
+    )(shift_table, ref_image)
     local = shift_table.shape[0]
     image = None
     done = []

time: 102 us -> 102 us (level)
    ppermute x1, waiting for transfers between devices: 2.42 us -> 0.99 us  [on_device(): down = lax.ppermute(pair, 'offset', turn(-1))]
where the time goes in v6:
time: 102 us
  starting transfers between devices  28.5 us (28%)
  blocking collectives  24 us (24%)
  Pallas kernels  23.5 us (23%)
  waiting for transfers between devices  20.9 us (20%)
  local copies, waits for them, and re-layouts  4.01 us (4%)
    all_to_all x1, blocking collectives, on_device(): parts = lax.all_to_all(parts, 'offset', 0, 0)  24 us
    pallas_call x4, Pallas kernels, on_device(): pl.pallas_call(functools.partial(image_kernel, call, first, last), in_spe...  17.8 us
    ppermute x2, waiting for transfers between devices, on_device(): next_down = lax.ppermute(down, 'offset', turn(-1))  6.99 us
    ppermute x1, waiting for transfers between devices, on_device(): got_out = lax.ppermute(send_out, 'space', outer_x)  5.7 us
    ppermute x2, starting transfers between devices, on_device(): next_up = lax.ppermute(up, 'offset', turn(1))  5.63 us
    ppermute x1, starting transfers between devices, on_device(): up = lax.ppermute(pair, 'offset', turn(1))  4.92 us
    ppermute x1, starting transfers between devices, on_device(): down = lax.ppermute(pair, 'offset', turn(-1))  4.91 us
    ppermute x1, starting transfers between devices, on_device(): got_out = lax.ppermute(edge, 'space', outer_x)  4.24 us
  transfers between devices with their start and end apart: 15, of which 7 were waited for; matrix products, arithmetic and copies ran while one was open for 1% of the time, Pallas kernels for 14%

profile of v6, /device:TPU:16, one launch (start us, length us, event | category | flops | bytes accessed | tf_op | source)
XLA Modules:
  0.0 101.8 jit_solution(7046297586427120128)
XLA Ops:
  0.6 1.6 %edges.1 = (f32[5,4,16,128]{3,2,1,0:T(8,128)}, f32[5,16,128]{2,1,0:T(8,128)}) custom-call(f32[4,16,128]{2,1,0:T(8,128)} %refs_0_.1, f32[4,16,128]{2,1,0:T(8,128)} %refs_1_.5, f32[4,16,128]{2,1,0:T(8,128)} %refs_2_.5, f32[4,16,128]{2,1,0:T(8,128)} %refs_3_.1, f32[4,16,128]{2,1,0:T(8,128)} %refs_4_.1), custom_call_target="tpu_custom_call" | custom-call | tf_op jit(solution)/shard_map/edges/pallas_call | solution.py:390
  2.2 4.2 %collective-permute-start.1 = (f32[5,16,128]{2,1,0:T(8,128)}, f32[5,16,128]{2,1,0:T(8,128)S(1)}, u32[]{:S(2)}, u32[]{:S(2)}) collective-permute-start(f32[5,16,128]{2,1,0:T(8,128)} %get-tuple-element.48), channel_id=1, source_target_pairs={{16,32},{32,16},{48,64},{64,48},{80,96},{96,80},{112,128},{128,112... | collective-permute-start | bytes 122888 | tf_op jit(solution)/shard_map/ppermute | solution.py:400
  6.4 0.9 collective-permute-start
  7.4 0.9 copy-done.2
  8.3 1.8 %collective-permute-done.1.outer_ref = f32[5,16,128]{2,1,0:T(8,128)S(1)} collective-permute-done((f32[5,16,128]{2,1,0:T(8,128)}, f32[5,16,128]{2,1,0:T(8,128)S(1)}, u32[]{:S(2)}, u32[]{:S(2)}) %collective-permute-start.1) | collective-permute-done | bytes 40992 | tf_op jit(solution)/shard_map/ppermute | solution.py:400
  10.1 0.6 widen.1
  10.8 1.6 %collective-permute-start.2 = (f32[25,16,128]{2,1,0:T(8,128)S(1)}, f32[25,16,128]{2,1,0:T(8,128)S(1)}, u32[]{:S(2)}, u32[]{:S(2)}) collective-permute-start(f32[25,16,128]{2,1,0:T(8,128)S(1)} %get-tuple-element.49.own_ref), channel_id=1, source_target_pairs={{0,1},{1,0},{2,3},{3,2},{4,5},{5,4},{6,7},{7,6},{8,9},{9,8},{10,11... | collective-permute-start | bytes 614408 | tf_op jit(solution)/shard_map/ppermute | solution.py:416
  12.3 1.3 %collective-permute-start.4 = (f32[5,8,256]{2,1,0:T(8,128)S(1)}, f32[5,8,256]{2,1,0:T(8,128)S(1)}, u32[]{:S(2)}, u32[]{:S(2)}) collective-permute-start(f32[5,8,256]{2,1,0:T(8,128)S(1)} %get-tuple-element.50), channel_id=1, source_target_pairs={{1,3},{2,0},{3,5},{4,2},{5,7},{6,4},{7,9},{8,6},{9,11},{10,8},{11,... | collective-permute-start | bytes 122888 | tf_op jit(solution)/shard_map/ppermute | solution.py:418
  13.6 0.7 collective-permute-start.3
  14.3 3.9 %collective-permute-done.4.far_ref = f32[5,8,256]{2,1,0:T(8,128)S(1)} collective-permute-done((f32[5,8,256]{2,1,0:T(8,128)S(1)}, f32[5,8,256]{2,1,0:T(8,128)S(1)}, u32[]{:S(2)}, u32[]{:S(2)}) %collective-permute-start.4) | collective-permute-done | bytes 40992 | tf_op jit(solution)/shard_map/ppermute | solution.py:418
  18.2 1.3 %wave.1 = f32[2,18,16,128]{3,2,1,0:T(8,128)S(1)} custom-call(s32[3]{0:T(128)S(1)} %pad_add_fusion.where_ref.refs_0_, f32[25,16,128]{2,1,0:T(8,128)S(1)} %get-tuple-element.49.own_ref, f32[25,16,128]{2,1,0:T(8,128)S(1)} %collective-permute-done.2.other_ref, f32[5,8,256]{2,1,0:T(8,128)S(1)} %collective-permute-done.3.near_ref, ...), custom_call_target="tpu_custom_call" | custom-call | tf_op jit(solution)/shard_map/wave/pallas_call | solution.py:420
  19.5 4.9 %collective-permute-start.6 = (f32[2,18,16,128]{3,2,1,0:T(8,128)S(1)}, f32[2,18,16,128]{3,2,1,0:T(8,128)S(1)}, u32[]{:S(2)}, u32[]{:S(2)}) collective-permute-start(f32[2,18,16,128]{3,2,1,0:T(8,128)S(1)} %wave.1), channel_id=1, source_target_pairs={{0,2},{1,3},{2,4},{3,5},{4,6},{5,7},{6,8},{7,9},{8,10},{9,11},{10,... | collective-permute-start | bytes 884744 | tf_op jit(solution)/shard_map/ppermute | solution.py:448
  24.4 4.9 %collective-permute-start.5 = (f32[2,18,16,128]{3,2,1,0:T(8,128)S(1)}, f32[2,18,16,128]{3,2,1,0:T(8,128)S(1)}, u32[]{:S(2)}, u32[]{:S(2)}) collective-permute-start(f32[2,18,16,128]{3,2,1,0:T(8,128)S(1)} %wave.1), channel_id=1, source_target_pairs={{0,14},{1,15},{2,0},{3,1},{4,2},{5,3},{6,4},{7,5},{8,6},{9,7},{10,... | collective-permute-start | bytes 884744 | tf_op jit(solution)/shard_map/ppermute | solution.py:447
  29.4 0.8 copy.16.shifts_ref.refs_1_
  30.1 2.2 %copy-done = bf16[16,4,256,128]{3,2,1,0:T(8,128)(2,1)S(1)} copy-done((bf16[16,4,256,128]{3,2,1,0:T(8,128)(2,1)S(1)}, bf16[16,4,256,128]{3,2,1,0:T(8,128)(2,1)}, u32[]{:S(2)}) %copy-start) | copy-done | bytes 4194328
  32.3 0.7 touch.1.refs_3_
  33.0 1.0 collective-permute-done.6
  34.0 3.4 %collective-permute-start.7 = (f32[2,18,16,128]{3,2,1,0:T(8,128)S(1)}, f32[2,18,16,128]{3,2,1,0:T(8,128)S(1)}, u32[]{:S(2)}, u32[]{:S(2)}) collective-permute-start(f32[2,18,16,128]{3,2,1,0:T(8,128)S(1)} %collective-permute-done.5), channel_id=1, source_target_pairs={{0,14},{1,15},{2,0},{3,1},{4,2},{5,3},{6,4},{7,5},{8,6},{9,7},{10,... | collective-permute-start | bytes 884744 | tf_op jit(solution)/shard_map/ppermute | solution.py:452
  37.4 4.9 %image.4 = (bf16[16,4,256,128]{3,2,1,0:T(8,128)(2,1)}, f32[4,40,128]{2,1,0:T(8,128)S(1)}, f32[4,40,128]{2,1,0:T(8,128)S(1)}, f32[4,48,128]{2,1,0:T(8,128)S(1)}, ...) custom-call(s32[3]{0:T(128)S(1)} %pad_add_fusion.where_ref.refs_0_, ...), custom_call_target="tpu_custom_call" | custom-call | flops 20000000 | bytes 8000000 | tf_op jit(solution)/shard_map/image/pallas_call | solution.py:484
  42.4 3.5 %collective-permute-done.8 = f32[2,18,16,128]{3,2,1,0:T(8,128)S(1)} collective-permute-done((f32[2,18,16,128]{3,2,1,0:T(8,128)S(1)}, f32[2,18,16,128]{3,2,1,0:T(8,128)S(1)}, u32[]{:S(2)}, u32[]{:S(2)}) %collective-permute-start.8) | collective-permute-done | bytes 294944 | tf_op jit(solution)/shard_map/ppermute | solution.py:453
  45.8 2.3 %collective-permute-start.9 = (f32[2,18,16,128]{3,2,1,0:T(8,128)S(1)}, f32[2,18,16,128]{3,2,1,0:T(8,128)S(1)}, u32[]{:S(2)}, u32[]{:S(2)}) collective-permute-start(f32[2,18,16,128]{3,2,1,0:T(8,128)S(1)} %collective-permute-done.7), channel_id=1, source_target_pairs={{0,14},{1,15},{2,0},{3,1},{4,2},{5,3},{6,4},{7,5},{8,6},{9,7},{10,... | collective-permute-start | bytes 884744 | tf_op jit(solution)/shard_map/ppermute | solution.py:452
  48.2 4.4 %image.5 = (bf16[16,4,256,128]{3,2,1,0:T(8,128)(2,1)}, f32[4,24,128]{2,1,0:T(8,128)S(1)}, f32[4,24,128]{2,1,0:T(8,128)S(1)}, f32[4,40,128]{2,1,0:T(8,128)S(1)}, ...) custom-call(s32[3]{0:T(128)S(1)} %pad_add_fusion.where_ref.refs_0_, ...), custom_call_target="tpu_custom_call", output_to_operand_aliasing={{0}: (11, {})} | custom-call | flops 20000000 | bytes 8000000 | tf_op jit(solution)/shard_map/image/pallas_call | solution.py:484
  52.6 1.5 %collective-permute-done.9 = f32[2,18,16,128]{3,2,1,0:T(8,128)S(1)} collective-permute-done((f32[2,18,16,128]{3,2,1,0:T(8,128)S(1)}, f32[2,18,16,128]{3,2,1,0:T(8,128)S(1)}, u32[]{:S(2)}, u32[]{:S(2)}) %collective-permute-start.9) | collective-permute-done | bytes 294944 | tf_op jit(solution)/shard_map/ppermute | solution.py:452
  54.1 3.5 %collective-permute-done.10 = f32[2,18,16,128]{3,2,1,0:T(8,128)S(1)} collective-permute-done((f32[2,18,16,128]{3,2,1,0:T(8,128)S(1)}, f32[2,18,16,128]{3,2,1,0:T(8,128)S(1)}, u32[]{:S(2)}, u32[]{:S(2)}) %collective-permute-start.10) | collective-permute-done | bytes 294944 | tf_op jit(solution)/shard_map/ppermute | solution.py:453
  57.8 2.3 %collective-permute-start.12 = (f32[18,16,128]{2,1,0:T(8,128)S(1)}, f32[18,16,128]{2,1,0:T(8,128)S(1)}, u32[]{:S(2)}, u32[]{:S(2)}) collective-permute-start(f32[18,16,128]{2,1,0:T(8,128)S(1)} %get-tuple-element.93.refs_8_), channel_id=1, source_target_pairs={{0,2},{1,3},{2,4},{3,5},{4,6},{5,7},{6,8},{7,9},{8,10},{9,11},{10,... | collective-permute-start | bytes 442376 | tf_op jit(solution)/shard_map/ppermute | solution.py:456
  60.0 4.4 %image.6 = (bf16[16,4,256,128]{3,2,1,0:T(8,128)(2,1)}, f32[4,24,128]{2,1,0:T(8,128)S(1)}, f32[4,24,128]{2,1,0:T(8,128)S(1)}, f32[4,40,128]{2,1,0:T(8,128)S(1)}, ...) custom-call(s32[3]{0:T(128)S(1)} %pad_add_fusion.where_ref.refs_0_, ...), custom_call_target="tpu_custom_call", output_to_operand_aliasing={{0}: (11, {})} | custom-call | flops 20000000 | bytes 8000000 | tf_op jit(solution)/shard_map/image/pallas_call | solution.py:484
  64.5 4.0 %image.7 = (bf16[16,4,256,128]{3,2,1,0:T(8,128)(2,1)}, f32[16,64,128]{2,1,0:T(8,128)S(1)}, f32[64,128]{1,0:T(8,128)S(1)}, f32[64,128]{1,0:T(8,128)S(1)}) custom-call(s32[3]{0:T(128)S(1)} %pad_add_fusion.where_ref.refs_0_, s32[16,2]{1,0:T(8,128)S(1)} %copy.16.shifts_ref.refs_1_, ...), custom_call_target="tpu_custom_call", output_to_operand_aliasing={{0}: (9, {})} | custom-call | flops 20000000 | bytes 8000000 | tf_op jit(solution)/shard_map/image/pallas_call | solution.py:484
  68.6 1.9 %collective-permute-start.14 = (f32[64,128]{1,0:T(8,128)S(1)}, f32[64,128]{1,0:T(8,128)S(1)}, u32[]{:S(2)}, u32[]{:S(2)}) collective-permute-start(f32[64,128]{1,0:T(8,128)S(1)} %get-tuple-element.91), channel_id=1, source_target_pairs={{16,32},{32,16},{48,64},{64,48},{80,96},{96,80},{112,128},{128,112... | collective-permute-start | bytes 98312 | tf_op jit(solution)/shard_map/ppermute | solution.py:507
  70.5 5.7 %collective-permute-done.14.outer_ref = f32[64,128]{1,0:T(8,128)S(1)} collective-permute-done((f32[64,128]{1,0:T(8,128)S(1)}, f32[64,128]{1,0:T(8,128)S(1)}, u32[]{:S(2)}, u32[]{:S(2)}) %collective-permute-start.14) | collective-permute-done | bytes 32800 | tf_op jit(solution)/shard_map/ppermute | solution.py:507
  76.2 0.9 merge.1
  77.1 24.0 %all_to_all.5.parts_ref = f32[16,64,128]{2,1,0:T(8,128)S(1)} all-to-all(f32[16,64,128]{2,1,0:T(8,128)S(1)} %merge.1), channel_id=1, replica_groups=mesh['space'=16,'offset'=16] {'offset'}, dimensions={0} | all-to-all | bytes 1048576 | tf_op jit(solution)/shard_map/all_to_all | solution.py:514
  101.1 0.6 total.1
  (24 shorter events, 0.4 us)
Async XLA Ops:
  2.2 7.9 %collective-permute-start.1 = (f32[5,16,128]{2,1,0:T(8,128)}, f32[5,16,128]{2,1,0:T(8,128)S(1)}, u32[]{:S(2)}, u32[]{:S(2)}) collective-permute-start(f32[5,16,128]{2,1,0:T(8,128)} %get-tuple-element.48), channel_id=1, source_target_pairs={{16,32},{32,16},{48,64},{64,48},{80,96},{96,80},{112,128},{128,112... | collective-permute-start | bytes 122888 | tf_op jit(solution)/shard_map/ppermute | solution.py:400
  6.4 3.7 %collective-permute-start = (f32[5,16,128]{2,1,0:T(8,128)}, f32[5,16,128]{2,1,0:T(8,128)S(1)}, u32[]{:S(2)}, u32[]{:S(2)}) collective-permute-start(f32[5,16,128]{2,1,0:T(8,128)} %get-tuple-element.48), channel_id=1, source_target_pairs={{0,16},{16,0},{32,48},{48,32},{64,80},{80,64},{96,112},{112,96},{1... | collective-permute-start | bytes 122888 | tf_op jit(solution)/shard_map/ppermute | solution.py:399
  7.4 0.9 copy-start.2
  10.8 7.5 %collective-permute-start.2 = (f32[25,16,128]{2,1,0:T(8,128)S(1)}, f32[25,16,128]{2,1,0:T(8,128)S(1)}, u32[]{:S(2)}, u32[]{:S(2)}) collective-permute-start(f32[25,16,128]{2,1,0:T(8,128)S(1)} %get-tuple-element.49.own_ref), channel_id=1, source_target_pairs={{0,1},{1,0},{2,3},{3,2},{4,5},{5,4},{6,7},{7,6},{8,9},{9,8},{10,11... | collective-permute-start | bytes 614408 | tf_op jit(solution)/shard_map/ppermute | solution.py:416
  12.3 5.9 %collective-permute-start.4 = (f32[5,8,256]{2,1,0:T(8,128)S(1)}, f32[5,8,256]{2,1,0:T(8,128)S(1)}, u32[]{:S(2)}, u32[]{:S(2)}) collective-permute-start(f32[5,8,256]{2,1,0:T(8,128)S(1)} %get-tuple-element.50), channel_id=1, source_target_pairs={{1,3},{2,0},{3,5},{4,2},{5,7},{6,4},{7,9},{8,6},{9,11},{10,8},{11,... | collective-permute-start | bytes 122888 | tf_op jit(solution)/shard_map/ppermute | solution.py:418
  13.6 4.6 %collective-permute-start.3 = (f32[5,8,256]{2,1,0:T(8,128)S(1)}, f32[5,8,256]{2,1,0:T(8,128)S(1)}, u32[]{:S(2)}, u32[]{:S(2)}) collective-permute-start(f32[5,8,256]{2,1,0:T(8,128)S(1)} %get-tuple-element.50), channel_id=1, source_target_pairs={{1,2},{2,1},{3,4},{4,3},{5,6},{6,5},{7,8},{8,7},{9,10},{10,9},{11,... | collective-permute-start | bytes 122888 | tf_op jit(solution)/shard_map/ppermute | solution.py:417
  19.5 14.4 %collective-permute-start.6 = (f32[2,18,16,128]{3,2,1,0:T(8,128)S(1)}, f32[2,18,16,128]{3,2,1,0:T(8,128)S(1)}, u32[]{:S(2)}, u32[]{:S(2)}) collective-permute-start(f32[2,18,16,128]{3,2,1,0:T(8,128)S(1)} %wave.1), channel_id=1, source_target_pairs={{0,2},{1,3},{2,4},{3,5},{4,6},{5,7},{6,8},{7,9},{8,10},{9,11},{10,... | collective-permute-start | bytes 884744 | tf_op jit(solution)/shard_map/ppermute | solution.py:448
  24.4 9.5 %collective-permute-start.5 = (f32[2,18,16,128]{3,2,1,0:T(8,128)S(1)}, f32[2,18,16,128]{3,2,1,0:T(8,128)S(1)}, u32[]{:S(2)}, u32[]{:S(2)}) collective-permute-start(f32[2,18,16,128]{3,2,1,0:T(8,128)S(1)} %wave.1), channel_id=1, source_target_pairs={{0,14},{1,15},{2,0},{3,1},{4,2},{5,3},{6,4},{7,5},{8,6},{9,7},{10,... | collective-permute-start | bytes 884744 | tf_op jit(solution)/shard_map/ppermute | solution.py:447
  30.1 2.2 %copy-start = (bf16[16,4,256,128]{3,2,1,0:T(8,128)(2,1)S(1)}, bf16[16,4,256,128]{3,2,1,0:T(8,128)(2,1)}, u32[]{:S(2)}) copy-start(bf16[16,4,256,128]{3,2,1,0:T(8,128)(2,1)} %refs_2_.9) | copy-start | bytes 12582916
  32.3 5.1 %copy-start.1 = (bf16[16,4,256,128]{3,2,1,0:T(8,128)(2,1)S(1)}, bf16[16,4,256,128]{3,2,1,0:T(8,128)(2,1)}, u32[]{:S(2)}) copy-start(bf16[16,4,256,128]{3,2,1,0:T(8,128)(2,1)} %refs_2_.9) | copy-start | bytes 12582916
  34.0 8.4 %collective-permute-start.7 = (f32[2,18,16,128]{3,2,1,0:T(8,128)S(1)}, f32[2,18,16,128]{3,2,1,0:T(8,128)S(1)}, u32[]{:S(2)}, u32[]{:S(2)}) collective-permute-start(f32[2,18,16,128]{3,2,1,0:T(8,128)S(1)} %collective-permute-done.5), channel_id=1, source_target_pairs={{0,14},{1,15},{2,0},{3,1},{4,2},{5,3},{6,4},{7,5},{8,6},{9,7},{10,... | collective-permute-start | bytes 884744 | tf_op jit(solution)/shard_map/ppermute | solution.py:452
  37.4 8.5 %collective-permute-start.8 = (f32[2,18,16,128]{3,2,1,0:T(8,128)S(1)}, f32[2,18,16,128]{3,2,1,0:T(8,128)S(1)}, u32[]{:S(2)}, u32[]{:S(2)}) collective-permute-start(f32[2,18,16,128]{3,2,1,0:T(8,128)S(1)} %collective-permute-done.6), channel_id=1, source_target_pairs={{0,2},{1,3},{2,4},{3,5},{4,6},{5,7},{6,8},{7,9},{8,10},{9,11},{10,... | collective-permute-start | bytes 884744 | tf_op jit(solution)/shard_map/ppermute | solution.py:453
  45.8 8.3 %collective-permute-start.9 = (f32[2,18,16,128]{3,2,1,0:T(8,128)S(1)}, f32[2,18,16,128]{3,2,1,0:T(8,128)S(1)}, u32[]{:S(2)}, u32[]{:S(2)}) collective-permute-start(f32[2,18,16,128]{3,2,1,0:T(8,128)S(1)} %collective-permute-done.7), channel_id=1, source_target_pairs={{0,14},{1,15},{2,0},{3,1},{4,2},{5,3},{6,4},{7,5},{8,6},{9,7},{10,... | collective-permute-start | bytes 884744 | tf_op jit(solution)/shard_map/ppermute | solution.py:452
  48.1 9.5 %collective-permute-start.10 = (f32[2,18,16,128]{3,2,1,0:T(8,128)S(1)}, f32[2,18,16,128]{3,2,1,0:T(8,128)S(1)}, u32[]{:S(2)}, u32[]{:S(2)}) collective-permute-start(f32[2,18,16,128]{3,2,1,0:T(8,128)S(1)} %collective-permute-done.8), channel_id=1, source_target_pairs={{0,2},{1,3},{2,4},{3,5},{4,6},{5,7},{6,8},{7,9},{8,10},{9,11},{10,... | collective-permute-start | bytes 884744 | tf_op jit(solution)/shard_map/ppermute | solution.py:453
  57.6 6.8 %collective-permute-start.11 = (f32[18,16,128]{2,1,0:T(8,128)S(1)}, f32[18,16,128]{2,1,0:T(8,128)S(1)}, u32[]{:S(2)}, u32[]{:S(2)}) collective-permute-start(f32[18,16,128]{2,1,0:T(8,128)S(1)} %get-tuple-element.95.refs_5_.refs_3_), channel_id=1, source_target_pairs={{0,14},{1,15},{2,0},{3,1},{4,2},{5,3},{6,4},{7,5},{8,6},{9,7},{10,... | collective-permute-start | bytes 442376 | tf_op jit(solution)/shard_map/ppermute | solution.py:455
  57.8 6.7 %collective-permute-start.12 = (f32[18,16,128]{2,1,0:T(8,128)S(1)}, f32[18,16,128]{2,1,0:T(8,128)S(1)}, u32[]{:S(2)}, u32[]{:S(2)}) collective-permute-start(f32[18,16,128]{2,1,0:T(8,128)S(1)} %get-tuple-element.93.refs_8_), channel_id=1, source_target_pairs={{0,2},{1,3},{2,4},{3,5},{4,6},{5,7},{6,8},{7,9},{8,10},{9,11},{10,... | collective-permute-start | bytes 442376 | tf_op jit(solution)/shard_map/ppermute | solution.py:456
  68.5 2.0 %collective-permute-start.13 = (f32[64,128]{1,0:T(8,128)S(1)}, f32[64,128]{1,0:T(8,128)S(1)}, u32[]{:S(2)}, u32[]{:S(2)}) collective-permute-start(f32[64,128]{1,0:T(8,128)S(1)} %get-tuple-element.90), channel_id=1, source_target_pairs={{0,16},{16,0},{32,48},{48,32},{64,80},{80,64},{96,112},{112,96},{1... | collective-permute-start | bytes 98312 | tf_op jit(solution)/shard_map/ppermute | solution.py:506
  68.6 7.6 %collective-permute-start.14 = (f32[64,128]{1,0:T(8,128)S(1)}, f32[64,128]{1,0:T(8,128)S(1)}, u32[]{:S(2)}, u32[]{:S(2)}) collective-permute-start(f32[64,128]{1,0:T(8,128)S(1)} %get-tuple-element.91), channel_id=1, source_target_pairs={{16,32},{32,16},{48,64},{64,48},{80,96},{96,80},{112,128},{128,112... | collective-permute-start | bytes 98312 | tf_op jit(solution)/shard_map/ppermute | solution.py:507
